TPU v7x, 32 devices: a whole 2x2x4 slice. The times are simulated.
32 devices in a mesh: dp: 8 (over y, x, core), tensor: 4 (over z).
Axes of the slice: x: 2, y: 2, z: 4, core: 2. Of those that a mesh axis runs over, the one named last changes fastest.
Arguments:
- tokens: bfloat16 [8192, 2048], P(('dp', 'tensor')), may hold values from -6 to 6
- gain_in: float32 [2048], replicated, may hold values from 0.1 to 1.9
- w_query: bfloat16 [2048, 2048], P(None, 'tensor'), may hold values from -0.125 to 0.125
- w_key: bfloat16 [2048, 2048], P(None, 'tensor'), may hold values from -0.125 to 0.125
- w_value: bfloat16 [2048, 2048], P(None, 'tensor'), may hold values from -0.125 to 0.125
- w_alpha: bfloat16 [2048, 16], P(None, 'tensor'), may hold values from -0.125 to 0.125
- w_beta: bfloat16 [2048, 16], P(None, 'tensor'), may hold values from -0.125 to 0.125
- w_gate_out: bfloat16 [2048, 2048], P(None, 'tensor'), may hold values from -0.125 to 0.125
- conv_query: float32 [4, 2048], P(None, 'tensor'), may hold values from -3 to 3
- conv_key: float32 [4, 2048], P(None, 'tensor'), may hold values from -3 to 3
- conv_value: float32 [4, 2048], P(None, 'tensor'), may hold values from -3 to 3
- decay_log: float32 [16], P('tensor'), may hold values from -7.5 to -1.5
- decay_bias: float32 [16], P('tensor'), may hold values from -1 to 1
- head_gain: float32 [2048], P('tensor'), may hold values from 0.1 to 1.9
- w_out: bfloat16 [2048, 2048], P('tensor'), may hold values from -0.1875 to 0.1875
- gain_mid: float32 [2048], replicated, may hold values from 0.1 to 1.9
- w_gate: bfloat16 [2048, 5632], P(None, 'tensor'), may hold values from -0.125 to 0.125
- w_up: bfloat16 [2048, 5632], P(None, 'tensor'), may hold values from -0.125 to 0.125
- w_down: bfloat16 [5632, 2048], P('tensor'), may hold values from -0.15625 to 0.15625
- out_grad: bfloat16 [8192, 2048], P('dp'), may hold values from -6 to 6
- doc_lengths: int32 [1, 4], replicated, may hold values from 1 to 4608, as said below
Outputs:
- output: bfloat16 [8192, 2048], P(('dp', 'tensor'))
- input_grad: float32 [8192, 2048], P(('dp', 'tensor'))
- gain_in_grad: float32 [2048], replicated
- w_query_grad: float32 [2048, 2048], P('dp', 'tensor')
- w_key_grad: float32 [2048, 2048], P('dp', 'tensor')
- w_value_grad: float32 [2048, 2048], P('dp', 'tensor')
- w_alpha_grad: float32 [2048, 16], P('dp', 'tensor')
- w_beta_grad: float32 [2048, 16], P('dp', 'tensor')
- w_gate_out_grad: float32 [2048, 2048], P('dp', 'tensor')
- conv_query_grad: float32 [4, 2048], replicated
- conv_key_grad: float32 [4, 2048], replicated
- conv_value_grad: float32 [4, 2048], replicated
- decay_log_grad: float32 [16], replicated
- decay_bias_grad: float32 [16], replicated
- head_gain_grad: float32 [2048], replicated
- w_out_grad: float32 [2048, 2048], P('tensor', 'dp')
- gain_mid_grad: float32 [2048], replicated
- w_gate_grad: float32 [2048, 5632], P('dp', 'tensor')
- w_up_grad: float32 [2048, 5632], P('dp', 'tensor')
- w_down_grad: float32 [5632, 2048], P('tensor', 'dp')
Inputs may be any that keep to these rules, and one draw needn't show every extreme that they name: `doc_lengths`: each row holds the lengths of the 4 documents of one packed sequence in order; a row sums to 8192, and its longest document has exactly 4608 tokens.
All inputs are finite; a program needn't handle non-finite values.
Results may differ from a plain program's by a relative error of at most 0.013.
The roundings to bfloat16 on the way count: a program that leaves them out, or rounds other values in their place, can miss the bound.
Values may be sent and summed in bfloat16 or wider, within the bound.
A program may use at most 256 MiB of HBM per device.

v0:
```python
import math

import jax
import jax.numpy as jnp
from jax import lax
from jax.sharding import PartitionSpec as P

BLOCK = 64


HIGHEST_PRECISION = lax.Precision.HIGHEST
epsilon = 1e-06


def shifted_2(shard, axis, by):
    devices = lax.axis_size(axis)
    pairs = [(i, i + by) for i in range(devices) if 0 <= i + by < devices]
    return lax.ppermute(shard, axis, pairs)


def prefix(value, axis, join, neutral, backward):
    count, mine = (lax.axis_size(axis), lax.axis_index(axis))
    pieces = jax.tree.map(lambda part: lax.all_gather(part, axis), value)
    if backward:
        pieces = jax.tree.map(lambda part: part[::-1], pieces)
        mine = count - 1 - mine
    total = jax.tree.map(
        lambda part, zero: jnp.full_like(part, 0) + jnp.asarray(zero, part.dtype), value, neutral
    )

    def step(position, total):
        longer = join(total, jax.tree.map(lambda part: part[position], pieces))
        return jax.tree.map(lambda new, old: jnp.where(position < mine, new, old), longer, total)

    return lax.fori_loop(0, count - 1, step, total)


def batched(form, left, right):
    return jnp.einsum(form, left, right, precision=HIGHEST_PRECISION)


def row_norm(values, gain):
    return values * lax.rsqrt(jnp.mean(values * values, axis=-1, keepdims=True) + epsilon) * gain


def unit_rows(values):
    return values * lax.rsqrt(jnp.sum(values * values, axis=-1, keepdims=True) + epsilon)


def unit_inverse(lower_part):
    block_size = lower_part.shape[-1]
    identity = jnp.eye(block_size, dtype=lower_part.dtype)
    powers = -lower_part
    result = identity + powers
    for squaring in range(block_size.bit_length() - 2):
        powers = batched("hij,hjk->hik", powers, powers)
        result = batched("hij,hjk->hik", result, identity + powers)
    return result


def block_step(carry_state, block_inputs):
    query_block, key_block, value_block, beta_block, decay_block, doc_block, prior_doc = (
        block_inputs
    )
    block_size = query_block.shape[1]
    row_ids = lax.broadcasted_iota(jnp.int32, (block_size, block_size), 0)
    column_ids = lax.broadcasted_iota(jnp.int32, (block_size, block_size), 1)
    inside = (doc_block[:, None] == doc_block[None, :]) & (row_ids >= column_ids)
    strict = inside & (row_ids > column_ids)
    cumulative = jnp.cumsum(decay_block, axis=1)
    spread_log = cumulative[:, :, None] - cumulative[:, None, :]
    weights_in = jnp.where(inside, jnp.exp(jnp.where(inside, spread_log, 0.0)), 0.0)
    carried = jnp.where(doc_block == prior_doc, 1.0, 0.0)
    from_start = jnp.exp(cumulative) * carried
    key_gram = batched("hid,hjd->hij", key_block, key_block)
    lower_part = jnp.where(strict, beta_block[:, :, None] * key_gram * weights_in, 0.0)
    inverse = unit_inverse(lower_part)
    write_keys = batched("hij,hjd->hid", inverse, (beta_block * from_start)[:, :, None] * key_block)
    write_values = batched("hij,hjd->hid", inverse, beta_block[:, :, None] * value_block)
    fresh_values = write_values - batched("hid,hde->hie", write_keys, carry_state)
    scores = jnp.where(inside, batched("hid,hjd->hij", query_block, key_block) * weights_in, 0.0)
    outputs = batched("hid,hde->hie", query_block * from_start[:, :, None], carry_state) + batched(
        "hij,hje->hie", scores, fresh_values
    )
    last_row = weights_in[:, block_size - 1, :]
    new_state = from_start[:, block_size - 1][:, None, None] * carry_state + batched(
        "hcd,hce->hde", key_block * last_row[:, :, None], fresh_values
    )
    return (new_state, outputs)


def run_blocks(start_state, queries, keys_in, values_in, beta_rows, decays, doc_blocks, prior_docs):
    return lax.scan(
        jax.checkpoint(block_step),
        start_state,
        (queries, keys_in, values_in, beta_rows, decays, doc_blocks, prior_docs),
    )


def features(extended, alpha_raw, beta_raw, conv_all, decay_log, decay_bias, doc_ext, block_size):
    conv_taps = conv_all.shape[1]
    row_total = alpha_raw.shape[0]
    head_count = alpha_raw.shape[1]
    doc_ids = doc_ext[conv_taps - 1 :]
    summed = jnp.zeros((3, row_total, extended.shape[2]), jnp.float32)
    for offset in range(conv_taps):
        shifted = lax.slice_in_dim(extended, offset, offset + row_total, axis=1)
        same_doc = lax.slice_in_dim(doc_ext, offset, offset + row_total) == doc_ids
        summed = (
            summed
            + jnp.where(same_doc[None, :, None], shifted, 0.0) * conv_all[:, offset][:, None, :]
        )
    convolved = jax.nn.silu(summed).reshape(3, row_total, head_count, -1)
    head_size = convolved.shape[-1]
    queries = unit_rows(convolved[0]) / math.sqrt(head_size)
    keys_in = unit_rows(convolved[1])
    values_in = convolved[2]
    beta_rows = jax.nn.sigmoid(beta_raw)
    decays = -jnp.exp(decay_log) * jax.nn.softplus(alpha_raw + decay_bias)
    block_count = row_total // block_size

    def blocks_of(values):
        return jnp.swapaxes(values.reshape(block_count, block_size, head_count, -1), 1, 2)

    def flat_blocks(values):
        return jnp.swapaxes(values.reshape(block_count, block_size, head_count), 1, 2)

    return (
        blocks_of(queries),
        blocks_of(keys_in),
        blocks_of(values_in),
        flat_blocks(beta_rows),
        flat_blocks(decays),
    )


def head_outputs(
    queries,
    keys_in,
    values_in,
    beta_rows,
    decays,
    gate_raw,
    gain_heads,
    start_state,
    doc_blocks,
    prior_docs,
):
    final_state, outputs = run_blocks(
        start_state, queries, keys_in, values_in, beta_rows, decays, doc_blocks, prior_docs
    )
    block_count, head_count, block_size, head_size = outputs.shape
    rows_out = jnp.swapaxes(outputs, 1, 2).reshape(block_count * block_size, head_count, head_size)
    normed = rows_out * lax.rsqrt(jnp.mean(rows_out * rows_out, axis=-1, keepdims=True) + epsilon)
    gated = (
        normed
        * gain_heads.reshape(head_count, head_size)
        * jax.nn.silu(gate_raw).reshape(-1, head_count, head_size)
    )
    return (gated.reshape(block_count * block_size, head_count * head_size), final_state)


def combine_maps(earlier, later):
    return (
        batched("hij,hjk->hik", later[0], earlier[0]),
        batched("hij,hjk->hik", later[0], earlier[1]) + later[1],
    )


def contract_rows(left, right):
    return lax.dot_general(
        left, right, (((0,), (0,)), ((), ())), preferred_element_type=jnp.float32
    )


def contract_cols(left, right):
    return lax.dot_general(
        left, right, (((1,), (1,)), ((), ())), preferred_element_type=jnp.float32
    )


def widen_full(local_part, tensor_parts, tensor_index, along):
    full_shape = list(local_part.shape)
    full_shape[along] = full_shape[along] * tensor_parts
    full_part = jnp.zeros(tuple(full_shape), jnp.float32)
    return lax.dynamic_update_slice_in_dim(
        full_part, local_part, tensor_index * local_part.shape[along], along
    )


def sum_mlp_grads(gate_part, up_part, down_part):
    return (
        lax.psum_scatter(gate_part, "dp", scatter_dimension=0, tiled=True),
        lax.psum_scatter(up_part, "dp", scatter_dimension=0, tiled=True),
        lax.psum_scatter(down_part, "dp", scatter_dimension=1, tiled=True),
    )


def local(
    tokens,
    gain_in,
    w_query,
    w_key,
    w_value,
    w_alpha,
    w_beta,
    w_gate_out,
    conv_query,
    conv_key,
    conv_value,
    decay_log,
    decay_bias,
    head_gain,
    w_out,
    gain_mid,
    w_gate,
    w_up,
    w_down,
    out_grad,
    doc_lengths,
):
    rows_own = tokens.shape[0]
    tensor_parts = lax.axis_size("tensor")
    group_rows = rows_own * tensor_parts
    seq_total = group_rows * lax.axis_size("dp")
    tensor_index = lax.axis_index("tensor")
    conv_taps = conv_query.shape[0]
    head_count = w_alpha.shape[1]
    key_width = w_query.shape[1]
    head_size = key_width // head_count
    starts = (
        jnp.cumsum(doc_lengths, axis=1)
        - doc_lengths
        + seq_total * lax.broadcasted_iota(jnp.int32, doc_lengths.shape, 0)
    ).reshape(-1)
    positions = (
        lax.axis_index("dp") * group_rows
        + lax.iota(jnp.int32, group_rows + conv_taps - 1)
        - (conv_taps - 1)
    )
    doc_ext = jnp.sum((positions[:, None] >= starts[None, :]).astype(jnp.int32), axis=1) - 1
    doc_blocks = doc_ext[conv_taps - 1 :].reshape(-1, BLOCK)
    prior_docs = doc_ext[conv_taps - 2 : conv_taps - 2 + group_rows : BLOCK]
    own_rows = tokens.astype(jnp.float32)
    normed_in = row_norm(own_rows, gain_in).astype(jnp.bfloat16)
    normed_all = lax.all_gather(normed_in, "tensor", axis=0, tiled=True)
    projected = jnp.stack(
        [
            jnp.dot(normed_all, w_query, preferred_element_type=jnp.float32),
            jnp.dot(normed_all, w_key, preferred_element_type=jnp.float32),
            jnp.dot(normed_all, w_value, preferred_element_type=jnp.float32),
        ]
    ).astype(jnp.bfloat16)
    alpha_raw = jnp.dot(normed_all, w_alpha, preferred_element_type=jnp.float32)
    beta_raw = jnp.dot(normed_all, w_beta, preferred_element_type=jnp.float32)
    gate_raw = jnp.dot(normed_all, w_gate_out, preferred_element_type=jnp.float32)
    rim_rows = shifted_2(projected[:, group_rows - (conv_taps - 1) :, :], "dp", 1)
    extended = jnp.concatenate([rim_rows, projected], axis=1).astype(jnp.float32)
    conv_all = jnp.stack([conv_query, conv_key, conv_value])

    def feature_map(extended, alpha_raw, beta_raw, conv_all, decay_log, decay_bias):
        return features(
            extended, alpha_raw, beta_raw, conv_all, decay_log, decay_bias, doc_ext, BLOCK
        )

    feature_set, feature_back = jax.vjp(
        feature_map, extended, alpha_raw, beta_raw, conv_all, decay_log, decay_bias
    )
    queries, keys_in, values_in, beta_rows, decays = feature_set
    value_size = values_in.shape[-1]
    identity = jnp.broadcast_to(
        jnp.eye(head_size, dtype=jnp.float32), (head_count, head_size, head_size)
    )
    start_aug = jnp.concatenate(
        [jnp.zeros((head_count, head_size, value_size), jnp.float32), identity], axis=2
    )
    values_aug = jnp.concatenate(
        [values_in, jnp.zeros(values_in.shape[:-1] + (head_size,), jnp.float32)], axis=3
    )
    final_aug, unused_rows = run_blocks(
        start_aug, queries, keys_in, values_aug, beta_rows, decays, doc_blocks, prior_docs
    )
    offsets = final_aug[:, :, :value_size]
    transfer = final_aug[:, :, value_size:]
    unused_map, state_in = prefix(
        (transfer, offsets), "dp", combine_maps, (identity, jnp.zeros_like(offsets)), False
    )

    def mixer_map(queries, keys_in, values_in, beta_rows, decays, gate_raw, gain_heads, state_in):
        return head_outputs(
            queries,
            keys_in,
            values_in,
            beta_rows,
            decays,
            gate_raw,
            gain_heads,
            state_in,
            doc_blocks,
            prior_docs,
        )

    (mixed_out, final_state), mixer_back = jax.vjp(
        mixer_map, queries, keys_in, values_in, beta_rows, decays, gate_raw, head_gain, state_in
    )
    mixed_low = mixed_out.astype(jnp.bfloat16)
    mixer_rows = lax.psum_scatter(
        jnp.dot(mixed_low, w_out, preferred_element_type=jnp.float32),
        "tensor",
        scatter_dimension=0,
        tiled=True,
    )
    residual = own_rows + mixer_rows
    normed_mid = row_norm(residual, gain_mid).astype(jnp.bfloat16)
    mid_all = lax.all_gather(normed_mid, "tensor", axis=0, tiled=True)
    gate_pre = jnp.dot(mid_all, w_gate, preferred_element_type=jnp.float32)
    up_pre = jnp.dot(mid_all, w_up, preferred_element_type=jnp.float32)
    activated = (jax.nn.silu(gate_pre) * up_pre).astype(jnp.bfloat16)
    mlp_rows = lax.psum_scatter(
        jnp.dot(activated, w_down, preferred_element_type=jnp.float32),
        "tensor",
        scatter_dimension=0,
        tiled=True,
    )
    output = (residual + mlp_rows).astype(jnp.bfloat16)
    grad_own = lax.dynamic_slice_in_dim(out_grad, tensor_index * rows_own, rows_own, 0).astype(
        jnp.float32
    )
    grad_act = contract_cols(out_grad, w_down)
    sigmoid_gate = jax.nn.sigmoid(gate_pre)
    grad_gate = (grad_act * up_pre * sigmoid_gate * (1.0 + gate_pre * (1.0 - sigmoid_gate))).astype(
        jnp.bfloat16
    )
    grad_up = (grad_act * (gate_pre * sigmoid_gate)).astype(jnp.bfloat16)
    grad_mid = lax.psum_scatter(
        contract_cols(grad_gate, w_gate) + contract_cols(grad_up, w_up),
        "tensor",
        scatter_dimension=0,
        tiled=True,
    )
    grad_down_w = contract_rows(activated, out_grad)
    grad_gate_w = contract_rows(mid_all, grad_gate)
    grad_up_w = contract_rows(mid_all, grad_up)
    unused_mid, norm_mid_back = jax.vjp(row_norm, residual, gain_mid)
    grad_res_norm, grad_gain_mid = norm_mid_back(grad_mid)
    grad_residual = grad_own + grad_res_norm
    grad_mixer_all = lax.all_gather(
        grad_residual.astype(jnp.bfloat16), "tensor", axis=0, tiled=True
    )
    grad_mixed = contract_cols(grad_mixer_all, w_out)
    grad_out_w = contract_rows(mixed_low, grad_mixer_all)
    first_pass = mixer_back((grad_mixed, jnp.zeros_like(state_in)))
    unused_grad_map, state_grad = prefix(
        (jnp.swapaxes(transfer, 1, 2), first_pass[7]),
        "dp",
        combine_maps,
        (identity, jnp.zeros_like(state_in)),
        True,
    )
    mixer_grads = mixer_back((grad_mixed, state_grad))
    grad_ext, grad_alpha, grad_beta, grad_conv, grad_decay_log, grad_decay_bias = feature_back(
        mixer_grads[:5]
    )
    rim_grad = shifted_2(grad_ext[:, : conv_taps - 1, :], "dp", -1)
    grad_projected = grad_ext[:, conv_taps - 1 :, :]
    grad_projected = grad_projected.at[:, group_rows - (conv_taps - 1) :, :].add(rim_grad)
    grad_proj_low = grad_projected.astype(jnp.bfloat16)
    grad_alpha_low = grad_alpha.astype(jnp.bfloat16)
    grad_beta_low = grad_beta.astype(jnp.bfloat16)
    grad_gate_low = mixer_grads[5].astype(jnp.bfloat16)
    summed = (
        contract_cols(grad_proj_low[0], w_query)
        + contract_cols(grad_proj_low[1], w_key)
        + contract_cols(grad_proj_low[2], w_value)
    )
    summed = summed + contract_cols(grad_alpha_low, w_alpha)
    summed = summed + contract_cols(grad_beta_low, w_beta)
    grad_normed = lax.psum_scatter(
        summed + contract_cols(grad_gate_low, w_gate_out), "tensor", scatter_dimension=0, tiled=True
    )
    grad_query_w = contract_rows(normed_all, grad_proj_low[0])
    grad_key_w = contract_rows(normed_all, grad_proj_low[1])
    grad_value_w = contract_rows(normed_all, grad_proj_low[2])
    grad_alpha_w = contract_rows(normed_all, grad_alpha_low)
    grad_beta_w = contract_rows(normed_all, grad_beta_low)
    grad_gate_out_w = contract_rows(normed_all, grad_gate_low)
    unused_in, norm_in_back = jax.vjp(row_norm, own_rows, gain_in)
    grad_tokens, grad_gain_in = norm_in_back(grad_normed)
    input_grad = grad_residual + grad_tokens
    mixer_summed = (
        lax.psum_scatter(grad_query_w, "dp", scatter_dimension=0, tiled=True),
        lax.psum_scatter(grad_key_w, "dp", scatter_dimension=0, tiled=True),
        lax.psum_scatter(grad_value_w, "dp", scatter_dimension=0, tiled=True),
        lax.psum_scatter(grad_alpha_w, "dp", scatter_dimension=0, tiled=True),
        lax.psum_scatter(grad_beta_w, "dp", scatter_dimension=0, tiled=True),
        lax.psum_scatter(grad_gate_out_w, "dp", scatter_dimension=0, tiled=True),
        lax.psum_scatter(grad_out_w, "dp", scatter_dimension=1, tiled=True),
    )
    mlp_summed = sum_mlp_grads(grad_gate_w, grad_up_w, grad_down_w)
    small_summed = lax.psum(
        (
            widen_full(grad_conv, tensor_parts, tensor_index, 2),
            widen_full(grad_decay_log, tensor_parts, tensor_index, 0),
            widen_full(grad_decay_bias, tensor_parts, tensor_index, 0),
            widen_full(mixer_grads[6], tensor_parts, tensor_index, 0),
            grad_gain_in,
            grad_gain_mid,
        ),
        ("dp", "tensor"),
    )
    return (
        output,
        input_grad,
        small_summed[4],
        mixer_summed[0],
        mixer_summed[1],
        mixer_summed[2],
        mixer_summed[3],
        mixer_summed[4],
        mixer_summed[5],
        small_summed[0][0],
        small_summed[0][1],
        small_summed[0][2],
        small_summed[1],
        small_summed[2],
        small_summed[3],
        mixer_summed[6],
        small_summed[5],
        mlp_summed[0],
        mlp_summed[1],
        mlp_summed[2],
    )


def solution(mesh):
    placed = (
        P(("dp", "tensor"), None),
        P(),
        P(None, "tensor"),
        P(None, "tensor"),
        P(None, "tensor"),
        P(None, "tensor"),
        P(None, "tensor"),
        P(None, "tensor"),
        P(None, "tensor"),
        P(None, "tensor"),
        P(None, "tensor"),
        P("tensor"),
        P("tensor"),
        P("tensor"),
        P("tensor", None),
        P(),
        P(None, "tensor"),
        P(None, "tensor"),
        P("tensor", None),
        P("dp", None),
        P(),
    )
    return jax.shard_map(
        local,
        mesh=mesh,
        in_specs=placed,
        out_specs=(
            P(("dp", "tensor"), None),
            P(("dp", "tensor"), None),
            P(),
            P("dp", "tensor"),
            P("dp", "tensor"),
            P("dp", "tensor"),
            P("dp", "tensor"),
            P("dp", "tensor"),
            P("dp", "tensor"),
            P(),
            P(),
            P(),
            P(),
            P(),
            P(),
            P("tensor", "dp"),
            P(),
            P("dp", "tensor"),
            P("dp", "tensor"),
            P("tensor", "dp"),
        ),
        check_vma=False,
    )
```

profile of v0, /device:TPU:12, one launch (start us, length us, event | category | flops | bytes accessed | tf_op | source)
XLA Modules:
  0.0 2950.7 jit_solution(14092897893531845944)
XLA Ops:
  13.6 78.6 %all-gather.12.cloned.1.call-done = bf16[1024,2048]{1,0:T(8,128)(2,1)} async-done(((bf16[256,2048]{1,0:T(8,128)(2,1)}), bf16[1024,2048]{1,0:T(8,128)(2,1)}) %all-gather.12.cloned.1.call-update) | async-done | bytes 4194320 | tf_op jit(solution)/shard_map/all_gather | solution.py:246
  142.6 171.6 %while.96 = (s32[]{:T(128)}, f32[4,128,256]{2,1,0:T(8,128)S(1)}, f32[16,4,64]{2,1,0:T(4,128)S(1)}, s32[16,64]{1,0:T(8,128)S(1)}, s32[16]{0:T(128)S(1)}, /*index=...) while((s32[]{:T(128)}, f32[4,128,256]{2,1,0:T(8,128)S(1)}, ...), condition=%wide.region_6.7_spmd, body=%wide.region_4.6_spmd.sunk | while | flops 428585344 | bytes 5591737 | solution.py:93
  329.5 15.4 all-gather.18.cloned.1.call-done
  344.9 30.4 %all-gather.20.cloned.1.call-done = f32[32,128,128]{2,1,0:T(8,128)} async-done(((f32[4,128,128]{2,1,0:T(8,128)}), f32[32,128,128]{2,1,0:T(8,128)}) %all-gather.20.cloned.1.call-update) | async-done | bytes 2097168 | tf_op jit(solution)/shard_map/all_gather | solution.py:23
  385.7 235.2 %while.98 = (s32[]{:T(128)}, f32[4,128,128]{2,1,0:T(8,128)S(1)}, f32[16,4,64,128]{3,2,1,0:T(8,128)}, f32[16,4,128,128]{3,2,1,0:T(8,128)}, f32[16,4,64]{2,1,0:T(4...) while((s32[]{:T(128)}, f32[4,128,128]{2,1,0:T(8,128)S(1)}, ...), condition=%wide.region_12.13_spmd.clone.clone, body=%wide.region_10.12_spmd.clone.clone.sunk | while | flops 403370368 | bytes 6000849 | solution.py:93
  639.9 144.3 %reduce-scatter.19.cloned.1.call-done = f32[256,2048]{1,0:T(8,128)} async-done(((f32[1024,2048]{1,0:T(8,128)}), f32[256,2048]{1,0:T(8,128)}) %reduce-scatter.19.cloned.1.call-update) | async-done | bytes 2097168 | tf_op jit(solution)/shard_map/reduce_scatter | solution.py:307
  788.7 79.5 %all-gather.14.cloned.1.call-done = bf16[1024,2048]{1,0:T(8,128)(2,1)} async-done(((bf16[256,2048]{1,0:T(8,128)(2,1)}), bf16[1024,2048]{1,0:T(8,128)(2,1)}) %all-gather.14.cloned.1.call-update) | async-done | bytes 4194320 | tf_op jit(solution)/shard_map/all_gather | solution.py:315
  868.2 12.0 fusion.317
  890.6 14.6 multiply_convert_fusion
  915.9 11.0 convolution_add_fusion.30
  927.0 145.2 %reduce-scatter.23.cloned.1.call-done = f32[256,2048]{1,0:T(8,128)} async-done(((f32[1024,2048]{1,0:T(8,128)}), f32[256,2048]{1,0:T(8,128)}) %reduce-scatter.23.cloned.1.call-update) | async-done | bytes 2097168 | tf_op jit(solution)/shard_map/reduce_scatter | solution.py:335
  1079.7 78.5 %all-gather.16.cloned.1.call-done = bf16[1024,2048]{1,0:T(8,128)(2,1)} async-done(((bf16[256,2048]{1,0:T(8,128)(2,1)}), bf16[1024,2048]{1,0:T(8,128)(2,1)}) %all-gather.16.cloned.1.call-update) | async-done | bytes 4194320 | tf_op jit(solution)/shard_map/all_gather | solution.py:347
  1176.2 154.5 %while.100 = (s32[]{:T(128)}, f32[4,128,128]{2,1,0:T(8,128)S(1)}, f32[16,4,64,128]{3,2,1,0:T(8,128)}, f32[16,4,64,128]{3,2,1,0:T(8,128)}, f32[16,4,64]{2,1,0:T(4...) while((s32[]{:T(128)}, f32[4,128,128]{2,1,0:T(8,128)S(1)}, ...), condition=%wide.region_22.23_spmd.clone, body=%wide.region_20.22_spmd.clone.sunk | while | flops 378302848 | bytes 6566631 | solution.py:93
  1342.1 18.3 all-gather.24.cloned.1.call-done
  1378.9 464.8 %while.97 = (s32[]{:T(128)}, f32[4,128,128]{2,1,0:T(8,128)S(1)}, f32[16,4,64,128]{3,2,0,1:T(8,128)}, f32[16,4,64,128]{3,2,0,1:T(8,128)}, f32[16,4,64,128]{3,2,0,...) while((s32[]{:T(128)}, f32[4,128,128]{2,1,0:T(8,128)S(1)}, ...), condition=%wide.region_36.37_spmd, body=%wide.region_25.36_spmd.sunk | while | flops 1085076864 | bytes 20078184 | solution.py:93
  1926.2 17.9 add_add_fusion
  1944.2 11.7 fusion.319
  1956.0 11.9 fusion.325
  1967.9 12.1 fusion.326
  1980.2 11.3 fusion.327
  2032.6 66.6 %all-reduce.18.cloned.1.call-done = f32[3,4,2048]{2,1,0:T(4,128)} async-done(((f32[3,4,2048]{2,1,0:T(4,128)}), f32[3,4,2048]{2,1,0:T(4,128)}) %all-reduce.18.cloned.1.call-update) | async-done | bytes 98320 | tf_op jit(solution)/shard_map/psum | solution.py:400
  2100.6 144.2 %reduce-scatter.25.cloned.1.call-done = f32[256,2048]{1,0:T(8,128)} async-done(((f32[1024,2048]{1,0:T(8,128)}), f32[256,2048]{1,0:T(8,128)}) %reduce-scatter.25.cloned.1.call-update) | async-done | bytes 2097168 | tf_op jit(solution)/shard_map/reduce_scatter | solution.py:378
  2247.1 47.2 %all-reduce.15 = (f32[2048]{0:T(1024)}, f32[16]{0:T(128)}, f32[16]{0:T(128)}, f32[2048]{0:T(1024)}, f32[2048]{0:T(1024)}) all-reduce(f32[2048]{0:T(1024)S(1)} %get-tuple-element.1320, f32[16]{0:T(128)S(1)} %multiply_dynamic-update-slice_fusion, f32[16]{0:T(128)S(1)} %dynamic_update_slice.74, ...), channel_id=1, replica_groups=mesh['dp'=8,'tensor'=4] {'dp','tensor'}, use_global_device_ids=true, to_apply=%region_42.43 | all-reduce | flops 6176 | bytes 49408 | tf_op jit(solution)/shard_map/psum | solution.py:400
  2294.3 99.0 %reduce-scatter.21.cloned.1.call-done = f32[256,2048]{1,0:T(8,128)} async-done(((f32[1024,2048]{1,0:T(8,128)}), f32[256,2048]{1,0:T(8,128)}) %reduce-scatter.21.cloned.1.call-update) | async-done | bytes 2097168 | tf_op jit(solution)/shard_map/reduce_scatter | solution.py:319
  2399.9 85.0 %reduce-scatter.37.cloned.1.call-done = f32[256,1408]{1,0:T(8,128)} async-done(((f32[2048,1408]{1,0:T(8,128)}), f32[256,1408]{1,0:T(8,128)}) %reduce-scatter.37.cloned.1.call-update) | async-done | bytes 1441808 | tf_op jit(solution)/shard_map/reduce_scatter | solution.py:193
  2484.9 90.8 %reduce-scatter.39.cloned.1.call-done = f32[256,1408]{1,0:T(8,128)} async-done(((f32[2048,1408]{1,0:T(8,128)}), f32[256,1408]{1,0:T(8,128)}) %reduce-scatter.39.cloned.1.call-update) | async-done | bytes 1441808 | tf_op jit(solution)/shard_map/reduce_scatter | solution.py:194
  2575.7 90.7 %reduce-scatter.41.cloned.1.call-done = f32[1408,256]{1,0:T(8,128)} async-done(((f32[1408,2048]{1,0:T(8,128)}), f32[1408,256]{1,0:T(8,128)}) %reduce-scatter.41.cloned.1.call-update) | async-done | bytes 1441808 | tf_op jit(solution)/shard_map/reduce_scatter | solution.py:195
  2666.5 55.2 %reduce-scatter.35.cloned.1.call-done = f32[512,256]{1,0:T(8,128)} async-done(((f32[512,2048]{1,0:T(8,128)}), f32[512,256]{1,0:T(8,128)}) %reduce-scatter.35.cloned.1.call-update) | async-done | bytes 524304 | tf_op jit(solution)/shard_map/reduce_scatter | solution.py:397
  2721.7 55.7 %reduce-scatter.33.cloned.1.call-done = f32[256,512]{1,0:T(8,128)} async-done(((f32[2048,512]{1,0:T(8,128)}), f32[256,512]{1,0:T(8,128)}) %reduce-scatter.33.cloned.1.call-update) | async-done | bytes 524304 | tf_op jit(solution)/shard_map/reduce_scatter | solution.py:396
  2777.3 55.1 %reduce-scatter.27.cloned.1.call-done = f32[256,512]{1,0:T(8,128)} async-done(((f32[2048,512]{1,0:T(8,128)}), f32[256,512]{1,0:T(8,128)}) %reduce-scatter.27.cloned.1.call-update) | async-done | bytes 524304 | tf_op jit(solution)/shard_map/reduce_scatter | solution.py:391
  2832.4 55.7 %reduce-scatter.29.cloned.1.call-done = f32[256,512]{1,0:T(8,128)} async-done(((f32[2048,512]{1,0:T(8,128)}), f32[256,512]{1,0:T(8,128)}) %reduce-scatter.29.cloned.1.call-update) | async-done | bytes 524304 | tf_op jit(solution)/shard_map/reduce_scatter | solution.py:392
  2888.1 55.3 %reduce-scatter.31.cloned.1.call-done = f32[256,512]{1,0:T(8,128)} async-done(((f32[2048,512]{1,0:T(8,128)}), f32[256,512]{1,0:T(8,128)}) %reduce-scatter.31.cloned.1.call-update) | async-done | bytes 524304 | tf_op jit(solution)/shard_map/reduce_scatter | solution.py:393
  (3068 shorter events, 1344.5 us)
Async XLA Ops:
  7.2 626.9 %copy-start = (bf16[512,2048]{1,0:T(8,128)(2,1)S(1)}, bf16[512,2048]{1,0:T(8,128)(2,1)}, u32[]{:S(2)}) copy-start(bf16[512,2048]{1,0:T(8,128)(2,1)} %param.49) | copy-start | bytes 6291460
  7.2 85.0 %all-gather.12.cloned.1.call-start = ((), (), s32[]{:S(2)}) async-start(), calls=%async_computation.14 | async-start | bytes 5242880 | tf_op jit(solution)/shard_map/all_gather | solution.py:246
  12.6 332.3 %all-gather.18.cloned.1.call-start = ((), (), s32[]{:S(2)}) async-start(), calls=%async_computation.30 | async-start | bytes 2359296 | tf_op jit(solution)/shard_map/all_gather | solution.py:23
  102.3 7.7 collective-permute-start
  315.6 59.7 %all-gather.20.cloned.1.call-start = ((), (), s32[]{:S(2)}) async-start(), calls=%async_computation.31 | async-start | bytes 2359296 | tf_op jit(solution)/shard_map/all_gather | solution.py:23
  316.3 467.8 %reduce-scatter.19.cloned.1.call-start = ((), (), s32[]{:S(2)}) async-start(), calls=%async_computation.15 | async-start | bytes 10485760 | tf_op jit(solution)/shard_map/reduce_scatter | solution.py:307
  639.8 228.4 %all-gather.14.cloned.1.call-start = ((), (), s32[]{:S(2)}) async-start(), calls=%async_computation.16 | async-start | bytes 5242880 | tf_op jit(solution)/shard_map/all_gather | solution.py:315
  786.7 289.0 %copy-start.61 = (f32[256]{0:T(256)}, f32[256]{0:T(256)S(1)}, u32[]{:S(2)}) copy-start(f32[256]{0:T(256)S(1)} %fusion.274) | copy-start | bytes 3076
  788.7 283.5 %reduce-scatter.23.cloned.1.call-start = ((), (), s32[]{:S(2)}) async-start(), calls=%async_computation.18 | async-start | bytes 10485760 | tf_op jit(solution)/shard_map/reduce_scatter | solution.py:335
  926.9 231.4 %all-gather.16.cloned.1.call-start = ((), (), s32[]{:S(2)}) async-start(), calls=%async_computation.19 | async-start | bytes 5242880 | tf_op jit(solution)/shard_map/all_gather | solution.py:347
  1078.8 252.8 %all-gather.22.cloned.1.call-start = ((), (), s32[]{:S(2)}) async-start(), calls=%async_computation.32 | async-start | bytes 2359296 | tf_op jit(solution)/shard_map/all_gather | solution.py:23
  1079.7 280.8 %all-gather.24.cloned.1.call-start = ((), (), s32[]{:S(2)}) async-start(), calls=%async_computation.33 | async-start | bytes 2359296 | tf_op jit(solution)/shard_map/all_gather | solution.py:23
  1331.4 698.0 %reduce-scatter.45.cloned.1.call-start = ((), (), s32[]{:S(2)}) async-start(), calls=%async_computation.35 | async-start | bytes 1179648
  1378.9 468.4 %copy-start.39 = (f32[1024,4]{0,1:T(4,128)S(1)}, f32[1024,4]{0,1:T(4,128)}, u32[]{:S(2)}) copy-start(f32[1024,4]{0,1:T(4,128)} %copy-done.38) | copy-start | bytes 49156
  1882.5 22.2 collective-permute-start.1
  1895.4 135.6 %reduce-scatter.43.cloned.1.call-start = ((), (), s32[]{:S(2)}) async-start(), calls=%async_computation.34 | async-start | bytes 1179648
  1899.9 199.3 %all-reduce.18.cloned.1.call-start = ((), (), s32[]{:S(2)}) async-start(), calls=%async_computation.25 | async-start | bytes 196608 | tf_op jit(solution)/shard_map/psum | solution.py:400
  1904.7 340.1 %reduce-scatter.25.cloned.1.call-start = ((), (), s32[]{:S(2)}) async-start(), calls=%async_computation.20 | async-start | bytes 10485760 | tf_op jit(solution)/shard_map/reduce_scatter | solution.py:378
  1944.1 449.1 %reduce-scatter.21.cloned.1.call-start = ((), (), s32[]{:S(2)}) async-start(), calls=%async_computation.17 | async-start | bytes 10485760 | tf_op jit(solution)/shard_map/reduce_scatter | solution.py:319
  1955.9 529.0 %reduce-scatter.37.cloned.1.call-start = ((), (), s32[]{:S(2)}) async-start(), calls=%async_computation.27 | async-start | bytes 12976128 | tf_op jit(solution)/shard_map/reduce_scatter | solution.py:193
  1967.9 607.8 %reduce-scatter.39.cloned.1.call-start = ((), (), s32[]{:S(2)}) async-start(), calls=%async_computation.28 | async-start | bytes 12976128 | tf_op jit(solution)/shard_map/reduce_scatter | solution.py:194
  1980.1 686.4 %reduce-scatter.41.cloned.1.call-start = ((), (), s32[]{:S(2)}) async-start(), calls=%async_computation.29 | async-start | bytes 12976128 | tf_op jit(solution)/shard_map/reduce_scatter | solution.py:195
  1991.5 730.2 %reduce-scatter.35.cloned.1.call-start = ((), (), s32[]{:S(2)}) async-start(), calls=%async_computation.26 | async-start | bytes 4718592 | tf_op jit(solution)/shard_map/reduce_scatter | solution.py:397
  1999.3 778.0 %reduce-scatter.33.cloned.1.call-start = ((), (), s32[]{:S(2)}) async-start(), calls=%async_computation.24 | async-start | bytes 4718592 | tf_op jit(solution)/shard_map/reduce_scatter | solution.py:396
  2007.1 825.3 %reduce-scatter.27.cloned.1.call-start = ((), (), s32[]{:S(2)}) async-start(), calls=%async_computation.21 | async-start | bytes 4718592 | tf_op jit(solution)/shard_map/reduce_scatter | solution.py:391
  2014.4 873.7 %reduce-scatter.29.cloned.1.call-start = ((), (), s32[]{:S(2)}) async-start(), calls=%async_computation.22 | async-start | bytes 4718592 | tf_op jit(solution)/shard_map/reduce_scatter | solution.py:392
  2021.3 922.0 %reduce-scatter.31.cloned.1.call-start = ((), (), s32[]{:S(2)}) async-start(), calls=%async_computation.23 | async-start | bytes 4718592 | tf_op jit(solution)/shard_map/reduce_scatter | solution.py:393
  2028.4 265.9 %copy-start.74 = (f32[256]{0:T(256)S(1)}, f32[256]{0:T(256)}, u32[]{:S(2)}) copy-start(f32[256]{0:T(256)} %copy-done.73) | copy-start | bytes 3076
  2028.4 364.9 %copy-start.43 = (f32[2048]{0:T(1024)S(1)}, f32[2048]{0:T(1024)}, u32[]{:S(2)}) copy-start(f32[2048]{0:T(1024)} %param.50) | copy-start | bytes 24580
  2028.4 364.9 %copy-start.62 = (f32[256]{0:T(256)S(1)}, f32[256]{0:T(256)}, u32[]{:S(2)}) copy-start(f32[256]{0:T(256)} %copy-done.61) | copy-start | bytes 3076
  2028.4 364.9 %copy-start.72 = (f32[256]{0:T(256)S(1)}, f32[256]{0:T(256)}, u32[]{:S(2)}) copy-start(f32[256]{0:T(256)} %copy-done.71) | copy-start | bytes 3076
  2393.3 550.1 %copy-start.1 = (bf16[512,2048]{1,0:T(8,128)(2,1)S(1)}, bf16[512,2048]{1,0:T(8,128)(2,1)}, u32[]{:S(2)}) copy-start(bf16[512,2048]{1,0:T(8,128)(2,1)} %param.49) | copy-start | bytes 6291460
  (97 other events, 2525.1 us)
Sparse Core Ops, SparseCore 0:
  12.7 79.4 all-gather.11
  315.7 29.1 all-gather.17
  347.4 27.8 all-gather.19
  639.9 144.2 reduce-scatter.18
  788.8 79.3 all-gather.13
  927.0 145.1 reduce-scatter.22
  1078.9 79.3 all-gather.15
  1160.7 28.7 all-gather.21
  1331.6 28.8 all-gather.23
  1895.5 35.9 reduce-scatter.44
  1935.3 36.0 reduce-scatter.42
  1976.7 122.4 all-reduce.17
  2101.5 143.1 reduce-scatter.24
  2247.0 146.2 reduce-scatter.20
  2397.2 87.7 reduce-scatter.36
  2488.9 86.8 reduce-scatter.38
  2579.6 86.7 reduce-scatter.40
  2670.3 51.3 reduce-scatter.34
  2726.0 51.3 reduce-scatter.32
  2781.1 51.2 reduce-scatter.26
  2836.7 51.3 reduce-scatter.28
  2892.0 51.2 reduce-scatter.30
where the time goes:
time: 2960 us; the launch traced here: 2950 us
  waiting for transfers between devices  1440 us (49%)
  matrix products  1020 us (34%)
  local copies, waits for them, and re-layouts  230 us (8%)
  other arithmetic  166 us (6%)
  blocking collectives  47.2 us (2%)
    dot_general x1630, matrix products, batched(): return jnp.einsum(form, left, right, precision=HIGHEST_PRECISION)  791 us
    reduce_scatter x1, waiting for transfers between devices, local(): lax.psum_scatter(contract_cols(grad_gate, w_gate) + contract_cols(grad_up...  145 us
    reduce_scatter x1, waiting for transfers between devices, local(): lax.psum_scatter(jnp.dot(mixed_low, w_out, preferred_element_type=jnp.flo...  144 us
    reduce_scatter x1, waiting for transfers between devices, local(): lax.psum_scatter(summed + contract_cols(grad_gate_low, w_gate_out), 'tens...  144 us
    reduce_scatter x1, waiting for transfers between devices, local(): lax.psum_scatter(jnp.dot(activated, w_down, preferred_element_type=jnp.fl...  99 us
    dot_general x10, matrix products, contract_cols(): lax.dot_general(left, right, (((1,), (1,)), ((), ())), preferred_element_...  93.9 us
    reduce_scatter x1, waiting for transfers between devices, sum_mlp_grads(): lax.psum_scatter(up_part, 'dp', scatter_dimension=0, tiled=True)  90.8 us
    reduce_scatter x1, waiting for transfers between devices, sum_mlp_grads(): lax.psum_scatter(down_part, 'dp', scatter_dimension=1, tiled=True)  90.7 us
  transfers between devices with their start and end apart: 24, of which 19 were waited for; matrix products, arithmetic and copies ran while one was open for 12% of the time, Pallas kernels for 0%

commit v1 on v0

v1 whole, which is shorter than its diff:
```python
import functools
import math

import jax
import jax.numpy as jnp
from jax import lax
from jax.experimental import pallas as pl
from jax.experimental.pallas import tpu as pltpu
from jax.sharding import PartitionSpec as P

CHUNK = 128
HALO = 16
epsilon = 1e-06
F32 = jnp.float32
LOW = jnp.bfloat16
NN = (((1,), (0,)), ((), ()))
NT = (((1,), (1,)), ((), ()))
TN = (((0,), (0,)), ((), ()))


def mm(left, right, dims=NN):
    return lax.dot_general(
        left, right, dims, precision=lax.Precision.HIGH, preferred_element_type=F32
    )


def mm_full(left, right, dims=NN):
    return lax.dot_general(
        left, right, dims, precision=lax.Precision.HIGHEST, preferred_element_type=F32
    )


def iota(shape, dim):
    return lax.broadcasted_iota(jnp.int32, shape, dim)


def doc_of(positions, scalars, docs):
    total = jnp.zeros_like(positions) - 1
    for j in range(docs):
        total = total + jnp.where(positions >= scalars[1 + j], 1, 0)
    return total


def chunk_masks(position, scalars, docs):
    shape = (CHUNK, CHUNK)
    row, col = iota(shape, 0), iota(shape, 1)
    doc_row = doc_of(row + position, scalars, docs)
    doc_col = doc_of(col + position, scalars, docs)
    same = doc_row == doc_col
    prior = jnp.int32(-1)
    last = jnp.int32(-1)
    for j in range(docs):
        prior = prior + jnp.where(position - 1 >= scalars[1 + j], 1, 0)
        last = last + jnp.where(position + CHUNK - 1 >= scalars[1 + j], 1, 0)
    return {
        "row": row,
        "col": col,
        "inside": same & (row >= col),
        "strict": same & (row > col),
        "carried": (doc_row == prior)[:, :1],
        "in_last": (doc_row == last)[:, :1],
        "last_carried": last == prior,
        "back": [
            None if s == 0 else (doc_row == doc_of(row + (position - s), scalars, docs))[:, :1]
            for s in range(4)
        ],
    }


def shifted_rows(main, before, back):
    ext = jnp.concatenate([before[HALO - 8 :], main], axis=0)
    rows = [main]
    for s in range(1, 4):
        rows.append(jnp.where(back[s], pltpu.roll(ext, s, 0)[8:], 0.0))
    return rows


def conv_sum(rows, taps):
    total = rows[0] * taps[3:4, :]
    for s in range(1, 4):
        total = total + rows[s] * taps[3 - s : 4 - s, :]
    return total


def softplus(x):
    return jnp.maximum(x, 0.0) + jnp.log1p(jnp.exp(-jnp.abs(x)))


def gates(narrow, params, masks):
    shifted = narrow + params[0:1, :]
    rate = -jnp.exp(params[1:2, :])
    decays = rate * softplus(shifted)
    lower = jnp.where(masks["row"] >= masks["col"], 1.0, 0.0)
    total = mm_full(lower, decays)
    return shifted, rate, decays, jax.nn.sigmoid(narrow), total, total.T


def decay_terms(h, total, total_row, masks):
    col = total[:, h : h + 1]
    row = total_row[h : h + 1, :]
    spread = jnp.where(
        masks["inside"], jnp.exp(jnp.where(masks["inside"], col - row, 0.0)), 0.0
    )
    start = jnp.where(masks["carried"], jnp.exp(col), 0.0)
    end = total[CHUNK - 1 : CHUNK, h : h + 1]
    to_last = jnp.where(masks["in_last"], jnp.exp(jnp.where(masks["in_last"], end - col, 0.0)), 0.0)
    keep = jnp.where(masks["last_carried"], jnp.exp(end), 0.0)
    return spread, start, to_last, keep


def lanes(h):
    return slice(h * 128, h * 128 + 128)


def features(pieces, befores, taps, masks, heads):
    out = []
    for i in range(3):
        rows = shifted_rows(pieces[i], befores[i], masks["back"])
        pre = conv_sum(rows, taps[4 * i : 4 * i + 4, :])
        out.append((rows, pre, jax.nn.sigmoid(pre)))
    return out


def unit(values):
    return lax.rsqrt(jnp.sum(values * values, axis=-1, keepdims=True) + epsilon)


def load_pieces(step, mains, priors, rims):
    pieces = [m[...].astype(F32) for m in mains]
    befores = [
        jnp.where(step == 0, r[...].astype(F32), p[...].astype(F32)) for p, r in zip(priors, rims)
    ]
    return pieces, befores


def intra_kernel(docs, heads, scalars, *refs):
    mains, priors, rims = refs[0:3], refs[3:6], refs[6:9]
    narrow_ref, taps_ref, params_ref = refs[9:12]
    x_ref, p_ref, kg_ref, w_ref, u_ref, qt_ref, ou_ref, t_ref, o_ref, tot_ref = refs[12:22]
    run = refs[22]
    step = pl.program_id(0)
    position = scalars[0] + step * CHUNK
    masks = chunk_masks(position, scalars, docs)
    pieces, befores = load_pieces(step, mains, priors, rims)
    feats = features(pieces, befores, taps_ref[...], masks, heads)
    _, _, _, beta, total, total_row = gates(narrow_ref[...], params_ref[...], masks)
    eye = jnp.where(masks["row"] == masks["col"], 1.0, 0.0)
    conv = [pre * sg for _, pre, sg in feats]
    hs = range(heads)
    q, k, v, terms, b = [], [], [], [], []
    for h in hs:
        cq, ck = conv[0][:, lanes(h)], conv[1][:, lanes(h)]
        q.append(cq * (unit(cq) * (1.0 / math.sqrt(128.0))))
        k.append(ck * unit(ck))
        v.append(conv[2][:, lanes(h)])
        terms.append(decay_terms(h, total, total_row, masks))
        b.append(beta[:, heads + h : heads + h + 1])
    kg = [jnp.where(masks["strict"], mm(k[h], k[h], NT) * terms[h][0], 0.0) for h in hs]
    p = [mm(q[h], k[h], NT) * terms[h][0] for h in hs]
    a = [b[h] * kg[h] for h in hs]
    pair = (masks["row"] >> 1) == (masks["col"] >> 1)
    x = [eye - jnp.where(pair, a[h], 0.0) for h in hs]
    for level in range(1, 7):
        wide = (masks["row"] >> (level + 1)) == (masks["col"] >> (level + 1))
        off = wide & ((masks["row"] >> level) != (masks["col"] >> level))
        lx = [mm(jnp.where(off, a[h], 0.0), x[h]) for h in hs]
        x = [x[h] - mm(x[h], lx[h]) for h in hs]
    wu = [
        mm(x[h], jnp.concatenate([(b[h] * terms[h][1]) * k[h], b[h] * v[h]], axis=1)) for h in hs
    ]
    pwu = [mm(p[h], wu[h]) for h in hs]
    kwu = [mm(terms[h][2] * k[h], wu[h], TN) for h in hs]

    @pl.when(step == 0)
    def _():
        for h in hs:
            run[h] = jnp.concatenate([jnp.zeros((128, 128), F32), eye], axis=1)

    for h in hs:
        x_ref[0, h] = x[h]
        p_ref[0, h] = p[h]
        kg_ref[0, h] = kg[h]
        w_ref[:, lanes(h)] = wu[h][:, :128]
        u_ref[:, lanes(h)] = wu[h][:, 128:]
        qt_ref[:, lanes(h)] = terms[h][1] * q[h] - pwu[h][:, :128]
        ou_ref[:, lanes(h)] = pwu[h][:, 128:]
        transfer = terms[h][3] * eye - kwu[h][:, :128]
        offset = kwu[h][:, 128:]
        t_ref[0, h] = transfer
        o_ref[0, h] = offset
        new = mm(transfer, run[h])
        new = jnp.concatenate([new[:, :128] + offset, new[:, 128:]], axis=1)
        run[h] = new
        tot_ref[h] = new


def rows_spec(width, chunks, reverse=False):
    if reverse:
        return pl.BlockSpec((CHUNK, width), lambda c, *_: (chunks - 1 - c, 0))
    return pl.BlockSpec((CHUNK, width), lambda c, *_: (c, 0))


def halo_spec(width, chunks, reverse=False):
    per = CHUNK // HALO
    if reverse:
        return pl.BlockSpec(
            (HALO, width), lambda c, *_: (jnp.maximum((chunks - 1 - c) * per - 1, 0), 0)
        )
    return pl.BlockSpec((HALO, width), lambda c, *_: (jnp.maximum(c * per - 1, 0), 0))


def tile_spec(heads, chunks, reverse=False):
    if reverse:
        return pl.BlockSpec((1, heads, 128, 128), lambda c, *_: (chunks - 1 - c, 0, 0, 0))
    return pl.BlockSpec((1, heads, 128, 128), lambda c, *_: (c, 0, 0, 0))


def whole_spec(*shape):
    zeros = (0,) * len(shape)
    return pl.BlockSpec(shape, lambda c, *_: zeros)


def sds(*shape, dtype=F32):
    return jax.ShapeDtypeStruct(shape, dtype)


PARAMS = dict(vmem_limit_bytes=56 * 1024 * 1024, dimension_semantics=("arbitrary",))


def cost(flops, moved):
    return pl.CostEstimate(flops=int(flops), bytes_accessed=int(moved), transcendentals=0)


def intra(scalars, pieces, rims, narrow, taps, params, docs, heads):
    rows, width = pieces[0].shape
    chunks = rows // CHUNK
    tiles, flat = sds(chunks, heads, 128, 128), sds(rows, width)
    return pl.pallas_call(
        functools.partial(intra_kernel, docs, heads),
        out_shape=(tiles, tiles, tiles, flat, flat, flat, flat, tiles, tiles, sds(heads, 128, 256)),
        grid_spec=pltpu.PrefetchScalarGridSpec(
            num_scalar_prefetch=1,
            grid=(chunks,),
            in_specs=[rows_spec(width, chunks)] * 3
            + [halo_spec(width, chunks)] * 3
            + [whole_spec(HALO, width)] * 3
            + [rows_spec(128, chunks), whole_spec(16, width), whole_spec(8, 128)],
            out_specs=[tile_spec(heads, chunks)] * 3
            + [rows_spec(width, chunks)] * 4
            + [tile_spec(heads, chunks)] * 2
            + [whole_spec(heads, 128, 256)],
            scratch_shapes=[pltpu.VMEM((heads, 128, 256), F32)],
        ),
        compiler_params=pltpu.CompilerParams(**PARAMS),
        cost_estimate=cost(chunks * heads * 60 * 3 * 2 * 128**3, 30 * rows * width * 4),
        name="intra",
    )(scalars, *pieces, *pieces, *rims, narrow, taps, params)


def outward_kernel(heads, s_in, w_ref, u_ref, qt_ref, ou_ref, t_ref, o_ref, gate_ref, gain_ref,
                   out_ref, v2_ref, s_ref, mixed_ref, run):
    step = pl.program_id(0)

    @pl.when(step == 0)
    def _():
        run[...] = s_in[...]

    hs = range(heads)
    state = [run[h] for h in hs]
    full = [
        mm(
            jnp.concatenate([qt_ref[:, lanes(h)], w_ref[:, lanes(h)], t_ref[0, h]], axis=0),
            state[h],
        )
        for h in hs
    ]
    for h in hs:
        out = full[h][:128] + ou_ref[:, lanes(h)]
        v2_ref[:, lanes(h)] = u_ref[:, lanes(h)] - full[h][128:256]
        s_ref[0, h] = state[h]
        run[h] = full[h][256:] + o_ref[0, h]
        out_ref[:, lanes(h)] = out
        gate = gate_ref[:, lanes(h)]
        scale = lax.rsqrt(jnp.mean(out * out, axis=-1, keepdims=True) + epsilon)
        mixed_ref[:, lanes(h)] = (
            out * scale * gain_ref[0:1, lanes(h)] * (gate * jax.nn.sigmoid(gate))
        ).astype(LOW)


def outward(s_in, w, u, qt, ou, t, o, gate, gain, heads):
    rows, width = w.shape
    chunks = rows // CHUNK
    flat, tiles = rows_spec(width, chunks), tile_spec(heads, chunks)
    return pl.pallas_call(
        functools.partial(outward_kernel, heads),
        out_shape=(sds(rows, width), sds(rows, width), sds(chunks, heads, 128, 128), sds(rows, width, dtype=LOW)),
        grid=(chunks,),
        in_specs=[whole_spec(heads, 128, 128), flat, flat, flat, flat, tiles, tiles, flat, whole_spec(8, width)],
        out_specs=[flat, flat, tiles, flat],
        scratch_shapes=[pltpu.VMEM((heads, 128, 128), F32)],
        compiler_params=pltpu.CompilerParams(**PARAMS),
        cost_estimate=cost(chunks * heads * 9 * 2 * 128**3, 11 * rows * width * 4),
        name="outward",
    )(s_in, w, u, qt, ou, t, o, gate, gain)


def inward_kernel(heads, gm_ref, out_ref, gate_ref, gain_ref, qt_ref, t_ref,
                  do_ref, dgate_ref, dgain_ref, tot_ref, run):
    step = pl.program_id(0)

    @pl.when(step == 0)
    def _():
        run[...] = jnp.zeros_like(run)
        dgain_ref[...] = jnp.zeros_like(dgain_ref)

    hs = range(heads)
    grads = []
    for h in hs:
        out, gate, gm = out_ref[:, lanes(h)], gate_ref[:, lanes(h)], gm_ref[:, lanes(h)]
        gain = gain_ref[0:1, lanes(h)]
        scale = lax.rsqrt(jnp.mean(out * out, axis=-1, keepdims=True) + epsilon)
        normed = out * scale
        sg = jax.nn.sigmoid(gate)
        act = gate * sg
        gn = gm * normed
        dgate_ref[:, lanes(h)] = (gn * gain * (sg * (1.0 + gate * (1.0 - sg)))).astype(LOW)
        dgain_ref[:, lanes(h)] += jnp.sum((gn * act).reshape(CHUNK // 8, 8, 128), axis=0)
        dn = gm * gain * act
        do = scale * (dn - normed * jnp.mean(dn * normed, axis=-1, keepdims=True))
        do_ref[:, lanes(h)] = do
        grads.append(do)
    for h in hs:
        left = jnp.concatenate([qt_ref[:, lanes(h)], t_ref[0, h]], axis=0)
        new = mm(left, jnp.concatenate([grads[h], run[h]], axis=0), TN)
        run[h] = new
        tot_ref[h] = new


def inward(gm, out, gate, gain, qt, t, heads):
    rows, width = gm.shape
    chunks = rows // CHUNK
    flat, tiles = rows_spec(width, chunks, True), tile_spec(heads, chunks, True)
    return pl.pallas_call(
        functools.partial(inward_kernel, heads),
        out_shape=(sds(rows, width), sds(rows, width, dtype=LOW), sds(8, width), sds(heads, 128, 128)),
        grid=(chunks,),
        in_specs=[flat, flat, flat, whole_spec(8, width), flat, tiles],
        out_specs=[flat, flat, whole_spec(8, width), whole_spec(heads, 128, 128)],
        scratch_shapes=[pltpu.VMEM((heads, 128, 128), F32)],
        compiler_params=pltpu.CompilerParams(**PARAMS),
        cost_estimate=cost(chunks * heads * 6 * 2 * 128**3, 7 * rows * width * 4),
        name="inward",
    )(gm, out, gate, gain, qt, t)


def back_kernel(docs, heads, chunks, scalars, *refs):
    mains, priors, rims = refs[0:3], refs[3:6], refs[6:9]
    narrow_ref, taps_ref, params_ref, ds_in = refs[9:13]
    (do_ref, v2_ref, s_ref, x_ref, p_ref, kg_ref, w_ref, u_ref, qt_ref, t_ref) = refs[13:23]
    gq_ref, gk_ref, gv_ref, tail_ref, rim_ref, gnarrow_ref, gtaps_ref, gparams_ref = refs[23:31]
    run, after = refs[31:33]
    rev = pl.program_id(0)
    step = chunks - 1 - rev
    position = scalars[0] + step * CHUNK

    @pl.when(rev == 0)
    def _():
        run[...] = ds_in[...]
        after[...] = jnp.zeros_like(after)
        gtaps_ref[...] = jnp.zeros_like(gtaps_ref)
        gparams_ref[...] = jnp.zeros_like(gparams_ref)

    masks = chunk_masks(position, scalars, docs)
    pieces, befores = load_pieces(step, mains, priors, rims)
    taps = taps_ref[...]
    feats = features(pieces, befores, taps, masks, heads)
    shifted, rate, decays, beta, total, total_row = gates(narrow_ref[...], params_ref[...], masks)
    conv = [pre * sg for _, pre, sg in feats]
    lane = masks["col"]
    hs = range(heads)
    q, k, v, uq, uk, terms, b = [], [], [], [], [], [], []
    root = 1.0 / math.sqrt(128.0)
    for h in hs:
        cq, ck = conv[0][:, lanes(h)], conv[1][:, lanes(h)]
        uq.append(unit(cq))
        uk.append(unit(ck))
        q.append(cq * (uq[h] * root))
        k.append(ck * uk[h])
        v.append(conv[2][:, lanes(h)])
        terms.append(decay_terms(h, total, total_row, masks))
        b.append(beta[:, heads + h : heads + h + 1])
    do = [do_ref[:, lanes(h)] for h in hs]
    v2 = [v2_ref[:, lanes(h)] for h in hs]
    dsn = [run[h] for h in hs]
    kt = [terms[h][2] * k[h] for h in hs]
    dv2 = [mm(p_ref[0, h], do[h], TN) + mm(kt[h], dsn[h]) for h in hs]
    for h in hs:
        left = jnp.concatenate([qt_ref[:, lanes(h)], t_ref[0, h]], axis=0)
        run[h] = mm(left, jnp.concatenate([do[h], dsn[h]], axis=0), TN)
    states = [s_ref[0, h] for h in hs]
    both = [mm(jnp.concatenate([do[h], dv2[h]], axis=0), states[h], NT) for h in hs]
    dp = [jnp.where(masks["inside"], mm(do[h], v2[h], NT), 0.0) for h in hs]
    dkt = [mm(v2[h], dsn[h], NT) for h in hs]
    dx = [mm(x_ref[0, h], jnp.concatenate([-both[h][128:], dv2[h]], axis=1), TN) for h in hs]
    da = [
        jnp.where(
            masks["strict"],
            -mm(dx[h], jnp.concatenate([w_ref[:, lanes(h)], u_ref[:, lanes(h)]], axis=1), NT),
            0.0,
        )
        for h in hs
    ]
    gdecay = jnp.zeros((CHUNK, CHUNK), F32)
    gbeta = jnp.zeros((CHUNK, CHUNK), F32)
    minus = jnp.zeros((CHUNK, CHUNK), F32)
    dq, dk, dv = [], [], []
    for h in hs:
        spread, start, to_last, keep = terms[h]
        doq = both[h][:128]
        dqk = dp[h] * spread
        kgh = kg_ref[0, h]
        z = da[h] * kgh
        dkk = b[h] * da[h] * spread
        dxk, dxv = dx[h][:, :128], dx[h][:, 128:]
        stacked = jnp.concatenate([dqk, dkk], axis=0)
        forward = mm(stacked, k[h])
        backward = mm(stacked, jnp.concatenate([q[h], k[h]], axis=0), TN)
        kx = jnp.sum(k[h] * dxk, axis=-1, keepdims=True)
        dq.append(start * doq + forward[:128])
        dk.append(
            backward + forward[128:] + to_last * dkt[h] + (b[h] * start) * dxk
        )
        dv.append(b[h] * dxv)
        gb = (
            jnp.sum(z, axis=-1, keepdims=True)
            + jnp.sum(v[h] * dxv, axis=-1, keepdims=True)
            + start * kx
        )
        gamgrad = b[h] * z + dp[h] * p_ref[0, h]
        dstart = jnp.sum(q[h] * doq, axis=-1, keepdims=True) + b[h] * kx
        dlast = jnp.sum(k[h] * dkt[h], axis=-1, keepdims=True) * to_last
        dkeep = jnp.sum(states[h] * dsn[h], keepdims=True) * keep
        gcol = jnp.sum(gamgrad, axis=-1, keepdims=True) + dstart * start - dlast
        end = jnp.sum(dlast, keepdims=True) + dkeep
        gcol = gcol + jnp.where(masks["row"][:, :1] == CHUNK - 1, end, 0.0)
        grow = jnp.sum(gamgrad, axis=0, keepdims=True)
        gdecay = jnp.where(lane == h, gcol, gdecay)
        gbeta = jnp.where(lane == heads + h, gb, gbeta)
        minus = jnp.where(masks["row"] == h, grow, minus)
    gdecay = gdecay - minus.T
    upper = jnp.where(masks["row"] <= masks["col"], 1.0, 0.0)
    dg = mm_full(upper, gdecay)
    galpha = dg * rate * jax.nn.sigmoid(shifted)
    gnarrow_ref[...] = jnp.where(lane < heads, galpha, gbeta * beta * (1.0 - beta)).astype(LOW)
    gparams_ref[0:8, :] += jnp.sum((galpha).reshape(CHUNK // 8, 8, 128), axis=0)
    gparams_ref[8:16, :] += jnp.sum((dg * decays).reshape(CHUNK // 8, 8, 128), axis=0)

    outs = (gq_ref, gk_ref, gv_ref)
    for i in range(3):
        rows, pre, sg = feats[i]
        pieces_d = []
        for h in hs:
            if i == 2:
                pieces_d.append(dv[h])
            else:
                inv = uq[h] if i == 0 else uk[h]
                grad = dq[h] * root if i == 0 else dk[h]
                normal = conv[i][:, lanes(h)] * inv
                pieces_d.append(
                    inv * (grad - normal * jnp.sum(grad * normal, axis=-1, keepdims=True))
                )
        dc = jnp.concatenate(pieces_d, axis=1)
        ds = dc * (sg * (1.0 + pre * (1.0 - sg)))
        grad = ds * taps[4 * i + 3 : 4 * i + 4, :]
        rim = jnp.zeros((8, ds.shape[1]), F32)
        gtaps_ref[4 * i + 3] += jnp.sum((ds * rows[0]).reshape(CHUNK // 8, 8, -1), axis=0)
        for s in range(1, 4):
            tap = taps[4 * i + 3 - s : 4 * i + 4 - s, :]
            masked = jnp.where(masks["back"][s], ds, 0.0)
            gtaps_ref[4 * i + 3 - s] += jnp.sum((ds * rows[s]).reshape(CHUNK // 8, 8, -1), axis=0)
            ext = jnp.concatenate([masked, after[3 * i + s - 1]], axis=0)
            grad = grad + pltpu.roll(ext, CHUNK + 8 - s, 0)[:CHUNK] * tap
            after[3 * i + s - 1] = masked[:8]
            front = jnp.concatenate([jnp.zeros_like(masked[:8]), masked[:8]], axis=0)
            rim = rim + pltpu.roll(front, 16 - s, 0)[:8] * tap
        outs[i][...] = grad.astype(LOW)
        rim_ref[i] = rim

        @pl.when(rev == 0)
        def _():
            tail_ref[i] = grad[CHUNK - HALO :]


def back(scalars, pieces, rims, narrow, taps, params, ds_in, do, v2, s, x, p, kg, w, u, qt, t, docs, heads):
    rows, width = pieces[0].shape
    chunks = rows // CHUNK
    flat, tiles = rows_spec(width, chunks, True), tile_spec(heads, chunks, True)
    low = sds(rows, width, dtype=LOW)
    return pl.pallas_call(
        functools.partial(back_kernel, docs, heads, chunks),
        out_shape=(
            low, low, low, sds(3, HALO, width), sds(3, 8, width), sds(rows, 128, dtype=LOW),
            sds(12, 8, width), sds(16, 128),
        ),
        grid_spec=pltpu.PrefetchScalarGridSpec(
            num_scalar_prefetch=1,
            grid=(chunks,),
            in_specs=[flat] * 3
            + [halo_spec(width, chunks, True)] * 3
            + [whole_spec(HALO, width)] * 3
            + [rows_spec(128, chunks, True), whole_spec(16, width), whole_spec(8, 128)]
            + [whole_spec(heads, 128, 128), flat, flat, tiles, tiles, tiles, tiles, flat, flat, flat, tiles],
            out_specs=[flat] * 3
            + [whole_spec(3, HALO, width), whole_spec(3, 8, width), rows_spec(128, chunks, True)]
            + [whole_spec(12, 8, width), whole_spec(16, 128)],
            scratch_shapes=[pltpu.VMEM((heads, 128, 128), F32), pltpu.VMEM((9, 8, width), F32)],
        ),
        compiler_params=pltpu.CompilerParams(**PARAMS),
        cost_estimate=cost(chunks * heads * 60 * 2 * 128**3, 16 * rows * width * 4),
        name="back",
    )(scalars, *pieces, *pieces, *rims, narrow, taps, params, ds_in, do, v2, s, x, p, kg, w, u, qt, t)


def chain_kernel(heads, backward, scalars, *refs):
    mine, count = scalars[0], pl.num_programs(0)
    step = pl.program_id(0)
    out_ref = refs[-1]

    @pl.when(step == 0)
    def _():
        out_ref[...] = jnp.zeros_like(out_ref)

    if backward:
        maps_ref, sums_ref = refs[0], refs[1]

        @pl.when(count - 1 - step > mine)
        def _():
            for h in range(heads):
                out_ref[h] = mm(maps_ref[0, h][:, 128:], out_ref[h], TN) + sums_ref[0, h]
    else:
        maps_ref = refs[0]

        @pl.when(step < mine)
        def _():
            for h in range(heads):
                piece = maps_ref[0, h]
                out_ref[h] = mm(piece[:, 128:], out_ref[h]) + piece[:, :128]


def chain(mine, maps, sums, heads):
    count = maps.shape[0]
    backward = sums is not None
    at = (lambda c, *_: (count - 1 - c, 0, 0, 0)) if backward else (lambda c, *_: (c, 0, 0, 0))
    specs = [pl.BlockSpec((1, heads, 128, 256), at)]
    args = [maps]
    if backward:
        specs.append(pl.BlockSpec((1, heads, 128, 128), at))
        args.append(sums)
    return pl.pallas_call(
        functools.partial(chain_kernel, heads, backward),
        out_shape=sds(heads, 128, 128),
        grid_spec=pltpu.PrefetchScalarGridSpec(
            num_scalar_prefetch=1,
            grid=(count,),
            in_specs=specs,
            out_specs=whole_spec(heads, 128, 128),
        ),
        compiler_params=pltpu.CompilerParams(**PARAMS),
        cost_estimate=cost(count * heads * 3 * 2 * 128**3, count * heads * 3 * 128 * 128 * 4),
        name="chain",
    )(mine, *args)


def contract_rows(left, right):
    return lax.dot_general(left, right, TN, preferred_element_type=F32)


def contract_cols(left, right):
    return lax.dot_general(left, right, NT, preferred_element_type=F32)


def dot(left, right):
    return jnp.dot(left, right, preferred_element_type=F32)


def row_norm(values, gain):
    return values * lax.rsqrt(jnp.mean(values * values, axis=-1, keepdims=True) + epsilon) * gain


def norm_back(values, gain, grad):
    inv = lax.rsqrt(jnp.mean(values * values, axis=-1, keepdims=True) + epsilon)
    scaled = grad * gain
    inner = jnp.mean(scaled * values, axis=-1, keepdims=True)
    return inv * scaled - values * (inner * inv * inv * inv), jnp.sum(grad * values * inv, axis=0)


def after(values, *first):
    out = lax.optimization_barrier((values,) + first)
    return out[0]


def local(
    tokens,
    gain_in,
    w_query,
    w_key,
    w_value,
    w_alpha,
    w_beta,
    w_gate_out,
    conv_query,
    conv_key,
    conv_value,
    decay_log,
    decay_bias,
    head_gain,
    w_out,
    gain_mid,
    w_gate,
    w_up,
    w_down,
    out_grad,
    doc_lengths,
):
    rows_own, model = tokens.shape
    tensor_parts, dp_parts = lax.axis_size("tensor"), lax.axis_size("dp")
    tensor_index, dp_index = lax.axis_index("tensor"), lax.axis_index("dp")
    group_rows = rows_own * tensor_parts
    seq_total = group_rows * dp_parts
    heads = w_alpha.shape[1]
    width = w_query.shape[1]
    docs = doc_lengths.shape[0] * doc_lengths.shape[1]
    starts = (
        jnp.cumsum(doc_lengths, axis=1)
        - doc_lengths
        + seq_total * lax.broadcasted_iota(jnp.int32, doc_lengths.shape, 0)
    ).reshape(-1)
    scalars = jnp.concatenate([(dp_index * group_rows).reshape(1), starts]).astype(jnp.int32)
    mine = dp_index.reshape(1).astype(jnp.int32)
    taps = jnp.concatenate([conv_query, conv_key, conv_value, jnp.zeros((4, width), F32)])
    params = jnp.zeros((8, 128), F32).at[0, :heads].set(decay_bias).at[1, :heads].set(decay_log)
    gain_heads = jnp.broadcast_to(head_gain[None], (8, width))
    w_narrow = jnp.pad(jnp.concatenate([w_alpha, w_beta], axis=1), ((0, 0), (0, 128 - 2 * heads)))

    own_rows = tokens.astype(F32)
    normed_in = row_norm(own_rows, gain_in).astype(LOW)
    normed_all = lax.all_gather(normed_in, "tensor", axis=0, tiled=True)
    grad_act = contract_cols(out_grad, w_down)
    half = width // 2
    core = lax.rem(dp_index, 2)
    out_half = lax.dynamic_slice_in_dim(w_out, core * half, half, 0)
    out_mine = lax.all_gather(out_half, "tensor", axis=0)
    out_other = lax.ppermute(out_mine, "dp", [(i, i ^ 1) for i in range(dp_parts)])
    w_out_full = jnp.stack(
        [jnp.where(core == 0, out_mine, out_other), jnp.where(core == 0, out_other, out_mine)],
        axis=1,
    ).reshape(width * tensor_parts, model)

    pieces = [dot(normed_all, w).astype(LOW) for w in (w_query, w_key, w_value)]
    narrow = dot(normed_all, w_narrow)
    forth = [(i, i + 1) for i in range(dp_parts - 1)]
    rims = lax.ppermute(
        jnp.stack([piece[group_rows - HALO :] for piece in pieces]), "dp", forth
    )
    rims = [rims[i] for i in range(3)]
    x, p, kg, w, u, qt, ou, t, o, totals = intra(
        scalars, pieces, rims, narrow, taps, params, docs, heads
    )
    gate_raw = dot(normed_all, w_gate_out)
    maps = lax.all_gather(totals, "dp", axis=0)
    state_in = chain(mine, maps, None, heads)
    rows_out, v2, s, mixed = outward(state_in, w, u, qt, ou, t, o, gate_raw, gain_heads, heads)

    mixed_own = lax.all_to_all(mixed, "tensor", split_axis=0, concat_axis=1, tiled=True)
    residual = own_rows + dot(mixed_own, w_out_full)
    normed_mid = row_norm(residual, gain_mid).astype(LOW)
    mid_all = lax.all_gather(normed_mid, "tensor", axis=0, tiled=True)
    gate_pre = dot(mid_all, w_gate)
    up_pre = dot(mid_all, w_up)
    sigmoid_gate = jax.nn.sigmoid(gate_pre)
    act = gate_pre * sigmoid_gate
    activated = (act * up_pre).astype(LOW)
    grad_gate = (grad_act * up_pre * sigmoid_gate * (1.0 + gate_pre * (1.0 - sigmoid_gate))).astype(LOW)
    grad_up = (grad_act * act).astype(LOW)
    grad_mid_part = (contract_cols(grad_gate, w_gate) + contract_cols(grad_up, w_up)).astype(LOW)
    grad_mid = lax.psum_scatter(grad_mid_part, "tensor", scatter_dimension=0, tiled=True).astype(F32)

    gate_grad = contract_rows(mid_all, grad_gate).astype(LOW)
    up_grad = contract_rows(mid_all, grad_up).astype(LOW)
    down_grad = contract_rows(out_grad, activated).astype(LOW)
    mlp_part = dot(activated, w_down).astype(LOW)
    ffn_grads = [
        lax.psum_scatter(part, "dp", scatter_dimension=0, tiled=True)
        for part in (gate_grad, up_grad, down_grad)
    ]

    grad_res_norm, gain_mid_grad = norm_back(residual, gain_mid, grad_mid)
    grad_own = lax.dynamic_slice_in_dim(out_grad, tensor_index * rows_own, rows_own, 0)
    grad_residual = grad_own.astype(F32) + grad_res_norm
    grad_mixer = grad_residual.astype(LOW)
    grad_mixed_own = contract_cols(grad_mixer, w_out_full).astype(LOW)
    grad_mixed = lax.all_to_all(
        grad_mixed_own, "tensor", split_axis=1, concat_axis=0, tiled=True
    ).astype(F32)
    mlp_rows = lax.psum_scatter(after(mlp_part, grad_mid), "tensor", scatter_dimension=0, tiled=True)
    output = (residual + mlp_rows.astype(F32)).astype(LOW)
    grad_mixer_all = lax.all_gather(after(grad_mixer, grad_mixed), "tensor", axis=0, tiled=True)

    do, gate_low, head_gain_part, ds_total = inward(
        grad_mixed, rows_out, gate_raw, gain_heads, qt, t, heads
    )
    sums = lax.all_gather(ds_total, "dp", axis=0)
    gate_out_grad = lax.psum_scatter(
        contract_rows(normed_all, gate_low).astype(LOW), "dp", scatter_dimension=0, tiled=True
    )
    grad_end = chain(mine, maps, sums, heads)
    gq, gk, gv, tails, rim_grad, narrow_low, taps_grad, params_grad = back(
        scalars, pieces, rims, narrow, taps, params, grad_end, do, v2, s, x, p, kg, w, u, qt, t,
        docs, heads,
    )
    out_w_grad = lax.psum_scatter(
        contract_rows(grad_mixer_all, mixed).astype(LOW), "dp", scatter_dimension=0, tiled=True
    )
    rim_back = lax.ppermute(rim_grad, "dp", [(i + 1, i) for i in range(dp_parts - 1)])
    tails = tails.at[:, HALO - 8 :].add(rim_back).astype(LOW)
    grads = [
        lax.dynamic_update_slice_in_dim(g, tails[i], group_rows - HALO, 0)
        for i, g in enumerate((gq, gk, gv))
    ]
    summed = contract_cols(gate_low, w_gate_out) + contract_cols(narrow_low, w_narrow)
    for g, weight in zip(grads, (w_query, w_key, w_value)):
        summed = summed + contract_cols(g, weight)
    grad_normed = lax.psum_scatter(
        summed.astype(LOW), "tensor", scatter_dimension=0, tiled=True
    ).astype(F32)
    narrow_grad = contract_rows(normed_all, narrow_low)[:, : 2 * heads].astype(LOW)
    qkv_grads = [
        lax.psum_scatter(
            contract_rows(normed_all, g).astype(LOW), "dp", scatter_dimension=0, tiled=True
        )
        for g in grads
    ]
    narrow_grad = lax.psum_scatter(narrow_grad, "dp", scatter_dimension=0, tiled=True).astype(F32)
    grad_tokens, gain_in_grad = norm_back(own_rows, gain_in, grad_normed)
    input_grad = grad_residual + grad_tokens

    params_grad = params_grad.reshape(2, 8, 128).sum(1)[:, :heads]
    flat = jnp.concatenate(
        [taps_grad.sum(1), head_gain_part.sum(0)[None]], axis=0
    )
    wide = lax.dynamic_update_slice_in_dim(
        jnp.zeros((13, width * tensor_parts), F32), flat, tensor_index * width, 1
    )
    thin = lax.dynamic_update_slice_in_dim(
        jnp.zeros((2, heads * tensor_parts), F32), params_grad, tensor_index * heads, 1
    )
    packed = jnp.concatenate([wide.reshape(-1), thin.reshape(-1), gain_in_grad, gain_mid_grad])
    packed = lax.psum(packed, ("dp", "tensor"))
    channels = width * tensor_parts
    wide = packed[: 13 * channels].reshape(13, channels)
    rest = packed[13 * channels :]
    all_heads = heads * tensor_parts
    return (
        output,
        input_grad,
        rest[2 * all_heads : 2 * all_heads + model],
        qkv_grads[0].astype(F32),
        qkv_grads[1].astype(F32),
        qkv_grads[2].astype(F32),
        narrow_grad[:, :heads],
        narrow_grad[:, heads:],
        gate_out_grad.astype(F32),
        wide[0:4],
        wide[4:8],
        wide[8:12],
        rest[all_heads : 2 * all_heads],
        rest[:all_heads],
        wide[12],
        out_w_grad.T.astype(F32),
        rest[2 * all_heads + model :],
        ffn_grads[0].astype(F32),
        ffn_grads[1].astype(F32),
        ffn_grads[2].T.astype(F32),
    )


def solution(mesh):
    placed = (
        P(("dp", "tensor"), None),
        P(),
        P(None, "tensor"),
        P(None, "tensor"),
        P(None, "tensor"),
        P(None, "tensor"),
        P(None, "tensor"),
        P(None, "tensor"),
        P(None, "tensor"),
        P(None, "tensor"),
        P(None, "tensor"),
        P("tensor"),
        P("tensor"),
        P("tensor"),
        P("tensor", None),
        P(),
        P(None, "tensor"),
        P(None, "tensor"),
        P("tensor", None),
        P("dp", None),
        P(),
    )
    return jax.shard_map(
        local,
        mesh=mesh,
        in_specs=placed,
        out_specs=(
            P(("dp", "tensor"), None),
            P(("dp", "tensor"), None),
            P(),
            P("dp", "tensor"),
            P("dp", "tensor"),
            P("dp", "tensor"),
            P("dp", "tensor"),
            P("dp", "tensor"),
            P("dp", "tensor"),
            P(),
            P(),
            P(),
            P(),
            P(),
            P(),
            P("tensor", "dp"),
            P(),
            P("dp", "tensor"),
            P("dp", "tensor"),
            P("tensor", "dp"),
        ),
        check_vma=False,
    )
```

time: 2960 us -> 1400 us (0.47)
  matrix products: 1020 us -> 204 us
  waiting for transfers between devices: 1440 us -> 942 us
  local copies, waits for them, and re-layouts: 230 us -> 21.1 us
  Pallas kernels: 0 us -> 122 us
  other arithmetic: 166 us -> 50.2 us
    dot_general x1658 -> x27, matrix products: 1010 us -> 204 us  [the longest x9 81.1 us: contract_cols(): return lax.dot_general(left, right, NT, preferred_element_type=F32)]
    reduce_scatter x12, waiting for transfers between devices: 1080 us -> 594 us  [the longest x3 129 us: local(): lax.psum_scatter(contract_rows(normed_all, g).astype(LOW), 'dp', scatter_...]
    pallas_call x0 -> x6, Pallas kernels: none -> 122 us  [the longest x1 47.8 us: back(): pl.pallas_call(functools.partial(back_kernel, docs, heads, chunks), out_s...]
    squeeze x183 -> x1, local copies, waits for them, and re-layouts: 96.8 us -> 0.61 us  [local(): rims = [rims[i] for i in range(3)]]
    all_gather x5 -> x4, waiting for transfers between devices: 143 us -> 57.7 us  [the longest x1 34.1 us: local(): maps = lax.all_gather(totals, 'dp', axis=0)]
    psum x1, waiting for transfers between devices: 66.6 us -> 123 us  [local(): packed = lax.psum(packed, ('dp', 'tensor'))]
    psum x1 -> x0, blocking collectives: 47.2 us -> none  [local(): lax.psum((widen_full(grad_conv, tensor_parts, tensor_index, 2), widen_ful...]
    mul x100 -> x2, other arithmetic: 36 us -> 0.02 us  [norm_back(): inner * inv * inv * inv]
  transfers between devices with their start and end apart: 24 -> 23, of which waited for: 19 -> 18; matrix products, arithmetic and copies ran while one was open for 12% -> 13% of each run, Pallas kernels for 0% -> 8%
where the time goes in v1:
time: 1400 us; the launch traced here: 1390 us
  waiting for transfers between devices  942 us (67%)
  matrix products  204 us (15%)
  Pallas kernels  122 us (9%)
  other arithmetic  50.2 us (4%)
  blocking collectives  28.5 us (2%)
  local copies, waits for them, and re-layouts  21.1 us (2%)
  between operations  14.9 us (1%)
    reduce_scatter x3, waiting for transfers between devices, local(): lax.psum_scatter(contract_rows(normed_all, g).astype(LOW), 'dp', scatter_...  129 us
    psum x1, waiting for transfers between devices, local(): packed = lax.psum(packed, ('dp', 'tensor'))  123 us
    reduce_scatter x3, waiting for transfers between devices, local(): lax.psum_scatter(part, 'dp', scatter_dimension=0, tiled=True)  117 us
    dot_general x9, matrix products, contract_cols(): return lax.dot_general(left, right, NT, preferred_element_type=F32)  81.1 us
    all_gather x1, waiting for transfers between devices, local(): mid_all = lax.all_gather(normed_mid, 'tensor', axis=0, tiled=True)  79.6 us
    reduce_scatter x1, waiting for transfers between devices, local(): lax.psum_scatter(grad_mid_part, 'tensor', scatter_dimension=0, tiled=True)  77.8 us
    reduce_scatter x1, waiting for transfers between devices, local(): lax.psum_scatter(after(mlp_part, grad_mid), 'tensor', scatter_dimension=0...  76.9 us
    all_gather x1, waiting for transfers between devices, local(): normed_all = lax.all_gather(normed_in, 'tensor', axis=0, tiled=True)  75.4 us
  transfers between devices with their start and end apart: 23, of which 18 were waited for; matrix products, arithmetic and copies ran while one was open for 13% of the time, Pallas kernels for 8%

profile of v1, /device:TPU:12, one launch (start us, length us, event | category | flops | bytes accessed | tf_op | source)
XLA Modules:
  0.0 1393.5 jit_solution(2574245500348029565)
XLA Ops:
  16.8 75.4 %all-gather.10.cloned.1.call-done = bf16[1024,2048]{1,0:T(8,128)(2,1)} async-done(((bf16[256,2048]{1,0:T(8,128)(2,1)}), bf16[1024,2048]{1,0:T(8,128)(2,1)}) %all-gather.10.cloned.1.call-update) | async-done | bytes 4194320 | tf_op jit(solution)/shard_map/all_gather | solution.py:647
  109.3 40.8 %intra.1 = (f32[8,4,128,128]{3,2,1,0:T(8,128)}, f32[8,4,128,128]{3,2,1,0:T(8,128)}, f32[8,4,128,128]{3,2,1,0:T(8,128)}, f32[1024,512]{1,0:T(8,128)}, f32[1024,51...) custom-call(s32[5]{0:T(128)} %pad_add_fusion.scalars, ...), custom_call_target="tpu_custom_call" | custom-call | flops 24159191040 | bytes 62914560 | tf_op jit(solution)/shard_map/intra/pallas_call | solution.py:238
  150.1 23.5 %all-gather.18.cloned.1.call-done = bf16[1024,2048]{1,0:T(8,128)(2,1)} async-done(((bf16[256,2048]{1,0:T(8,128)(2,1)}), bf16[1024,2048]{1,0:T(8,128)(2,1)}) %all-gather.18.cloned.1.call-update) | async-done | bytes 4194320 | tf_op jit(solution)/shard_map/all_gather | solution.py:652
  179.6 34.1 %all-gather.16.cloned.1.call-done = f32[32,128,256]{2,1,0:T(8,128)} async-done(((f32[4,128,256]{2,1,0:T(8,128)}), f32[32,128,256]{2,1,0:T(8,128)}) %all-gather.16.cloned.1.call-update) | async-done | bytes 4194320 | tf_op jit(solution)/shard_map/all_gather | solution.py:670
  220.2 11.5 outward.1
  252.4 9.5 all-to-all-done
  271.0 79.6 %all-gather.12.cloned.1.call-done = bf16[1024,2048]{1,0:T(8,128)(2,1)} async-done(((bf16[256,2048]{1,0:T(8,128)(2,1)}), bf16[1024,2048]{1,0:T(8,128)(2,1)}) %all-gather.12.cloned.1.call-update) | async-done | bytes 4194320 | tf_op jit(solution)/shard_map/all_gather | solution.py:677
  350.6 11.9 fusion.35
  362.4 10.6 fusion.34
  373.0 14.6 %multiply_convert_fusion = (bf16[1024,1408]{1,0:T(8,128)(2,1)}, bf16[1024,1408]{1,0:T(8,128)(2,1)S(1)}, bf16[1024,1408]{1,0:T(8,128)(2,1)}) fusion(f32[1024,1408]{1,0:T(8,128)} %fusion.34, f32[1024,1408]{1,0:T(8,128)} %fusion.35, bf16[1024,2048]{1,0:T(8,128)(2,1)S(1)} %copy-done.6, bf16[1408,2048]{1,0:T(8,128)(2,1)} %param.45), kind=kOutput, calls=%fused_computation.7 | convolution fusion | flops 5927206912 | bytes 30146560 | tf_op jit(solution)/shard_map/dot_general | solution.py:579
  387.6 9.8 fusion.36
  397.5 11.4 add_convert_fusion.1
  409.0 77.8 %reduce-scatter.13.cloned.1.call-done = bf16[256,2048]{1,0:T(8,128)(2,1)} async-done(((bf16[1024,2048]{1,0:T(8,128)(2,1)}), bf16[256,2048]{1,0:T(8,128)(2,1)}) %reduce-scatter.13.cloned.1.call-update) | async-done | bytes 1048592 | tf_op jit(solution)/shard_map/reduce_scatter | solution.py:686
  497.9 28.5 %all_to_all.32 = bf16[256,4,512]{2,0,1:T(8,128)(2,1)S(1)} all-to-all(bf16[256,4,512]{2,0,1:T(8,128)(2,1)S(1)} %bitcast.120), channel_id=1, replica_groups=mesh['dp'=8,'tensor'=4] {'tensor'}, dimensions={1} | all-to-all | bytes 2097152 | tf_op jit(solution)/shard_map/all_to_all | solution.py:702
  528.1 10.1 inward.1
  539.1 10.9 convolution_convert_fusion.1
  550.1 11.1 convolution_convert_fusion.2
  561.3 10.6 fusion
  585.5 47.8 %back.1 = (bf16[1024,512]{1,0:T(8,128)(2,1)}, bf16[1024,512]{1,0:T(8,128)(2,1)}, bf16[1024,512]{1,0:T(8,128)(2,1)}, f32[3,16,512]{2,1,0:T(8,128)}, f32[3,8,512]{...) custom-call(s32[5]{0:T(128)} %pad_add_fusion.scalars, ...), custom_call_target="tpu_custom_call" | custom-call | flops 8053063680 | bytes 33554432 | tf_op jit(solution)/shard_map/back/pallas_call | solution.py:499
  688.7 14.5 %add_convert_fusion = bf16[1024,2048]{1,0:T(8,128)(2,1)} fusion(f32[1024,2048]{1,0:T(8,128)} %fusion.40, f32[1024,2048]{1,0:T(8,128)} %fusion.39, f32[1024,2048]{1,0:T(8,128)} %fusion.38, f32[1024,2048]{1,0:T(8,128)} %fusion.37, bf16[1024,128]{1,0:T(8,128)(2,1)S(1)} %copy-done.8, bf16[2048,4]{0,1:T(4,128)(2,1)S(1)} %copy-done.16, ...), kind=kOutput, calls=%fused_computation.1 | convolution fusion | flops 549191680 | bytes 38043648 | tf_op jit(solution)/shard_map/dot_general | solution.py:579
  703.3 11.0 convolution_convert_fusion.3
  716.9 56.1 %reduce-scatter.31.cloned.1.call-done = bf16[256,1408]{1,0:T(8,128)(2,1)} async-done(((bf16[2048,1408]{1,0:T(8,128)(2,1)}), bf16[256,1408]{1,0:T(8,128)(2,1)}) %reduce-scatter.31.cloned.1.call-update) | async-done | bytes 720912 | tf_op jit(solution)/shard_map/reduce_scatter | solution.py:693
  775.3 60.4 %reduce-scatter.35.cloned.1.call-done = bf16[256,1408]{0,1:T(8,128)(2,1)} async-done(((bf16[2048,1408]{0,1:T(8,128)(2,1)}), bf16[256,1408]{0,1:T(8,128)(2,1)}) %reduce-scatter.35.cloned.1.call-update) | async-done | bytes 720912 | tf_op jit(solution)/shard_map/reduce_scatter | solution.py:693
  838.0 42.2 %reduce-scatter.27.cloned.1.call-done = bf16[256,512]{1,0:T(8,128)(2,1)} async-done(((bf16[2048,512]{1,0:T(8,128)(2,1)}), bf16[256,512]{1,0:T(8,128)(2,1)}) %reduce-scatter.27.cloned.1.call-update) | async-done | bytes 262160 | tf_op jit(solution)/shard_map/reduce_scatter | solution.py:713
  882.5 32.7 %reduce-scatter.25.cloned.1.call-done = bf16[256,8]{0,1:T(8,128)(2,1)} async-done(((bf16[2048,8]{0,1:T(8,128)(2,1)}), bf16[256,8]{0,1:T(8,128)(2,1)}) %reduce-scatter.25.cloned.1.call-update) | async-done | bytes 4112 | tf_op jit(solution)/shard_map/reduce_scatter | solution.py:743
  916.6 43.7 %reduce-scatter.19.cloned.1.call-done = bf16[256,512]{1,0:T(8,128)(2,1)} async-done(((bf16[2048,512]{1,0:T(8,128)(2,1)}), bf16[256,512]{1,0:T(8,128)(2,1)}) %reduce-scatter.19.cloned.1.call-update) | async-done | bytes 262160 | tf_op jit(solution)/shard_map/reduce_scatter | solution.py:738
  962.2 42.9 %reduce-scatter.23.cloned.1.call-done = bf16[256,512]{1,0:T(8,128)(2,1)} async-done(((bf16[2048,512]{1,0:T(8,128)(2,1)}), bf16[256,512]{1,0:T(8,128)(2,1)}) %reduce-scatter.23.cloned.1.call-update) | async-done | bytes 262160 | tf_op jit(solution)/shard_map/reduce_scatter | solution.py:738
  1006.9 42.6 %reduce-scatter.21.cloned.1.call-done = bf16[256,512]{1,0:T(8,128)(2,1)} async-done(((bf16[2048,512]{1,0:T(8,128)(2,1)}), bf16[256,512]{1,0:T(8,128)(2,1)}) %reduce-scatter.21.cloned.1.call-update) | async-done | bytes 262160 | tf_op jit(solution)/shard_map/reduce_scatter | solution.py:738
  1051.3 42.9 %reduce-scatter.29.cloned.1.call-done = bf16[256,512]{1,0:T(8,128)(2,1)} async-done(((bf16[2048,512]{1,0:T(8,128)(2,1)}), bf16[256,512]{1,0:T(8,128)(2,1)}) %reduce-scatter.29.cloned.1.call-update) | async-done | bytes 262160 | tf_op jit(solution)/shard_map/reduce_scatter | solution.py:721
  1098.1 75.1 %reduce-scatter.17.cloned.1.call-done = bf16[256,2048]{1,0:T(8,128)(2,1)} async-done(((bf16[1024,2048]{1,0:T(8,128)(2,1)}), bf16[256,2048]{1,0:T(8,128)(2,1)}) %reduce-scatter.17.cloned.1.call-update) | async-done | bytes 1048592 | tf_op jit(solution)/shard_map/reduce_scatter | solution.py:733
  1175.8 76.9 %reduce-scatter.15.cloned.1.call-done = bf16[256,2048]{1,0:T(8,128)(2,1)} async-done(((bf16[1024,2048]{1,0:T(8,128)(2,1)}), bf16[256,2048]{1,0:T(8,128)(2,1)}) %reduce-scatter.15.cloned.1.call-update) | async-done | bytes 1048592 | tf_op jit(solution)/shard_map/reduce_scatter | solution.py:705
  1258.3 123.0 %all-reduce.4.cloned.1.call-done = f32[30752]{0:T(1024)} async-done(((f32[30752]{0:T(1024)}), f32[30752]{0:T(1024)}) %all-reduce.4.cloned.1.call-update) | async-done | bytes 123024 | tf_op jit(solution)/shard_map/psum | solution.py:758
  (225 shorter events, 184.8 us)
Async XLA Ops:
  7.2 166.5 %copy-start = (bf16[2048,512]{1,0:T(8,128)(2,1)S(1)}, bf16[2048,512]{1,0:T(8,128)(2,1)}, u32[]{:S(2)}) copy-start(bf16[2048,512]{1,0:T(8,128)(2,1)} %param.34) | copy-start | bytes 6291460
  7.3 84.9 %all-gather.10.cloned.1.call-start = ((), (), s32[]{:S(2)}) async-start(), calls=%async_computation.14 | async-start | bytes 5242880 | tf_op jit(solution)/shard_map/all_gather | solution.py:647
  12.6 161.1 %all-gather.18.cloned.1.call-start = ((), (), s32[]{:S(2)}) async-start(), calls=%async_computation.31 | async-start | bytes 5242880 | tf_op jit(solution)/shard_map/all_gather | solution.py:652
  15.0 198.7 %all-gather.16.cloned.1.call-start = ((), (), s32[]{:S(2)}) async-start(), calls=%async_computation.30 | async-start | bytes 4718592 | tf_op jit(solution)/shard_map/all_gather | solution.py:670
  15.5 82.0 %copy-start.26 = (f32[8,128]{1,0:T(8,128)}, f32[8,128]{1,0:T(8,128)S(1)}, u32[]{:S(2)}) copy-start(f32[8,128]{1,0:T(8,128)S(1)} %scatter.9.refs_11_) | copy-start | bytes 12292
  102.4 6.3 collective-permute-start
  173.7 65.4 %collective-permute-start.1 = (bf16[4,256,2048]{2,1,0:T(8,128)(2,1)}, bf16[4,256,2048]{2,1,0:T(8,128)(2,1)}, u32[]{:S(2)}, u32[]{:S(2)}) collective-permute-start(bf16[4,256,2048]{2,1,0:T(8,128)(2,1)} %bitcast.118), channel_id=1, source_target_pairs={{0,4},{4,0},{8,12},{12,8},{16,20},{20,16},{24,28},{28,24},{1,5},{5... | collective-permute-start | bytes 12582920 | tf_op jit(solution)/shard_map/ppermute | solution.py:653
  233.9 28.0 %all-to-all-start = ((bf16[4,256,512]{1,2,0:T(8,128)(2,1)}), bf16[4,256,512]{1,2,0:T(8,128)(2,1)}, u32[]{:S(2)}, u32[]{:S(2)}) async-start(bf16[4,256,512]{1,2,0:T(8,128)(2,1)} %copy.47), calls=%async_computation | async-start | bytes 2097152 | tf_op jit(solution)/shard_map/all_to_all | solution.py:674
  239.0 111.5 %all-gather.12.cloned.1.call-start = ((), (), s32[]{:S(2)}) async-start(), calls=%async_computation.15 | async-start | bytes 5242880 | tf_op jit(solution)/shard_map/all_gather | solution.py:677
  270.7 216.1 %reduce-scatter.13.cloned.1.call-start = ((), (), s32[]{:S(2)}) async-start(), calls=%async_computation.16 | async-start | bytes 5242880 | tf_op jit(solution)/shard_map/reduce_scatter | solution.py:686
  408.9 170.3 %all-gather.20.cloned.1.call-start = ((), (), s32[]{:S(2)}) async-start(), calls=%async_computation.32 | async-start | bytes 2359296 | tf_op jit(solution)/shard_map/all_gather | solution.py:712
  538.3 119.3 %all-gather.14.cloned.1.call-start = ((), (), s32[]{:S(2)}) async-start(), calls=%async_computation.25 | async-start | bytes 5242880 | tf_op jit(solution)/shard_map/all_gather | solution.py:707
  539.0 175.5 %reduce-scatter.33.cloned.1.call-start = ((), (), s32[]{:S(2)}) async-start(), calls=%async_computation.28 | async-start | bytes 6488064 | tf_op jit(solution)/shard_map/reduce_scatter | solution.py:693
  550.0 222.9 %reduce-scatter.31.cloned.1.call-start = ((), (), s32[]{:S(2)}) async-start(), calls=%async_computation.27 | async-start | bytes 6488064 | tf_op jit(solution)/shard_map/reduce_scatter | solution.py:693
  561.2 274.5 %reduce-scatter.35.cloned.1.call-start = ((), (), s32[]{:S(2)}) async-start(), calls=%async_computation.29 | async-start | bytes 6488064 | tf_op jit(solution)/shard_map/reduce_scatter | solution.py:693
  571.9 308.4 %reduce-scatter.27.cloned.1.call-start = ((), (), s32[]{:S(2)}) async-start(), calls=%async_computation.24 | async-start | bytes 2359296 | tf_op jit(solution)/shard_map/reduce_scatter | solution.py:713
  579.1 336.2 %reduce-scatter.25.cloned.1.call-start = ((), (), s32[]{:S(2)}) async-start(), calls=%async_computation.23 | async-start | bytes 36864 | tf_op jit(solution)/shard_map/reduce_scatter | solution.py:743
  633.3 4.5 collective-permute-start.2
  637.7 322.6 %reduce-scatter.19.cloned.1.call-start = ((), (), s32[]{:S(2)}) async-start(), calls=%async_computation.20 | async-start | bytes 2359296 | tf_op jit(solution)/shard_map/reduce_scatter | solution.py:738
  644.8 360.3 %reduce-scatter.23.cloned.1.call-start = ((), (), s32[]{:S(2)}) async-start(), calls=%async_computation.22 | async-start | bytes 2359296 | tf_op jit(solution)/shard_map/reduce_scatter | solution.py:738
  650.8 398.7 %reduce-scatter.21.cloned.1.call-start = ((), (), s32[]{:S(2)}) async-start(), calls=%async_computation.21 | async-start | bytes 2359296 | tf_op jit(solution)/shard_map/reduce_scatter | solution.py:738
  657.5 436.7 %reduce-scatter.29.cloned.1.call-start = ((), (), s32[]{:S(2)}) async-start(), calls=%async_computation.26 | async-start | bytes 2359296 | tf_op jit(solution)/shard_map/reduce_scatter | solution.py:721
  663.9 509.3 %reduce-scatter.17.cloned.1.call-start = ((), (), s32[]{:S(2)}) async-start(), calls=%async_computation.18 | async-start | bytes 5242880 | tf_op jit(solution)/shard_map/reduce_scatter | solution.py:733
  703.2 549.6 %reduce-scatter.15.cloned.1.call-start = ((), (), s32[]{:S(2)}) async-start(), calls=%async_computation.17 | async-start | bytes 5242880 | tf_op jit(solution)/shard_map/reduce_scatter | solution.py:705
  714.3 123.7 %copy-start.19 = (f32[8,512]{1,0:T(8,128)S(1)}, f32[8,512]{1,0:T(8,128)}, u32[]{:S(2)}) copy-start(f32[8,512]{1,0:T(8,128)} %get-tuple-element.109) | copy-start | bytes 49156
  714.3 167.8 %copy-start.25 = (f32[16,128]{1,0:T(8,128)S(1)}, f32[16,128]{1,0:T(8,128)}, u32[]{:S(2)}) copy-start(f32[16,128]{1,0:T(8,128)} %get-tuple-element.110) | copy-start | bytes 24580
  714.3 168.1 %copy-start.10 = (f32[12,8,512]{2,1,0:T(8,128)S(1)}, f32[12,8,512]{2,1,0:T(8,128)}, u32[]{:S(2)}) copy-start(f32[12,8,512]{2,1,0:T(8,128)} %get-tuple-element.108) | copy-start | bytes 589828
  714.3 667.0 %all-reduce.4.cloned.1.call-start = ((), (), s32[]{:S(2)}) async-start(), calls=%async_computation.19 | async-start | bytes 253952 | tf_op jit(solution)/shard_map/psum | solution.py:758
  775.3 397.9 %copy-start.4 = (bf16[256,2048]{1,0:T(8,128)(2,1)S(1)}, bf16[256,2048]{1,0:T(8,128)(2,1)}, u32[]{:S(2)}) copy-start(bf16[256,2048]{1,0:T(8,128)(2,1)} %param.27) | copy-start | bytes 3145732
  775.3 397.9 %copy-start.12 = (f32[2048]{0:T(1024)S(1)}, f32[2048]{0:T(1024)}, u32[]{:S(2)}) copy-start(f32[2048]{0:T(1024)} %param.28) | copy-start | bytes 24580
  775.3 397.9 %copy-start.14 = (f32[256]{0:T(256)S(1)}, f32[256]{0:T(256)}, u32[]{:S(2)}) copy-start(f32[256]{0:T(256)} %copy-done.13) | copy-start | bytes 3076
  838.0 337.8 %copy-start.21 = (f32[256]{0:T(256)S(1)}, f32[256]{0:T(256)}, u32[]{:S(2)}) copy-start(f32[256]{0:T(256)} %copy-done.20) | copy-start | bytes 3076
  (40 other events, 326.0 us)
Sparse Core Ops, SparseCore 0:
  12.7 79.4 all-gather.9
  94.3 79.2 all-gather.17
  176.1 37.5 all-gather.15
  270.8 79.6 all-gather.11
  409.0 77.7 reduce-scatter.12
  538.4 28.1 all-gather.19
  568.2 78.3 all-gather.13
  650.5 59.9 reduce-scatter.32
  713.9 58.9 reduce-scatter.30
  776.6 59.0 reduce-scatter.34
  839.0 41.1 reduce-scatter.26
  883.9 31.2 reduce-scatter.24
  919.1 41.1 reduce-scatter.18
  963.8 41.2 reduce-scatter.22
  1008.2 41.2 reduce-scatter.20
  1053.0 41.2 reduce-scatter.28
  1096.4 76.7 reduce-scatter.16
  1175.5 77.2 reduce-scatter.14
  1258.3 122.8 all-reduce.3

commit v2 on v1

--- a/solution.py
+++ b/solution.py
@@ -304,7 +304,7 @@
     )(s_in, w, u, qt, ou, t, o, gate, gain)
 
 
-def inward_kernel(heads, gm_ref, out_ref, gate_ref, gain_ref, qt_ref, t_ref,
+def inward_kernel(heads, gm_ref, out_ref, gate_ref, gain_ref, qt_ref, t_ref, maps_ref,
                   do_ref, dgate_ref, dgain_ref, tot_ref, run):
     step = pl.program_id(0)
 
@@ -316,7 +316,8 @@
     hs = range(heads)
     grads = []
     for h in hs:
-        out, gate, gm = out_ref[:, lanes(h)], gate_ref[:, lanes(h)], gm_ref[:, lanes(h)]
+        out, gate = out_ref[:, lanes(h)], gate_ref[:, lanes(h)]
+        gm = gm_ref[:, lanes(h)].astype(F32)
         gain = gain_ref[0:1, lanes(h)]
         scale = lax.rsqrt(jnp.mean(out * out, axis=-1, keepdims=True) + epsilon)
         normed = out * scale
@@ -333,32 +334,32 @@
         left = jnp.concatenate([qt_ref[:, lanes(h)], t_ref[0, h]], axis=0)
         new = mm(left, jnp.concatenate([grads[h], run[h]], axis=0), TN)
         run[h] = new
-        tot_ref[h] = new
-
-
-def inward(gm, out, gate, gain, qt, t, heads):
+        tot_ref[h] = jnp.concatenate([new, maps_ref[h, :, 128:]], axis=1)
+
+
+def inward(gm, out, gate, gain, qt, t, maps, heads):
     rows, width = gm.shape
     chunks = rows // CHUNK
     flat, tiles = rows_spec(width, chunks, True), tile_spec(heads, chunks, True)
     return pl.pallas_call(
         functools.partial(inward_kernel, heads),
-        out_shape=(sds(rows, width), sds(rows, width, dtype=LOW), sds(8, width), sds(heads, 128, 128)),
+        out_shape=(sds(rows, width), sds(rows, width, dtype=LOW), sds(8, width), sds(heads, 128, 256)),
         grid=(chunks,),
-        in_specs=[flat, flat, flat, whole_spec(8, width), flat, tiles],
-        out_specs=[flat, flat, whole_spec(8, width), whole_spec(heads, 128, 128)],
+        in_specs=[flat, flat, flat, whole_spec(8, width), flat, tiles, whole_spec(heads, 128, 256)],
+        out_specs=[flat, flat, whole_spec(8, width), whole_spec(heads, 128, 256)],
         scratch_shapes=[pltpu.VMEM((heads, 128, 128), F32)],
         compiler_params=pltpu.CompilerParams(**PARAMS),
         cost_estimate=cost(chunks * heads * 6 * 2 * 128**3, 7 * rows * width * 4),
         name="inward",
-    )(gm, out, gate, gain, qt, t)
+    )(gm, out, gate, gain, qt, t, maps)
 
 
 def back_kernel(docs, heads, chunks, scalars, *refs):
     mains, priors, rims = refs[0:3], refs[3:6], refs[6:9]
     narrow_ref, taps_ref, params_ref, ds_in = refs[9:13]
     (do_ref, v2_ref, s_ref, x_ref, p_ref, kg_ref, w_ref, u_ref, qt_ref, t_ref) = refs[13:23]
-    gq_ref, gk_ref, gv_ref, tail_ref, rim_ref, gnarrow_ref, gtaps_ref, gparams_ref = refs[23:31]
-    run, after = refs[31:33]
+    grads_ref, tail_ref, rim_ref, gtaps_ref, gparams_ref = refs[23:28]
+    run, after = refs[28:30]
     rev = pl.program_id(0)
     step = chunks - 1 - rev
     position = scalars[0] + step * CHUNK
@@ -451,11 +452,13 @@
     upper = jnp.where(masks["row"] <= masks["col"], 1.0, 0.0)
     dg = mm_full(upper, gdecay)
     galpha = dg * rate * jax.nn.sigmoid(shifted)
-    gnarrow_ref[...] = jnp.where(lane < heads, galpha, gbeta * beta * (1.0 - beta)).astype(LOW)
+    width = pieces[0].shape[1]
+    grads_ref[:, 3 * width :] = jnp.where(
+        lane < heads, galpha, gbeta * beta * (1.0 - beta)
+    ).astype(LOW)
     gparams_ref[0:8, :] += jnp.sum((galpha).reshape(CHUNK // 8, 8, 128), axis=0)
     gparams_ref[8:16, :] += jnp.sum((dg * decays).reshape(CHUNK // 8, 8, 128), axis=0)
 
-    outs = (gq_ref, gk_ref, gv_ref)
     for i in range(3):
         rows, pre, sg = feats[i]
         pieces_d = []
@@ -483,23 +486,22 @@
             after[3 * i + s - 1] = masked[:8]
             front = jnp.concatenate([jnp.zeros_like(masked[:8]), masked[:8]], axis=0)
             rim = rim + pltpu.roll(front, 16 - s, 0)[:8] * tap
-        outs[i][...] = grad.astype(LOW)
-        rim_ref[i] = rim
+        grads_ref[:, i * width : (i + 1) * width] = grad.astype(LOW)
+        rim_ref[:, i * width : (i + 1) * width] = rim
 
         @pl.when(rev == 0)
         def _():
-            tail_ref[i] = grad[CHUNK - HALO :]
+            tail_ref[:, i * width : (i + 1) * width] = grad[CHUNK - HALO :]
 
 
 def back(scalars, pieces, rims, narrow, taps, params, ds_in, do, v2, s, x, p, kg, w, u, qt, t, docs, heads):
     rows, width = pieces[0].shape
     chunks = rows // CHUNK
     flat, tiles = rows_spec(width, chunks, True), tile_spec(heads, chunks, True)
-    low = sds(rows, width, dtype=LOW)
     return pl.pallas_call(
         functools.partial(back_kernel, docs, heads, chunks),
         out_shape=(
-            low, low, low, sds(3, HALO, width), sds(3, 8, width), sds(rows, 128, dtype=LOW),
+            sds(rows, 3 * width + 128, dtype=LOW), sds(HALO, 3 * width), sds(8, 3 * width),
             sds(12, 8, width), sds(16, 128),
         ),
         grid_spec=pltpu.PrefetchScalarGridSpec(
@@ -510,8 +512,8 @@
             + [whole_spec(HALO, width)] * 3
             + [rows_spec(128, chunks, True), whole_spec(16, width), whole_spec(8, 128)]
             + [whole_spec(heads, 128, 128), flat, flat, tiles, tiles, tiles, tiles, flat, flat, flat, tiles],
-            out_specs=[flat] * 3
-            + [whole_spec(3, HALO, width), whole_spec(3, 8, width), rows_spec(128, chunks, True)]
+            out_specs=[rows_spec(3 * width + 128, chunks, True)]
+            + [whole_spec(HALO, 3 * width), whole_spec(8, 3 * width)]
             + [whole_spec(12, 8, width), whole_spec(16, 128)],
             scratch_shapes=[pltpu.VMEM((heads, 128, 128), F32), pltpu.VMEM((9, 8, width), F32)],
         ),
@@ -521,56 +523,6 @@
     )(scalars, *pieces, *pieces, *rims, narrow, taps, params, ds_in, do, v2, s, x, p, kg, w, u, qt, t)
 
 
-def chain_kernel(heads, backward, scalars, *refs):
-    mine, count = scalars[0], pl.num_programs(0)
-    step = pl.program_id(0)
-    out_ref = refs[-1]
-
-    @pl.when(step == 0)
-    def _():
-        out_ref[...] = jnp.zeros_like(out_ref)
-
-    if backward:
-        maps_ref, sums_ref = refs[0], refs[1]
-
-        @pl.when(count - 1 - step > mine)
-        def _():
-            for h in range(heads):
-                out_ref[h] = mm(maps_ref[0, h][:, 128:], out_ref[h], TN) + sums_ref[0, h]
-    else:
-        maps_ref = refs[0]
-
-        @pl.when(step < mine)
-        def _():
-            for h in range(heads):
-                piece = maps_ref[0, h]
-                out_ref[h] = mm(piece[:, 128:], out_ref[h]) + piece[:, :128]
-
-
-def chain(mine, maps, sums, heads):
-    count = maps.shape[0]
-    backward = sums is not None
-    at = (lambda c, *_: (count - 1 - c, 0, 0, 0)) if backward else (lambda c, *_: (c, 0, 0, 0))
-    specs = [pl.BlockSpec((1, heads, 128, 256), at)]
-    args = [maps]
-    if backward:
-        specs.append(pl.BlockSpec((1, heads, 128, 128), at))
-        args.append(sums)
-    return pl.pallas_call(
-        functools.partial(chain_kernel, heads, backward),
-        out_shape=sds(heads, 128, 128),
-        grid_spec=pltpu.PrefetchScalarGridSpec(
-            num_scalar_prefetch=1,
-            grid=(count,),
-            in_specs=specs,
-            out_specs=whole_spec(heads, 128, 128),
-        ),
-        compiler_params=pltpu.CompilerParams(**PARAMS),
-        cost_estimate=cost(count * heads * 3 * 2 * 128**3, count * heads * 3 * 128 * 128 * 4),
-        name="chain",
-    )(mine, *args)
-
-
 def contract_rows(left, right):
     return lax.dot_general(left, right, TN, preferred_element_type=F32)
 
@@ -592,6 +544,642 @@
     scaled = grad * gain
     inner = jnp.mean(scaled * values, axis=-1, keepdims=True)
     return inv * scaled - values * (inner * inv * inv * inv), jnp.sum(grad * values * inv, axis=0)
+
+
+MESH = pl.DeviceIdType.MESH
+
+
+def greet(axis, parts):
+    me = lax.axis_index(axis)
+    barrier = pltpu.get_barrier_semaphore()
+
+    @pl.when(me > 0)
+    def _():
+        pl.semaphore_signal(barrier, inc=1, device_id={axis: me - 1}, device_id_type=MESH)
+
+    @pl.when(me < parts - 1)
+    def _():
+        pl.semaphore_signal(barrier, inc=1, device_id={axis: me + 1}, device_id_type=MESH)
+
+    inner = (me > 0) & (me < parts - 1)
+
+    @pl.when(inner)
+    def _():
+        pl.semaphore_wait(barrier, 2)
+
+    @pl.when(jnp.logical_not(inner))
+    def _():
+        pl.semaphore_wait(barrier, 1)
+
+
+def line_gather(parts, buf, sems, first, use):
+    me = lax.axis_index("tensor")
+    send_right, send_left, from_left, from_right = sems
+
+    def rightward(piece, step):
+        return pltpu.make_async_remote_copy(
+            src_ref=buf.at[piece],
+            dst_ref=buf.at[piece],
+            send_sem=send_right.at[step],
+            recv_sem=from_left.at[step],
+            device_id={"tensor": me + 1},
+            device_id_type=MESH,
+        )
+
+    def leftward(piece, step):
+        return pltpu.make_async_remote_copy(
+            src_ref=buf.at[piece],
+            dst_ref=buf.at[piece],
+            send_sem=send_left.at[step],
+            recv_sem=from_right.at[step],
+            device_id={"tensor": me - 1},
+            device_id_type=MESH,
+        )
+
+    def body(step, _):
+        low, high = me - step, me + step
+
+        @pl.when((step > 0) & (low >= 0))
+        def _():
+            rightward(low, step - 1).wait_recv()
+
+        @pl.when((low >= 0) & (me < parts - 1))
+        def _():
+            rightward(low, step).start()
+
+        @pl.when((step > 0) & (high < parts))
+        def _():
+            leftward(high, step - 1).wait_recv()
+
+        @pl.when((high < parts) & (me > 0))
+        def _():
+            leftward(high, step).start()
+
+        @pl.when(step == 0)
+        def _():
+            first()
+
+        @pl.when(low >= 0)
+        def _():
+            use(low)
+
+        @pl.when((step > 0) & (high < parts))
+        def _():
+            use(high)
+
+        return 0
+
+    lax.fori_loop(0, parts, body, 0)
+
+    def finish(step, _):
+        low, high = me - step, me + step
+
+        @pl.when((low >= 0) & (me < parts - 1))
+        def _():
+            rightward(low, step).wait_send()
+
+        @pl.when((high < parts) & (me > 0))
+        def _():
+            leftward(high, step).wait_send()
+
+        return 0
+
+    lax.fori_loop(0, parts, finish, 0)
+
+
+def norm_into(buf, me, source, gain):
+    rows = source.shape[0]
+
+    def body(i, _):
+        at = pl.ds(pl.multiple_of(i * 64, 64), 64)
+        values = source[at, :].astype(F32)
+        scale = lax.rsqrt(jnp.mean(values * values, axis=-1, keepdims=True) + epsilon)
+        buf[me, at, :] = (values * scale * gain[0:1, :]).astype(LOW)
+        return 0
+
+    lax.fori_loop(0, rows // 64, body, 0)
+
+
+def project_kernel(parts, tok_ref, gain_ref, narrow_w, *refs):
+    weights_in, all_ref = refs[0:4], refs[4]
+    q_ref, k_ref, v_ref, gate_ref, narrow_ref = refs[5:10]
+    buf, weights = refs[10], refs[11:15]
+    sems, load_sem, store_sem = refs[15:19], refs[19], refs[20]
+    me = lax.axis_index("tensor")
+    rows = tok_ref.shape[0]
+    loads = [
+        pltpu.make_async_copy(weights_in[i], weights[i], load_sem.at[i]) for i in range(4)
+    ]
+    for load in loads:
+        load.start()
+    norm_into(buf, me, tok_ref, gain_ref)
+    greet("tensor", parts)
+
+    def first():
+        for load in loads:
+            load.wait()
+
+    def stored(piece):
+        at = pl.ds(pl.multiple_of(piece * rows, rows), rows)
+        return pltpu.make_async_copy(buf.at[piece], all_ref.at[at, :], store_sem.at[piece])
+
+    def use(piece):
+        at = pl.ds(pl.multiple_of(piece * rows, rows), rows)
+        stored(piece).start()
+        values = buf[piece]
+        for w, out in zip(weights, (q_ref, k_ref, v_ref, gate_ref)):
+            out[at, :] = dot(values, w[...]).astype(out.dtype)
+        narrow_ref[at, :] = dot(values, narrow_w[...])
+
+    line_gather(parts, buf, sems, first, use)
+    for piece in range(parts):
+        stored(piece).wait()
+
+
+def vmem():
+    return pl.BlockSpec(memory_space=pltpu.VMEM)
+
+
+def hbm():
+    return pl.BlockSpec(memory_space=pl.ANY)
+
+
+def line_sems(parts):
+    return [pltpu.SemaphoreType.DMA((parts,))] * 4
+
+
+def comm_params(number):
+    return pltpu.CompilerParams(
+        collective_id=number, has_side_effects=True, vmem_limit_bytes=60 * 1024 * 1024
+    )
+
+
+def project(parts, tokens, gain, narrow_w, weights):
+    rows, model = tokens.shape
+    width = weights[0].shape[1]
+    total = rows * parts
+    low = sds(total, width, dtype=LOW)
+    return pl.pallas_call(
+        functools.partial(project_kernel, parts),
+        out_shape=(sds(total, model, dtype=LOW), low, low, low, sds(total, width), sds(total, 128)),
+        in_specs=[vmem()] * 3 + [hbm()] * 4,
+        out_specs=[hbm()] + [vmem()] * 5,
+        scratch_shapes=[pltpu.VMEM((parts, rows, model), LOW)]
+        + [pltpu.VMEM((model, width), LOW)] * 4
+        + line_sems(parts)
+        + [pltpu.SemaphoreType.DMA((4,)), pltpu.SemaphoreType.DMA((parts,))],
+        compiler_params=comm_params(1),
+        cost_estimate=cost(2 * total * model * (4 * width + 128), 60 * 2**20),
+        name="project",
+    )(tokens, gain, narrow_w, *weights)
+
+
+def feed_kernel(parts, res_ref, gain_ref, *refs):
+    weights_in, og_in = refs[0:3], refs[3]
+    all_ref, act_ref, gu_ref = refs[4:7]
+    buf, weights, og = refs[7], refs[8:11], refs[11]
+    sems, load_sem, store_sem = refs[12:16], refs[16], refs[17]
+    me = lax.axis_index("tensor")
+    rows = res_ref.shape[0]
+    units = weights_in[0].shape[1]
+    loads = [
+        pltpu.make_async_copy(src, dst, load_sem.at[i])
+        for i, (src, dst) in enumerate(zip(weights_in + (og_in,), weights + (og,)))
+    ]
+    for load in loads:
+        load.start()
+    norm_into(buf, me, res_ref, gain_ref)
+    greet("tensor", parts)
+    wg, wu, wd = weights
+
+    def first():
+        for load in loads:
+            load.wait()
+
+    def stored(piece):
+        at = pl.ds(pl.multiple_of(piece * rows, rows), rows)
+        return pltpu.make_async_copy(buf.at[piece], all_ref.at[at, :], store_sem.at[piece])
+
+    def tile(at, piece, column, size):
+        cols = pl.ds(pl.multiple_of(column, 128), size)
+        values = buf[piece]
+        gate = dot(values, wg[:, cols])
+        up = dot(values, wu[:, cols])
+        grad = contract_cols(og[at, :], wd[cols, :])
+        sg = jax.nn.sigmoid(gate)
+        act = gate * sg
+        act_ref[at, cols] = (act * up).astype(LOW)
+        gu_ref[at, cols] = (grad * up * sg * (1.0 + gate * (1.0 - sg))).astype(LOW)
+        gu_ref[at, pl.ds(pl.multiple_of(units + column, 128), size)] = (grad * act).astype(LOW)
+
+    def use(piece):
+        at = pl.ds(pl.multiple_of(piece * rows, rows), rows)
+        stored(piece).start()
+
+        def body(i, _):
+            tile(at, piece, i * 256, 256)
+            return 0
+
+        lax.fori_loop(0, units // 256, body, 0)
+        if units % 256:
+            tile(at, piece, units - units % 256, units % 256)
+
+    line_gather(parts, buf, sems, first, use)
+    for piece in range(parts):
+        stored(piece).wait()
+
+
+def feed(parts, residual, gain, weights, out_grad):
+    rows, model = residual.shape
+    units = weights[0].shape[1]
+    total = rows * parts
+    return pl.pallas_call(
+        functools.partial(feed_kernel, parts),
+        out_shape=(
+            sds(total, model, dtype=LOW), sds(total, units, dtype=LOW), sds(total, 2 * units, dtype=LOW),
+        ),
+        in_specs=[vmem()] * 2 + [hbm()] * 4,
+        out_specs=[hbm()] + [vmem()] * 2,
+        scratch_shapes=[pltpu.VMEM((parts, rows, model), LOW)]
+        + [pltpu.VMEM(w.shape, LOW) for w in weights]
+        + [pltpu.VMEM((total, model), LOW)]
+        + line_sems(parts)
+        + [pltpu.SemaphoreType.DMA((4,)), pltpu.SemaphoreType.DMA((parts,))],
+        compiler_params=comm_params(2),
+        cost_estimate=cost(6 * total * model * units, 120 * 2**20),
+        name="feed",
+    )(residual, gain, *weights, out_grad)
+
+
+SUBS = 2
+
+
+def scatter_kernel(parts, given, count, splits, *refs):
+    lefts, rights_in, out_ref = refs[0:given], refs[given : given + count], refs[given + count]
+    refs = refs[given + count + 1 :]
+    rights, (part, send_r, send_l, got_l, got_r) = refs[0:count], refs[count : count + 5]
+    sem_sr, sem_sl, sem_gl, sem_gr, load_sem = refs[count + 5 : count + 10]
+    me = lax.axis_index("tensor")
+    rows, model = out_ref.shape
+    size = rows // SUBS
+    loads = [
+        pltpu.make_async_copy(rights_in[i], rights[i], load_sem.at[i]) for i in range(count)
+    ]
+    for load in loads:
+        load.start()
+    greet("tensor", parts)
+    for load in loads:
+        load.wait()
+
+    def rightward(slot):
+        return pltpu.make_async_remote_copy(
+            src_ref=send_r.at[slot],
+            dst_ref=got_l.at[slot],
+            send_sem=sem_sr.at[slot],
+            recv_sem=sem_gl.at[slot],
+            device_id={"tensor": me + 1},
+            device_id_type=MESH,
+        )
+
+    def leftward(slot):
+        return pltpu.make_async_remote_copy(
+            src_ref=send_l.at[slot],
+            dst_ref=got_r.at[slot],
+            send_sem=sem_sl.at[slot],
+            recv_sem=sem_gr.at[slot],
+            device_id={"tensor": me - 1},
+            device_id_type=MESH,
+        )
+
+    def product(start, many, target):
+        at = pl.ds(pl.multiple_of(start, 128), many)
+
+        def body(j, _):
+            cols = pl.ds(pl.multiple_of(j * 256, 256), 256)
+            total = None
+            for i, (index, first, wide) in enumerate(splits):
+                term = contract_cols(lefts[index][at, first : first + wide], rights[i][cols, :])
+                total = term if total is None else total + term
+            target[:, cols] = total
+            return 0
+
+        lax.fori_loop(0, model // 256, body, 0)
+
+    half = part.at[pl.ds(0, size), :]
+
+    def go_right(piece, sub):
+        slot = piece * SUBS + sub
+
+        @pl.when(piece > me)
+        def _():
+            product(piece * rows + sub * size, size, half)
+
+            @pl.when(me > 0)
+            def _():
+                rightward(slot).wait_recv()
+                send_r[slot] = (half[...] + got_l[slot].astype(F32)).astype(LOW)
+
+            @pl.when(me == 0)
+            def _():
+                send_r[slot] = half[...].astype(LOW)
+
+            rightward(slot).start()
+
+    def go_left(piece, sub):
+        slot = piece * SUBS + sub
+
+        @pl.when(piece < me)
+        def _():
+            product(piece * rows + sub * size, size, half)
+
+            @pl.when(me < parts - 1)
+            def _():
+                leftward(slot).wait_recv()
+                send_l[slot] = (half[...] + got_r[slot].astype(F32)).astype(LOW)
+
+            @pl.when(me == parts - 1)
+            def _():
+                send_l[slot] = half[...].astype(LOW)
+
+            leftward(slot).start()
+
+    right_first = 2 * me < parts
+
+    def body(item, _):
+        step, sub = item // SUBS, item % SUBS
+        right, left = parts - 1 - step, step
+
+        @pl.when(right_first)
+        def _():
+            go_right(right, sub)
+
+        go_left(left, sub)
+
+        @pl.when(jnp.logical_not(right_first))
+        def _():
+            go_right(right, sub)
+
+        return 0
+
+    lax.fori_loop(0, (parts - 1) * SUBS, body, 0)
+    product(me * rows, rows, part)
+    for sub in range(SUBS):
+        at = slice(sub * size, sub * size + size)
+        slot = me * SUBS + sub
+        out_ref[at, :] = part[at, :]
+
+        @pl.when(me > 0)
+        def _():
+            rightward(slot).wait_recv()
+            out_ref[at, :] = out_ref[at, :] + got_l[slot].astype(F32)
+
+        @pl.when(me < parts - 1)
+        def _():
+            leftward(slot).wait_recv()
+            out_ref[at, :] = out_ref[at, :] + got_r[slot].astype(F32)
+
+    def finish(slot, _):
+        piece = slot // SUBS
+
+        @pl.when(piece > me)
+        def _():
+            rightward(slot).wait_send()
+
+        @pl.when(piece < me)
+        def _():
+            leftward(slot).wait_send()
+
+        return 0
+
+    lax.fori_loop(0, parts * SUBS, finish, 0)
+
+
+def scatter(parts, lefts, rights, splits, number):
+    total = lefts[0].shape[0]
+    model = rights[0].shape[0]
+    rows = total // parts
+    count = len(rights)
+    slots = pltpu.VMEM((parts * SUBS, rows // SUBS, model), LOW)
+    kernel = functools.partial(scatter_kernel, parts, len(lefts), count, splits)
+    return pl.pallas_call(
+        kernel,
+        out_shape=sds(rows, model),
+        in_specs=[vmem()] * len(lefts) + [hbm()] * count,
+        out_specs=vmem(),
+        scratch_shapes=[pltpu.VMEM(w.shape, LOW) for w in rights]
+        + [pltpu.VMEM((rows, model), F32)]
+        + [slots] * 4
+        + line_sems(parts * SUBS)
+        + [pltpu.SemaphoreType.DMA((count,))],
+        compiler_params=comm_params(number),
+        cost_estimate=cost(2 * total * model * sum(w.shape[1] for w in rights), 60 * 2**20),
+        name="scatter%d" % number,
+    )(*lefts, *rights)
+
+
+def state_kernel(count, heads, backward, own_ref, out_ref, buf, send_sem, pass_sem, got_sem, own_sem):
+    me = lax.axis_index("dp")
+    core = lax.rem(me, 2)
+    sibling = me + 1 - 2 * core
+    half = count // 2
+    barrier = pltpu.get_barrier_semaphore()
+
+    def peer(k):
+        return lax.rem(me + 2 * k, count)
+
+    def hello(k, _):
+        pl.semaphore_signal(barrier, inc=1, device_id={"dp": peer(k)}, device_id_type=MESH)
+        return 0
+
+    lax.fori_loop(1, half, hello, 0)
+    pl.semaphore_signal(barrier, inc=1, device_id={"dp": sibling}, device_id_type=MESH)
+    local = pltpu.make_async_copy(own_ref, buf.at[me], own_sem)
+    local.start()
+    local.wait()
+    pl.semaphore_wait(barrier, half)
+
+    def needed(source, target):
+        return source > target if backward else source < target
+
+    def copy(piece, target, sem):
+        return pltpu.make_async_remote_copy(
+            src_ref=buf.at[piece],
+            dst_ref=buf.at[piece],
+            send_sem=sem,
+            recv_sem=got_sem.at[piece],
+            device_id={"dp": target},
+            device_id_type=MESH,
+        )
+
+    def send(k, _):
+        target = peer(k)
+
+        @pl.when(needed(me, target))
+        def _():
+            copy(me, target, send_sem.at[target]).start()
+
+        return 0
+
+    @pl.when(needed(me, sibling))
+    def _():
+        copy(me, sibling, pass_sem.at[me]).start()
+
+    lax.fori_loop(1, half, send, 0)
+
+    def relay(k, _):
+        source = lax.rem(me + count - 2 * k, count)
+
+        @pl.when(needed(source, me))
+        def _():
+            copy(source, me, send_sem.at[source]).wait_recv()
+
+        @pl.when(needed(source, me) & needed(source, sibling))
+        def _():
+            copy(source, sibling, pass_sem.at[source]).start()
+
+        return 0
+
+    lax.fori_loop(1, half, relay, 0)
+    for h in range(heads):
+        out_ref[h] = jnp.zeros_like(out_ref[h])
+
+    def chain(step, _):
+        piece = count - 1 - step if backward else step
+
+        @pl.when(needed(piece, me) & (lax.rem(piece, 2) != core))
+        def _():
+            copy(piece, me, pass_sem.at[piece]).wait_recv()
+
+        @pl.when(needed(piece, me))
+        def _():
+            for h in range(heads):
+                both = buf[piece, h]
+                if backward:
+                    out_ref[h] = mm(both[:, 128:], out_ref[h], TN) + both[:, :128]
+                else:
+                    out_ref[h] = mm(both[:, 128:], out_ref[h]) + both[:, :128]
+
+        return 0
+
+    lax.fori_loop(0, count, chain, 0)
+
+    def finish(k, _):
+        target = peer(k)
+        source = lax.rem(me + count - 2 * k, count)
+
+        @pl.when(needed(me, target))
+        def _():
+            copy(me, target, send_sem.at[target]).wait_send()
+
+        @pl.when(needed(source, me) & needed(source, sibling))
+        def _():
+            copy(source, sibling, pass_sem.at[source]).wait_send()
+
+        return 0
+
+    lax.fori_loop(1, half, finish, 0)
+
+    @pl.when(needed(me, sibling))
+    def _():
+        copy(me, sibling, pass_sem.at[me]).wait_send()
+
+
+def exchange(count, own, heads, backward, number):
+    return pl.pallas_call(
+        functools.partial(state_kernel, count, heads, backward),
+        out_shape=sds(heads, 128, 128),
+        in_specs=[vmem()],
+        out_specs=vmem(),
+        scratch_shapes=[pltpu.VMEM((count, heads, 128, 256), F32)]
+        + [pltpu.SemaphoreType.DMA((count,))] * 3
+        + [pltpu.SemaphoreType.DMA],
+        compiler_params=comm_params(number),
+        cost_estimate=cost(count * heads * 6 * 128**3, count * heads * 256 * 128 * 4),
+        name="exchange%d" % number,
+    )(own)
+
+
+def totals_kernel(count, parts, kept, own_ref, wide_ref, flat_ref, buf, mid, send1, got1, send2, got2):
+    dp, z = lax.axis_index("dp"), lax.axis_index("tensor")
+    barrier = pltpu.get_barrier_semaphore()
+
+    def hello_dp(k, _):
+        pl.semaphore_signal(
+            barrier, inc=1, device_id={"dp": lax.rem(dp + k, count)}, device_id_type=MESH
+        )
+        return 0
+
+    def hello_z(k, _):
+        pl.semaphore_signal(
+            barrier, inc=1, device_id={"tensor": lax.rem(z + k, parts)}, device_id_type=MESH
+        )
+        return 0
+
+    lax.fori_loop(1, count, hello_dp, 0)
+    lax.fori_loop(1, parts, hello_z, 0)
+    buf[dp] = own_ref[...]
+    pl.semaphore_wait(barrier, count + parts - 2)
+
+    def over_dp(source, target):
+        return pltpu.make_async_remote_copy(
+            src_ref=buf.at[source],
+            dst_ref=buf.at[source],
+            send_sem=send1.at[target],
+            recv_sem=got1.at[source],
+            device_id={"dp": target},
+            device_id_type=MESH,
+        )
+
+    def over_z(source, target):
+        return pltpu.make_async_remote_copy(
+            src_ref=mid.at[source],
+            dst_ref=mid.at[source],
+            send_sem=send2.at[target],
+            recv_sem=got2.at[source],
+            device_id={"tensor": target},
+            device_id_type=MESH,
+        )
+
+    def each(total, me, action):
+        def body(k, _):
+            action(lax.rem(me + k, total))
+            return 0
+
+        lax.fori_loop(1, total, body, 0)
+
+    each(count, dp, lambda other: over_dp(dp, other).start())
+    each(count, dp, lambda other: over_dp(other, dp).wait_recv())
+    total = buf[0]
+    for i in range(1, count):
+        total = total + buf[i]
+    mid[z] = total
+    each(parts, z, lambda other: over_z(z, other).start())
+    each(parts, z, lambda other: over_z(other, z).wait_recv())
+    width = own_ref.shape[1]
+    flat = mid[0, kept:, :]
+    for i in range(parts):
+        wide_ref[:, i * width : (i + 1) * width] = mid[i, :kept, :]
+        if i:
+            flat = flat + mid[i, kept:, :]
+    flat_ref[...] = flat
+    each(count, dp, lambda other: over_dp(dp, other).wait_send())
+    each(parts, z, lambda other: over_z(z, other).wait_send())
+
+
+def totals_of(count, parts, own, kept, number):
+    rows, width = own.shape
+    return pl.pallas_call(
+        functools.partial(totals_kernel, count, parts, kept),
+        out_shape=(sds(kept, width * parts), sds(rows - kept, width)),
+        in_specs=[vmem()],
+        out_specs=[vmem(), vmem()],
+        scratch_shapes=[pltpu.VMEM((count, rows, width), F32), pltpu.VMEM((parts, rows, width), F32)]
+        + [pltpu.SemaphoreType.DMA((count,))] * 2
+        + [pltpu.SemaphoreType.DMA((parts,))] * 2,
+        compiler_params=comm_params(number),
+        cost_estimate=cost(count * rows * width, count * rows * width * 4),
+        name="totals",
+    )(own)
 
 
 def after(values, *first):
@@ -636,64 +1224,64 @@
         + seq_total * lax.broadcasted_iota(jnp.int32, doc_lengths.shape, 0)
     ).reshape(-1)
     scalars = jnp.concatenate([(dp_index * group_rows).reshape(1), starts]).astype(jnp.int32)
-    mine = dp_index.reshape(1).astype(jnp.int32)
     taps = jnp.concatenate([conv_query, conv_key, conv_value, jnp.zeros((4, width), F32)])
     params = jnp.zeros((8, 128), F32).at[0, :heads].set(decay_bias).at[1, :heads].set(decay_log)
     gain_heads = jnp.broadcast_to(head_gain[None], (8, width))
     w_narrow = jnp.pad(jnp.concatenate([w_alpha, w_beta], axis=1), ((0, 0), (0, 128 - 2 * heads)))
 
     own_rows = tokens.astype(F32)
-    normed_in = row_norm(own_rows, gain_in).astype(LOW)
-    normed_all = lax.all_gather(normed_in, "tensor", axis=0, tiled=True)
-    grad_act = contract_cols(out_grad, w_down)
+    gain_in_rows = jnp.broadcast_to(gain_in[None], (8, model))
+    gain_mid_rows = jnp.broadcast_to(gain_mid[None], (8, model))
+    normed_all, *pieces, gate_raw, narrow = project(
+        tensor_parts, tokens, gain_in_rows, w_narrow, (w_query, w_key, w_value, w_gate_out)
+    )
     half = width // 2
     core = lax.rem(dp_index, 2)
-    out_half = lax.dynamic_slice_in_dim(w_out, core * half, half, 0)
+    out_half = lax.dynamic_slice_in_dim(after(w_out, narrow), core * half, half, 0)
     out_mine = lax.all_gather(out_half, "tensor", axis=0)
-    out_other = lax.ppermute(out_mine, "dp", [(i, i ^ 1) for i in range(dp_parts)])
+    forth = [(i, i + 1) for i in range(dp_parts - 1)]
+    rims = lax.ppermute(
+        jnp.stack([piece[group_rows - HALO :] for piece in pieces]), "dp", forth
+    )
+    rims = [rims[i] for i in range(3)]
+    x, p, kg, w, u, qt, ou, t, o, totals = intra(
+        scalars, pieces, rims, narrow, taps, params, docs, heads
+    )
+    state_in = exchange(dp_parts, totals, heads, False, 3)
+    out_other = lax.ppermute(after(out_mine, state_in), "dp", [(i, i ^ 1) for i in range(dp_parts)])
     w_out_full = jnp.stack(
         [jnp.where(core == 0, out_mine, out_other), jnp.where(core == 0, out_other, out_mine)],
         axis=1,
     ).reshape(width * tensor_parts, model)
-
-    pieces = [dot(normed_all, w).astype(LOW) for w in (w_query, w_key, w_value)]
-    narrow = dot(normed_all, w_narrow)
-    forth = [(i, i + 1) for i in range(dp_parts - 1)]
-    rims = lax.ppermute(
-        jnp.stack([piece[group_rows - HALO :] for piece in pieces]), "dp", forth
-    )
-    rims = [rims[i] for i in range(3)]
-    x, p, kg, w, u, qt, ou, t, o, totals = intra(
-        scalars, pieces, rims, narrow, taps, params, docs, heads
-    )
-    gate_raw = dot(normed_all, w_gate_out)
-    maps = lax.all_gather(totals, "dp", axis=0)
-    state_in = chain(mine, maps, None, heads)
     rows_out, v2, s, mixed = outward(state_in, w, u, qt, ou, t, o, gate_raw, gain_heads, heads)
 
     mixed_own = lax.all_to_all(mixed, "tensor", split_axis=0, concat_axis=1, tiled=True)
     residual = own_rows + dot(mixed_own, w_out_full)
-    normed_mid = row_norm(residual, gain_mid).astype(LOW)
-    mid_all = lax.all_gather(normed_mid, "tensor", axis=0, tiled=True)
-    gate_pre = dot(mid_all, w_gate)
-    up_pre = dot(mid_all, w_up)
-    sigmoid_gate = jax.nn.sigmoid(gate_pre)
-    act = gate_pre * sigmoid_gate
-    activated = (act * up_pre).astype(LOW)
-    grad_gate = (grad_act * up_pre * sigmoid_gate * (1.0 + gate_pre * (1.0 - sigmoid_gate))).astype(LOW)
-    grad_up = (grad_act * act).astype(LOW)
-    grad_mid_part = (contract_cols(grad_gate, w_gate) + contract_cols(grad_up, w_up)).astype(LOW)
-    grad_mid = lax.psum_scatter(grad_mid_part, "tensor", scatter_dimension=0, tiled=True).astype(F32)
-
-    gate_grad = contract_rows(mid_all, grad_gate).astype(LOW)
-    up_grad = contract_rows(mid_all, grad_up).astype(LOW)
-    down_grad = contract_rows(out_grad, activated).astype(LOW)
+    mid_all, activated, grad_units = feed(
+        tensor_parts, residual, gain_mid_rows, (w_gate, w_up, w_down), out_grad
+    )
+    units = w_gate.shape[1]
+    ring = [(i, (i + 1) % tensor_parts) for i in range(tensor_parts)]
+
+    def piece_of(values, back_by):
+        index = lax.rem(tensor_index - back_by + tensor_parts, tensor_parts)
+        return lax.dynamic_slice_in_dim(values, index * rows_own, rows_own, 0)
+
+    def added(values, back_by, got):
+        return (piece_of(values, back_by).astype(F32) + got.astype(F32)).astype(LOW)
+
     mlp_part = dot(activated, w_down).astype(LOW)
-    ffn_grads = [
-        lax.psum_scatter(part, "dp", scatter_dimension=0, tiled=True)
-        for part in (gate_grad, up_grad, down_grad)
-    ]
-
+    mlp_run = lax.ppermute(piece_of(mlp_part, 1), "tensor", ring)
+    out_grad_2, activated_2, mlp_part = lax.optimization_barrier((out_grad, activated, mlp_part))
+    down_grad = contract_rows(out_grad_2, activated_2).astype(LOW)
+    units_grad = contract_rows(mid_all, after(grad_units, down_grad)).astype(LOW)
+    down_grad_sum = lax.psum_scatter(down_grad, "dp", scatter_dimension=0, tiled=True)
+    units_grad_sum = lax.psum_scatter(units_grad, "dp", scatter_dimension=0, tiled=True)
+
+    grad_mid = scatter(
+        tensor_parts, [after(grad_units, units_grad, mlp_run)], [w_gate, w_up],
+        ((0, 0, units), (0, units, units)), 4,
+    )
     grad_res_norm, gain_mid_grad = norm_back(residual, gain_mid, grad_mid)
     grad_own = lax.dynamic_slice_in_dim(out_grad, tensor_index * rows_own, rows_own, 0)
     grad_residual = grad_own.astype(F32) + grad_res_norm
@@ -701,86 +1289,91 @@
     grad_mixed_own = contract_cols(grad_mixer, w_out_full).astype(LOW)
     grad_mixed = lax.all_to_all(
         grad_mixed_own, "tensor", split_axis=1, concat_axis=0, tiled=True
-    ).astype(F32)
-    mlp_rows = lax.psum_scatter(after(mlp_part, grad_mid), "tensor", scatter_dimension=0, tiled=True)
-    output = (residual + mlp_rows.astype(F32)).astype(LOW)
-    grad_mixer_all = lax.all_gather(after(grad_mixer, grad_mixed), "tensor", axis=0, tiled=True)
+    )
+    mixer_pieces = [grad_mixer]
+    grad_mixer_1, mlp_run = lax.optimization_barrier((grad_mixer, mlp_run, grad_mixed))[:2]
+    mixer_pieces.append(lax.ppermute(grad_mixer_1, "tensor", ring))
+    for back_by in range(2, tensor_parts - 1):
+        mlp_run = lax.ppermute(added(mlp_part, back_by, mlp_run), "tensor", ring)
 
     do, gate_low, head_gain_part, ds_total = inward(
-        grad_mixed, rows_out, gate_raw, gain_heads, qt, t, heads
-    )
-    sums = lax.all_gather(ds_total, "dp", axis=0)
-    gate_out_grad = lax.psum_scatter(
-        contract_rows(normed_all, gate_low).astype(LOW), "dp", scatter_dimension=0, tiled=True
-    )
-    grad_end = chain(mine, maps, sums, heads)
-    gq, gk, gv, tails, rim_grad, narrow_low, taps_grad, params_grad = back(
+        grad_mixed, rows_out, gate_raw, gain_heads, qt, t, totals, heads
+    )
+    grad_end = exchange(dp_parts, ds_total, heads, True, 5)
+    grad_end, piece_1, mlp_run, _, _ = lax.optimization_barrier(
+        (grad_end, mixer_pieces[1], mlp_run, units_grad_sum, down_grad_sum)
+    )
+    mixer_pieces[1] = piece_1
+    mixer_pieces.append(lax.ppermute(piece_1, "tensor", ring))
+    mlp_run = lax.ppermute(added(mlp_part, tensor_parts - 1, mlp_run), "tensor", ring)
+    output = (residual + (piece_of(mlp_part, 0).astype(F32) + mlp_run.astype(F32))).astype(LOW)
+    grads, tails, rim_grad, taps_grad, params_grad = back(
         scalars, pieces, rims, narrow, taps, params, grad_end, do, v2, s, x, p, kg, w, u, qt, t,
         docs, heads,
     )
-    out_w_grad = lax.psum_scatter(
-        contract_rows(grad_mixer_all, mixed).astype(LOW), "dp", scatter_dimension=0, tiled=True
-    )
     rim_back = lax.ppermute(rim_grad, "dp", [(i + 1, i) for i in range(dp_parts - 1)])
-    tails = tails.at[:, HALO - 8 :].add(rim_back).astype(LOW)
-    grads = [
-        lax.dynamic_update_slice_in_dim(g, tails[i], group_rows - HALO, 0)
-        for i, g in enumerate((gq, gk, gv))
-    ]
-    summed = contract_cols(gate_low, w_gate_out) + contract_cols(narrow_low, w_narrow)
-    for g, weight in zip(grads, (w_query, w_key, w_value)):
-        summed = summed + contract_cols(g, weight)
-    grad_normed = lax.psum_scatter(
-        summed.astype(LOW), "tensor", scatter_dimension=0, tiled=True
-    ).astype(F32)
-    narrow_grad = contract_rows(normed_all, narrow_low)[:, : 2 * heads].astype(LOW)
-    qkv_grads = [
-        lax.psum_scatter(
-            contract_rows(normed_all, g).astype(LOW), "dp", scatter_dimension=0, tiled=True
+    tails = tails.at[HALO - 8 :].add(rim_back).astype(LOW)
+    grads = lax.dynamic_update_slice(grads, tails, (group_rows - HALO, 0))
+    grads, piece_last, _ = lax.optimization_barrier((grads, mixer_pieces[-1], mlp_run))
+    for _ in range(3, tensor_parts):
+        piece_last = lax.ppermute(piece_last, "tensor", ring)
+        mixer_pieces.append(piece_last)
+    grads_w = contract_rows(normed_all, grads).astype(LOW)
+    gate_w = contract_rows(normed_all, gate_low).astype(LOW)
+    grad_mixer_all = jnp.zeros((group_rows, model), LOW)
+    for back_by, piece in enumerate(mixer_pieces):
+        index = lax.rem(tensor_index - back_by + tensor_parts, tensor_parts)
+        grad_mixer_all = lax.dynamic_update_slice_in_dim(
+            grad_mixer_all, piece, index * rows_own, 0
         )
-        for g in grads
-    ]
-    narrow_grad = lax.psum_scatter(narrow_grad, "dp", scatter_dimension=0, tiled=True).astype(F32)
+    out_w = contract_rows(after(grad_mixer_all, grads_w, gate_w), mixed).astype(LOW)
+    mixer_grad = jnp.concatenate([grads_w, gate_w, out_w], axis=1)
+    mixer_sum = lax.psum_scatter(mixer_grad, "dp", scatter_dimension=0, tiled=True).astype(F32)
+    grad_normed = scatter(
+        tensor_parts, [after(grads, mixer_grad), gate_low],
+        [w_query, w_key, w_value, w_narrow, w_gate_out],
+        ((0, 0, width), (0, width, width), (0, 2 * width, width), (0, 3 * width, 128), (1, 0, width)),
+        6,
+    )
     grad_tokens, gain_in_grad = norm_back(own_rows, gain_in, grad_normed)
     input_grad = grad_residual + grad_tokens
 
-    params_grad = params_grad.reshape(2, 8, 128).sum(1)[:, :heads]
+    params_grad = params_grad.reshape(2, 8, 128).sum(1)
     flat = jnp.concatenate(
-        [taps_grad.sum(1), head_gain_part.sum(0)[None]], axis=0
-    )
-    wide = lax.dynamic_update_slice_in_dim(
-        jnp.zeros((13, width * tensor_parts), F32), flat, tensor_index * width, 1
-    )
-    thin = lax.dynamic_update_slice_in_dim(
-        jnp.zeros((2, heads * tensor_parts), F32), params_grad, tensor_index * heads, 1
-    )
-    packed = jnp.concatenate([wide.reshape(-1), thin.reshape(-1), gain_in_grad, gain_mid_grad])
-    packed = lax.psum(packed, ("dp", "tensor"))
-    channels = width * tensor_parts
-    wide = packed[: 13 * channels].reshape(13, channels)
-    rest = packed[13 * channels :]
-    all_heads = heads * tensor_parts
+        [
+            taps_grad.sum(1),
+            head_gain_part.sum(0)[None],
+            jnp.pad(params_grad, ((0, 1), (0, width - 128))),
+            gain_in_grad.reshape(-1, width),
+            gain_mid_grad.reshape(-1, width),
+        ],
+        axis=0,
+    )
+    wide, gains = totals_of(dp_parts, tensor_parts, flat, 16, 7)
+    by_head = wide[13:15].reshape(2, tensor_parts, width)[:, :, :heads].reshape(2, -1)
+    gains = gains.reshape(2, model)
+    start = 3 * width
     return (
         output,
         input_grad,
-        rest[2 * all_heads : 2 * all_heads + model],
-        qkv_grads[0].astype(F32),
-        qkv_grads[1].astype(F32),
-        qkv_grads[2].astype(F32),
-        narrow_grad[:, :heads],
-        narrow_grad[:, heads:],
-        gate_out_grad.astype(F32),
+        gains[0],
+        mixer_sum[:, :width],
+        mixer_sum[:, width : 2 * width],
+        mixer_sum[:, 2 * width : start],
+        mixer_sum[:, start : start + heads],
+        mixer_sum[:, start + heads : start + 2 * heads],
+        mixer_sum[:, start + 128 : start + 128 + width],
         wide[0:4],
         wide[4:8],
         wide[8:12],
-        rest[all_heads : 2 * all_heads],
-        rest[:all_heads],
+        by_head[1],
+        by_head[0],
         wide[12],
-        out_w_grad.T.astype(F32),
-        rest[2 * all_heads + model :],
-        ffn_grads[0].astype(F32),
-        ffn_grads[1].astype(F32),
-        ffn_grads[2].T.astype(F32),
+        mixer_sum[:, start + 128 + width :].T,
+        gains[1],
+        units_grad_sum[:, :units].astype(F32),
+        units_grad_sum[:, units:].astype(F32),
+        down_grad_sum.T.astype(F32),
     )
 
 

time: 1400 us -> 840 us (0.60)
  waiting for transfers between devices: 942 us -> 121 us
  Pallas kernels: 122 us -> 503 us
  matrix products: 204 us -> 66.8 us
  blocking collectives: 28.5 us -> 0 us
  local copies, waits for them, and re-layouts: 21.1 us -> 40 us
  starting transfers between devices: 10.8 us -> 25.2 us
    reduce_scatter x12 -> x3, waiting for transfers between devices: 594 us -> 0.03 us  [the longest x1 0.02 us: local(): lax.psum_scatter(units_grad, 'dp', scatter_dimension=0, tiled=True)]
    pallas_call x2 -> x7, Pallas kernels: 12.2 us -> 393 us  [the longest x2 167 us: scatter(): pl.pallas_call(kernel, out_shape=sds(rows, model), in_specs=[vmem()] * le...]
    all_gather x5 -> x0, waiting for transfers between devices: 189 us -> none  [the longest x1 79.6 us: local(): mid_all = lax.all_gather(normed_mid, 'tensor', axis=0, tiled=True)]
    psum x1 -> x0, waiting for transfers between devices: 123 us -> none  [local(): packed = lax.psum(packed, ('dp', 'tensor'))]
    ppermute x1 -> x7, waiting for transfers between devices: 0.01 us -> 84.8 us  [the longest x1 28.4 us: local(): mlp_run = lax.ppermute(piece_of(mlp_part, 1), 'tensor', ring)]
    dot_general x9 -> x1, matrix products: 81.1 us -> 3.58 us  [contract_cols(): return lax.dot_general(left, right, NT, preferred_element_type=F32)]
    dot_general x9 -> x2, matrix products: 57.5 us -> 18.2 us  [dot(): return jnp.dot(left, right, preferred_element_type=F32)]
    all_to_all x1 -> x0, blocking collectives: 28.5 us -> none  [local(): lax.all_to_all(grad_mixed_own, 'tensor', split_axis=1, concat_axis=0, til...]
  transfers between devices with their start and end apart: 23 -> 15, of which waited for: 18 -> 8; matrix products, arithmetic and copies ran while one was open for 13% -> 12% of each run, Pallas kernels for 8% -> 37%
where the time goes in v2:
time: 840 us; the launch traced here: 830 us
  Pallas kernels  503 us (60%)
  waiting for transfers between devices  121 us (14%)
  matrix products  66.8 us (8%)
  other arithmetic  58.1 us (7%)
  local copies, waits for them, and re-layouts  40 us (5%)
  starting transfers between devices  25.2 us (3%)
  between operations  14.8 us (2%)
    pallas_call x2, Pallas kernels, scatter(): pl.pallas_call(kernel, out_shape=sds(rows, model), in_specs=[vmem()] * le...  167 us
    pallas_call x1, Pallas kernels, feed(): pl.pallas_call(functools.partial(feed_kernel, parts), out_shape=(sds(tota...  77.2 us
    pallas_call x1, Pallas kernels, project(): pl.pallas_call(functools.partial(project_kernel, parts), out_shape=(sds(t...  75.2 us
    pallas_call x2, Pallas kernels, exchange(): pl.pallas_call(functools.partial(state_kernel, count, heads, backward), o...  56.8 us
    pallas_call x1, Pallas kernels, back(): pl.pallas_call(functools.partial(back_kernel, docs, heads, chunks), out_s...  47.7 us
    dot_general x5, matrix products, contract_rows(): return lax.dot_general(left, right, TN, preferred_element_type=F32)  45.1 us
    pallas_call x1, Pallas kernels, intra(): pl.pallas_call(functools.partial(intra_kernel, docs, heads), out_shape=(t...  41 us
    ppermute x1, waiting for transfers between devices, local(): mlp_run = lax.ppermute(piece_of(mlp_part, 1), 'tensor', ring)  28.4 us
  transfers between devices with their start and end apart: 15, of which 8 were waited for; matrix products, arithmetic and copies ran while one was open for 12% of the time, Pallas kernels for 37%

profile of v2, /device:TPU:12, one launch (start us, length us, event | category | flops | bytes accessed | tf_op | source)
XLA Modules:
  0.0 829.5 jit_solution(38845719061755455)
XLA Ops:
  10.7 75.2 %project.1 = (bf16[1024,2048]{1,0:T(8,128)(2,1)}, bf16[1024,512]{1,0:T(8,128)(2,1)}, bf16[1024,512]{1,0:T(8,128)(2,1)}, bf16[1024,512]{1,0:T(8,128)(2,1)}, f32[1024,512]{1,0:T(8,128)}, /*index=5*/f32[1024,128]{1,0:T(8,128)}) custom-call(bf16[256,2048]{1,0:T(8,128)(2,1)} %tok_ref.1, f32[8,2048]{1,0:T(8,128)} %broadcast_in_dim.12.gain_ref, ...), custom_call_target="tpu_custom_call" | custom-call | flops 9126805504 | bytes 62914560 | tf_op jit(solution)/shard_map/project/pallas_call | solution.py:722
  95.5 41.0 %intra.1 = (f32[8,4,128,128]{3,2,1,0:T(8,128)}, f32[8,4,128,128]{3,2,1,0:T(8,128)}, f32[8,4,128,128]{3,2,1,0:T(8,128)}, f32[1024,512]{1,0:T(8,128)}, f32[1024,51...) custom-call(s32[5]{0:T(128)} %pad_add_fusion.scalars, ...), custom_call_target="tpu_custom_call" | custom-call | flops 24159191040 | bytes 62914560 | tf_op jit(solution)/shard_map/intra/pallas_call | solution.py:238
  136.4 27.6 %exchange3.1.s_in = f32[4,128,128]{2,1,0:T(8,128)} custom-call(f32[4,128,256]{2,1,0:T(8,128)} %get-tuple-element.110.own_ref.maps_ref), custom_call_target="tpu_custom_call" | custom-call | flops 402653184 | bytes 4194304 | tf_op jit(solution)/shard_map/exchange3/pallas_call | solution.py:1088
  164.0 5.1 all-gather.3.cloned.1.call-done
  169.7 11.5 %outward.1 = (f32[1024,512]{1,0:T(8,128)}, f32[1024,512]{1,0:T(8,128)}, f32[8,4,128,128]{3,2,1,0:T(8,128)}, bf16[1024,512]{1,0:T(8,128)(2,1)}) custom-call(f32[4,128,128]{2,1,0:T(8,128)} %exchange3.1.s_in, f32[1024,512]{1,0:T(8,128)} %get-tuple-element.111.w_ref.refs_19_, f32[1024,512]{1,0:T(8,128)} %get-tuple-element.112.u_ref.refs_20_, ...), custom_call_target="tpu_custom_call" | custom-call | flops 1207959552 | bytes 23068672 | tf_op jit(solution)/shard_map/outward/pallas_call | solution.py:294
  183.4 6.5 all-to-all-start
  190.2 5.8 select_bitcast_fusion.1
  196.0 7.5 pad_maximum_fusion.1
  203.5 9.9 %all-to-all-done = bf16[4,256,512]{1,2,0:T(8,128)(2,1)S(1)} async-done(((bf16[4,256,512]{1,2,0:T(8,128)(2,1)}), bf16[4,256,512]{1,2,0:T(8,128)(2,1)S(1)}, u32[]{:S(2)}, u32[]{:S(2)}) %all-to-all-start) | async-done | bytes 1048608 | tf_op jit(solution)/shard_map/all_to_all | solution.py:1258
  213.4 7.1 multiply_reduce_fusion.2
  221.1 77.2 %feed.1 = (bf16[1024,2048]{1,0:T(8,128)(2,1)}, bf16[1024,1408]{1,0:T(8,128)(2,1)}, bf16[1024,2816]{1,0:T(8,128)(2,1)}) custom-call(f32[256,2048]{1,0:T(8,128)} %get-tuple-element.245.res_ref, f32[8,2048]{1,0:T(8,128)} %broadcast_in_dim.15.gain_ref, bf16[2048,1408]{1,0:T(8,128)(2,1)} %refs_1_.5, bf16[2048,1408]{1,0:T(8,128)(2,1)} %refs_2_.6, ...), custom_call_target="tpu_custom_call" | custom-call | flops 17716740096 | bytes 125829120 | tf_op jit(solution)/shard_map/feed/pallas_call | solution.py:796
  298.3 11.1 %convolution_convert_fusion.3 = bf16[1024,2048]{1,0:T(8,128)(2,1)} fusion(bf16[1024,1408]{1,0:T(8,128)(2,1)} %get-tuple-element.126, bf16[1408,2048]{1,0:T(8,128)(2,1)} %refs_2_.5), kind=kOutput, calls=%fused_computation.12 | convolution fusion | flops 5907677184 | bytes 12845056 | tf_op jit(solution)/shard_map/dot_general | solution.py:535
  309.4 8.7 %convolution_convert_fusion.2 = bf16[2048,1408]{1,0:T(8,128)(2,1)} fusion(bf16[1024,2048]{1,0:T(8,128)(2,1)S(1)} %copy-done.9, bf16[1024,1408]{1,0:T(8,128)(2,1)S(1)} %copy-done.28), kind=kOutput, calls=%fused_computation.4 | convolution fusion | flops 5908463616 | bytes 12845056 | tf_op jit(solution)/shard_map/dot_general | solution.py:527
  318.6 18.6 %convolution_convert_fusion = bf16[2048,2816]{1,0:T(8,128)(2,1)} fusion(bf16[1024,2048]{1,0:T(8,128)(2,1)} %get-tuple-element.124, bf16[1024,2816]{1,0:T(8,128)(2,1)} %get-tuple-element.128.refs_0_), kind=kOutput, calls=%fused_computation | convolution fusion | flops 11816927232 | bytes 21495808 | tf_op jit(solution)/shard_map/dot_general | solution.py:527
  340.6 28.4 %collective-permute-done.2 = bf16[256,2048]{1,0:T(8,128)(2,1)} collective-permute-done((bf16[256,2048]{1,0:T(8,128)(2,1)}, bf16[256,2048]{1,0:T(8,128)(2,1)}, u32[]{:S(2)}, u32[]{:S(2)}) %collective-permute-start.2) | collective-permute-done | bytes 1048608 | tf_op jit(solution)/shard_map/ppermute | solution.py:1274
  369.0 82.7 %scatter4.1 = f32[256,2048]{1,0:T(8,128)} custom-call(bf16[1024,2816]{1,0:T(8,128)(2,1)} %get-tuple-element.128.refs_0_, bf16[2048,1408]{1,0:T(8,128)(2,1)} %refs_1_.5, bf16[2048,1408]{1,0:T(8,128)(2,1)} %refs_2_.6), custom_call_target="tpu_custom_call" | custom-call | flops 11811160064 | bytes 62914560 | tf_op jit(solution)/shard_map/scatter4/pallas_call | solution.py:964
  465.7 4.2 all-to-all-start.1
  470.1 19.1 %all-to-all-done.1 = bf16[256,4,512]{2,0,1:T(8,128)(2,1)} async-done(((bf16[256,4,512]{2,0,1:T(8,128)(2,1)}), bf16[256,4,512]{2,0,1:T(8,128)(2,1)}, u32[]{:S(2)}, u32[]{:S(2)}) %all-to-all-start.1) | async-done | bytes 1048608 | tf_op jit(solution)/shard_map/all_to_all | solution.py:1290
  492.2 3.9 collective-permute-start.3
  496.1 10.4 %inward.1 = (f32[1024,512]{1,0:T(8,128)}, bf16[1024,512]{1,0:T(8,128)(2,1)}, f32[8,512]{1,0:T(8,128)}, f32[4,128,256]{2,1,0:T(8,128)}) custom-call(bf16[1024,512]{1,0:T(8,128)(2,1)} %bitcast.19.gm_ref, f32[1024,512]{1,0:T(8,128)} %get-tuple-element.129.out_ref, f32[1024,512]{1,0:T(8,128)} %get-tuple-element.117.gate_ref, ...), custom_call_target="tpu_custom_call" | custom-call | flops 805306368 | bytes 14680064 | tf_op jit(solution)/shard_map/inward/pallas_call | solution.py:344
  506.5 29.2 %exchange5.1.refs_12_ = f32[4,128,128]{2,1,0:T(8,128)} custom-call(f32[4,128,256]{2,1,0:T(8,128)} %get-tuple-element.130.own_ref), custom_call_target="tpu_custom_call" | custom-call | flops 402653184 | bytes 4194304 | tf_op jit(solution)/shard_map/exchange5/pallas_call | solution.py:1088
  535.8 6.2 convolution_convert_fusion.5
  542.1 47.7 %back.1 = (bf16[1024,1664]{1,0:T(8,128)(2,1)}, f32[16,1536]{1,0:T(8,128)}, f32[8,1536]{1,0:T(8,128)}, f32[12,8,512]{2,1,0:T(8,128)}, f32[16,128]{1,0:T(8,128)}) custom-call(s32[5]{0:T(128)} %pad_add_fusion.scalars, bf16[1024,512]{1,0:T(8,128)(2,1)} %get-tuple-element.106.refs_0_.refs_3_, bf16[1024,512]{1,0:T(8,128)(2,1)} %get-tuple-element.107.refs_1_.refs_4_, ...), custom_call_target="tpu_custom_call" | custom-call | flops 8053063680 | bytes 33554432 | tf_op jit(solution)/shard_map/back/pallas_call | solution.py:501
  589.8 4.3 collective-permute-start.6
  598.7 23.5 %collective-permute-done.5 = bf16[256,2048]{1,0:T(8,128)(2,1)S(1)} collective-permute-done((bf16[256,2048]{1,0:T(8,128)(2,1)S(1)}, bf16[256,2048]{1,0:T(8,128)(2,1)S(1)}, u32[]{:S(2)}, u32[]{:S(2)}) %collective-permute-start.5) | collective-permute-done | bytes 1048608 | tf_op jit(solution)/shard_map/ppermute | solution.py:1308
  622.3 19.8 %collective-permute-done.7 = bf16[256,2048]{1,0:T(8,128)(2,1)S(1)} collective-permute-done((bf16[256,2048]{1,0:T(8,128)(2,1)}, bf16[256,2048]{1,0:T(8,128)(2,1)S(1)}, u32[]{:S(2)}, u32[]{:S(2)}) %collective-permute-start.7) | collective-permute-done | bytes 1048608 | tf_op jit(solution)/shard_map/ppermute | solution.py:1307
  643.3 9.1 %convolution_convert_fusion.1 = bf16[2048,1664]{0,1:T(8,128)(2,1)S(1)} fusion(bf16[1024,2048]{1,0:T(8,128)(2,1)} %get-tuple-element.146, bf16[1024,1664]{1,0:T(8,128)(2,1)S(1)} %convert_dynamic-update-slice_fusion.refs_0_), kind=kOutput, calls=%fused_computation.3 | convolution fusion | flops 6982729728 | bytes 14417920 | tf_op jit(solution)/shard_map/dot_general | solution.py:527
  652.5 13.1 %collective-permute-done.8 = bf16[256,2048]{1,0:T(8,128)(2,1)S(1)} collective-permute-done((bf16[256,2048]{1,0:T(8,128)(2,1)S(1)}, bf16[256,2048]{1,0:T(8,128)(2,1)S(1)}, u32[]{:S(2)}, u32[]{:S(2)}) %collective-permute-start.8) | collective-permute-done | bytes 1048608 | tf_op jit(solution)/shard_map/ppermute | solution.py:1319
  668.2 17.9 %pad_maximum_fusion = bf16[2048,2688]{0,1:T(8,128)(2,1)} fusion(bf16[2048,512]{0,1:T(8,128)(2,1)S(1)} %convolution_convert_fusion.4, bf16[2048,512]{0,1:T(8,128)(2,1)S(1)} %copy-done.8, bf16[2048,1664]{0,1:T(8,128)(2,1)S(1)} %convolution_convert_fusion.1), kind=kLoop, calls=%fused_computation.1 | loop fusion | flops 33030144 | bytes 22020096 | tf_op jit(solution)/shard_map/concatenate | solution.py:1330
  692.2 84.5 %scatter6.1 = f32[256,2048]{1,0:T(8,128)} custom-call(bf16[1024,1664]{1,0:T(8,128)(2,1)} %copy-done.26, bf16[1024,512]{1,0:T(8,128)(2,1)} %get-tuple-element.147.refs_1_, bf16[2048,512]{1,0:T(8,128)(2,1)} %refs_2_.7, bf16[2048,512]{1,0:T(8,128)(2,1)} %refs_3_.5, bf16[2048,512]{1,0:T(8,128)(2,1)} %refs_4_.1, bf16[2048,128]{1,0:T(8,128)(2,1)} %pad.18.narrow_w.refs_5_, ...), custom_call_target="tpu_custom_call" | custom-call | flops 9126805504 | bytes 62914560 | tf_op jit(solution)/shard_map/scatter6/pallas_call | solution.py:964
  784.5 16.2 %totals.1 = (f32[16,2048]{1,0:T(8,128)}, f32[8,512]{1,0:T(8,128)}) custom-call(f32[24,512]{1,0:T(8,128)} %concatenate.25.own_ref), custom_call_target="tpu_custom_call" | custom-call | flops 98304 | bytes 393216 | tf_op jit(solution)/shard_map/totals/pallas_call | solution.py:1171
  807.7 5.8 fusion.3
  (154 shorter events, 76.0 us)
Async XLA Ops:
  7.2 78.8 %copy-start = (bf16[512,2048]{1,0:T(8,128)(2,1)S(1)}, bf16[512,2048]{1,0:T(8,128)(2,1)}, u32[]{:S(2)}) copy-start(bf16[512,2048]{1,0:T(8,128)(2,1)} %param.41) | copy-start | bytes 6291460
  7.2 161.9 %all-gather.3.cloned.1.call-start = ((), (), s32[]{:S(2)}) async-start(), calls=%async_computation.8 | async-start | bytes 5242880 | tf_op jit(solution)/shard_map/all_gather | solution.py:1241
  85.9 6.1 copy-start.23
  88.5 6.3 collective-permute-start
  95.5 73.6 %copy-start.22 = (f32[512]{0:T(512)S(1)}, f32[512]{0:T(512)}, u32[]{:S(2)}) copy-start(f32[512]{0:T(512)} %param.40) | copy-start | bytes 6148
  169.1 21.1 %collective-permute-start.1 = (bf16[4,256,2048]{2,1,0:T(8,128)(2,1)}, bf16[4,256,2048]{2,1,0:T(8,128)(2,1)}, u32[]{:S(2)}, u32[]{:S(2)}) collective-permute-start(bf16[4,256,2048]{2,1,0:T(8,128)(2,1)} %bitcast.71), channel_id=1, source_target_pairs={{0,4},{4,0},{8,12},{12,8},{16,20},{20,16},{24,28},{28,24},{1,5},{5... | collective-permute-start | bytes 12582920 | tf_op jit(solution)/shard_map/ppermute | solution.py:1251
  183.4 29.9 %all-to-all-start = ((bf16[4,256,512]{1,2,0:T(8,128)(2,1)}), bf16[4,256,512]{1,2,0:T(8,128)(2,1)S(1)}, u32[]{:S(2)}, u32[]{:S(2)}) async-start(bf16[4,256,512]{1,2,0:T(8,128)(2,1)} %copy.60), calls=%async_computation | async-start | bytes 2097152 | tf_op jit(solution)/shard_map/all_to_all | solution.py:1258
  190.0 352.1 %reduce-scatter.6.cloned.1.call-start = ((), (), s32[]{:S(2)}) async-start(), calls=%async_computation.6 | async-start | bytes 6488064 | tf_op jit(solution)/shard_map/reduce_scatter | solution.py:1278
  196.0 17.4 %copy-start.4 = (bf16[256,2048]{1,0:T(8,128)(2,1)S(1)}, bf16[256,2048]{1,0:T(8,128)(2,1)}, u32[]{:S(2)}) copy-start(bf16[256,2048]{1,0:T(8,128)(2,1)} %tok_ref.1) | copy-start | bytes 3145732
  213.4 7.1 copy-start.14
  298.3 11.1 %copy-start.9 = (bf16[1024,2048]{1,0:T(8,128)(2,1)S(1)}, bf16[1024,2048]{1,0:T(8,128)(2,1)}, u32[]{:S(2)}) copy-start(bf16[1024,2048]{1,0:T(8,128)(2,1)} %refs_3_.4) | copy-start | bytes 12582916
  298.3 11.1 %copy-start.28 = (bf16[1024,1408]{1,0:T(8,128)(2,1)S(1)}, bf16[1024,1408]{1,0:T(8,128)(2,1)}, u32[]{:S(2)}) copy-start(bf16[1024,1408]{1,0:T(8,128)(2,1)} %get-tuple-element.126) | copy-start | bytes 8650756
  318.1 224.0 %reduce-scatter.4.cloned.1.call-start = ((), (), s32[]{:S(2)}) async-start(), calls=%async_computation.5 | async-start | bytes 12976128 | tf_op jit(solution)/shard_map/reduce_scatter | solution.py:1279
  339.6 29.4 %collective-permute-start.2 = (bf16[256,2048]{1,0:T(8,128)(2,1)}, bf16[256,2048]{1,0:T(8,128)(2,1)}, u32[]{:S(2)}, u32[]{:S(2)}) collective-permute-start(bf16[256,2048]{1,0:T(8,128)(2,1)} %constant_dynamic-slice_fusion), channel_id=1, source_target_pairs={{0,1},{1,2},{2,3},{3,0},{4,5},{5,6},{6,7},{7,4},{8,9},{9,10},{10,1... | collective-permute-start | bytes 3145736 | tf_op jit(solution)/shard_map/ppermute | solution.py:1274
  340.6 111.1 %copy-start.2 = (f32[256,2048]{1,0:T(8,128)S(1)}, f32[256,2048]{1,0:T(8,128)}, u32[]{:S(2)}) copy-start(f32[256,2048]{1,0:T(8,128)} %get-tuple-element.245.res_ref) | copy-start | bytes 6291460
  451.7 9.4 %slice-start = ((s8[8388608]{0:T(1024)(128)(4,1)}), s8[4194304]{0:T(1024)(128)(4,1)S(1)}, s32[]{:S(2)}) async-start(s8[8388608]{0:T(1024)(128)(4,1)} %bitcast.67), calls=%async_computation.9 | async-start | bytes 8388608
  454.0 7.0 slice-start.1
  465.7 23.4 %all-to-all-start.1 = ((bf16[256,4,512]{2,0,1:T(8,128)(2,1)}), bf16[256,4,512]{2,0,1:T(8,128)(2,1)}, u32[]{:S(2)}, u32[]{:S(2)}) async-start(bf16[256,4,512]{2,0,1:T(8,128)(2,1)} %bitcast.73), calls=%async_computation.1 | async-start | bytes 2097152 | tf_op jit(solution)/shard_map/all_to_all | solution.py:1290
  470.0 343.6 %reduce-scatter.8.cloned.1.call-start = ((), (), s32[]{:S(2)}) async-start(), calls=%async_computation.7 | async-start | bytes 12386304 | tf_op jit(solution)/shard_map/reduce_scatter | solution.py:1331
  492.0 50.0 %collective-permute-start.4 = (bf16[256,2048]{1,0:T(8,128)(2,1)}, bf16[256,2048]{1,0:T(8,128)(2,1)}, u32[]{:S(2)}, u32[]{:S(2)}) collective-permute-start(bf16[256,2048]{1,0:T(8,128)(2,1)} %add_convert_fusion.2), channel_id=1, source_target_pairs={{0,1},{1,2},{2,3},{3,0},{4,5},{5,6},{6,7},{7,4},{8,9},{9,10},{10,1... | collective-permute-start | bytes 3145736 | tf_op jit(solution)/shard_map/ppermute | solution.py:1297
  492.2 49.8 %collective-permute-start.3 = (bf16[256,2048]{1,0:T(8,128)(2,1)}, bf16[256,2048]{1,0:T(8,128)(2,1)}, u32[]{:S(2)}, u32[]{:S(2)}) collective-permute-start(bf16[256,2048]{1,0:T(8,128)(2,1)} %get-tuple-element.131), channel_id=1, source_target_pairs={{0,1},{1,2},{2,3},{3,0},{4,5},{5,6},{6,7},{7,4},{8,9},{9,10},{10,1... | collective-permute-start | bytes 3145736 | tf_op jit(solution)/shard_map/ppermute | solution.py:1295
  542.1 55.2 %copy-start.7 = (bf16[1024,2048]{1,0:T(8,128)(2,1)S(1)}, bf16[1024,2048]{1,0:T(8,128)(2,1)}, u32[]{:S(2)}) copy-start(bf16[1024,2048]{1,0:T(8,128)(2,1)} %copy-done.6) | copy-start | bytes 12582916
  589.8 8.9 %copy-start.12 = (f32[16,1536]{1,0:T(8,128)S(1)}, f32[16,1536]{1,0:T(8,128)}, u32[]{:S(2)}) copy-start(f32[16,1536]{1,0:T(8,128)} %get-tuple-element.142) | copy-start | bytes 294916
  589.8 8.9 %copy-start.25 = (bf16[1024,1664]{1,0:T(8,128)(2,1)S(1)}, bf16[1024,1664]{1,0:T(8,128)(2,1)}, u32[]{:S(2)}) copy-start(bf16[1024,1664]{1,0:T(8,128)(2,1)} %get-tuple-element.141) | copy-start | bytes 10223620
  589.8 8.8 %collective-permute-start.6 = (f32[8,1536]{1,0:T(8,128)}, f32[8,1536]{1,0:T(8,128)S(1)}, u32[]{:S(2)}, u32[]{:S(2)}) collective-permute-start(f32[8,1536]{1,0:T(8,128)} %get-tuple-element.143), channel_id=1, source_target_pairs={{4,0},{8,4},{12,8},{16,12},{20,16},{24,20},{28,24},{5,1},{9,5},{13... | collective-permute-start | bytes 147464 | tf_op jit(solution)/shard_map/ppermute | solution.py:1314
  596.1 26.2 %collective-permute-start.5 = (bf16[256,2048]{1,0:T(8,128)(2,1)S(1)}, bf16[256,2048]{1,0:T(8,128)(2,1)S(1)}, u32[]{:S(2)}, u32[]{:S(2)}) collective-permute-start(bf16[256,2048]{1,0:T(8,128)(2,1)S(1)} %add_convert_fusion.1), channel_id=1, source_target_pairs={{0,1},{1,2},{2,3},{3,0},{4,5},{5,6},{6,7},{7,4},{8,9},{9,10},{10,1... | collective-permute-start | bytes 3145736 | tf_op jit(solution)/shard_map/ppermute | solution.py:1308
  597.2 44.8 %collective-permute-start.7 = (bf16[256,2048]{1,0:T(8,128)(2,1)}, bf16[256,2048]{1,0:T(8,128)(2,1)S(1)}, u32[]{:S(2)}, u32[]{:S(2)}) collective-permute-start(bf16[256,2048]{1,0:T(8,128)(2,1)} %collective-permute-done.3), channel_id=1, source_target_pairs={{0,1},{1,2},{2,3},{3,0},{4,5},{5,6},{6,7},{7,4},{8,9},{9,10},{10,1... | collective-permute-start | bytes 3145736 | tf_op jit(solution)/shard_map/ppermute | solution.py:1307
  598.7 53.6 %copy-start.26 = (bf16[1024,1664]{1,0:T(8,128)(2,1)}, bf16[1024,1664]{1,0:T(8,128)(2,1)S(1)}, u32[]{:S(2)}) copy-start(bf16[1024,1664]{1,0:T(8,128)(2,1)S(1)} %convert_dynamic-update-slice_fusion.refs_0_) | copy-start | bytes 10223620
  622.3 19.8 %copy-start.10 = (bf16[256,2048]{1,0:T(8,128)(2,1)}, bf16[256,2048]{1,0:T(8,128)(2,1)S(1)}, u32[]{:S(2)}) copy-start(bf16[256,2048]{1,0:T(8,128)(2,1)S(1)} %collective-permute-done.5) | copy-start | bytes 3145732
  642.0 23.6 %collective-permute-start.8 = (bf16[256,2048]{1,0:T(8,128)(2,1)S(1)}, bf16[256,2048]{1,0:T(8,128)(2,1)S(1)}, u32[]{:S(2)}, u32[]{:S(2)}) collective-permute-start(bf16[256,2048]{1,0:T(8,128)(2,1)S(1)} %collective-permute-done.7), channel_id=1, source_target_pairs={{0,1},{1,2},{2,3},{3,0},{4,5},{5,6},{6,7},{7,4},{8,9},{9,10},{10,1... | collective-permute-start | bytes 3145736 | tf_op jit(solution)/shard_map/ppermute | solution.py:1319
  652.4 13.4 %copy-start.11 = (bf16[1024,512]{1,0:T(8,128)(2,1)S(1)}, bf16[1024,512]{1,0:T(8,128)(2,1)}, u32[]{:S(2)}) copy-start(bf16[1024,512]{1,0:T(8,128)(2,1)} %get-tuple-element.118) | copy-start | bytes 3145732
  692.1 84.5 %copy-start.15 = (f32[2048]{0:T(1024)S(1)}, f32[2048]{0:T(1024)}, u32[]{:S(2)}) copy-start(f32[2048]{0:T(1024)} %param.28) | copy-start | bytes 24580
  (14 other events, 55.6 us)
Sparse Core Ops, SparseCore 0:
  87.2 81.8 all-gather.2
  318.2 66.5 reduce-scatter.5
  388.8 86.6 reduce-scatter.3
  686.3 85.8 reduce-scatter.7

commit v3 on v2

--- a/solution.py
+++ b/solution.py
@@ -358,8 +358,8 @@
     mains, priors, rims = refs[0:3], refs[3:6], refs[6:9]
     narrow_ref, taps_ref, params_ref, ds_in = refs[9:13]
     (do_ref, v2_ref, s_ref, x_ref, p_ref, kg_ref, w_ref, u_ref, qt_ref, t_ref) = refs[13:23]
-    grads_ref, tail_ref, rim_ref, gtaps_ref, gparams_ref = refs[23:28]
-    run, after = refs[28:30]
+    dgate_ref, grads_ref, tail_ref, rim_ref, gtaps_ref, gparams_ref = refs[23:29]
+    run, after = refs[29:31]
     rev = pl.program_id(0)
     step = chunks - 1 - rev
     position = scalars[0] + step * CHUNK
@@ -453,7 +453,8 @@
     dg = mm_full(upper, gdecay)
     galpha = dg * rate * jax.nn.sigmoid(shifted)
     width = pieces[0].shape[1]
-    grads_ref[:, 3 * width :] = jnp.where(
+    grads_ref[:, 3 * width + 128 :] = dgate_ref[...]
+    grads_ref[:, 3 * width : 3 * width + 128] = jnp.where(
         lane < heads, galpha, gbeta * beta * (1.0 - beta)
     ).astype(LOW)
     gparams_ref[0:8, :] += jnp.sum((galpha).reshape(CHUNK // 8, 8, 128), axis=0)
@@ -494,14 +495,14 @@
             tail_ref[:, i * width : (i + 1) * width] = grad[CHUNK - HALO :]
 
 
-def back(scalars, pieces, rims, narrow, taps, params, ds_in, do, v2, s, x, p, kg, w, u, qt, t, docs, heads):
+def back(scalars, pieces, rims, narrow, taps, params, ds_in, do, v2, s, x, p, kg, w, u, qt, t, dgate, docs, heads):
     rows, width = pieces[0].shape
     chunks = rows // CHUNK
     flat, tiles = rows_spec(width, chunks, True), tile_spec(heads, chunks, True)
     return pl.pallas_call(
         functools.partial(back_kernel, docs, heads, chunks),
         out_shape=(
-            sds(rows, 3 * width + 128, dtype=LOW), sds(HALO, 3 * width), sds(8, 3 * width),
+            sds(rows, 4 * width + 128, dtype=LOW), sds(HALO, 3 * width), sds(8, 3 * width),
             sds(12, 8, width), sds(16, 128),
         ),
         grid_spec=pltpu.PrefetchScalarGridSpec(
@@ -511,8 +512,8 @@
             + [halo_spec(width, chunks, True)] * 3
             + [whole_spec(HALO, width)] * 3
             + [rows_spec(128, chunks, True), whole_spec(16, width), whole_spec(8, 128)]
-            + [whole_spec(heads, 128, 128), flat, flat, tiles, tiles, tiles, tiles, flat, flat, flat, tiles],
-            out_specs=[rows_spec(3 * width + 128, chunks, True)]
+            + [whole_spec(heads, 128, 128), flat, flat, tiles, tiles, tiles, tiles, flat, flat, flat, tiles, flat],
+            out_specs=[rows_spec(4 * width + 128, chunks, True)]
             + [whole_spec(HALO, 3 * width), whole_spec(8, 3 * width)]
             + [whole_spec(12, 8, width), whole_spec(16, 128)],
             scratch_shapes=[pltpu.VMEM((heads, 128, 128), F32), pltpu.VMEM((9, 8, width), F32)],
@@ -520,7 +521,7 @@
         compiler_params=pltpu.CompilerParams(**PARAMS),
         cost_estimate=cost(chunks * heads * 60 * 2 * 128**3, 16 * rows * width * 4),
         name="back",
-    )(scalars, *pieces, *pieces, *rims, narrow, taps, params, ds_in, do, v2, s, x, p, kg, w, u, qt, t)
+    )(scalars, *pieces, *pieces, *rims, narrow, taps, params, ds_in, do, v2, s, x, p, kg, w, u, qt, t, dgate)
 
 
 def contract_rows(left, right):
@@ -736,9 +737,9 @@
 
 def feed_kernel(parts, res_ref, gain_ref, *refs):
     weights_in, og_in = refs[0:3], refs[3]
-    all_ref, act_ref, gu_ref = refs[4:7]
-    buf, weights, og = refs[7], refs[8:11], refs[11]
-    sems, load_sem, store_sem = refs[12:16], refs[16], refs[17]
+    all_ref, act_ref, gu_ref, mlp_ref = refs[4:8]
+    buf, weights, og = refs[8], refs[9:12], refs[12]
+    sems, load_sem, store_sem = refs[13:17], refs[17], refs[18]
     me = lax.axis_index("tensor")
     rows = res_ref.shape[0]
     units = weights_in[0].shape[1]
@@ -784,6 +785,13 @@
         if units % 256:
             tile(at, piece, units - units % 256, units % 256)
 
+        def down(i, _):
+            cols = pl.ds(pl.multiple_of(i * 256, 256), 256)
+            mlp_ref[at, cols] = dot(act_ref[at, :], wd[:, cols]).astype(LOW)
+            return 0
+
+        lax.fori_loop(0, mlp_ref.shape[1] // 256, down, 0)
+
     line_gather(parts, buf, sems, first, use)
     for piece in range(parts):
         stored(piece).wait()
@@ -797,16 +805,17 @@
         functools.partial(feed_kernel, parts),
         out_shape=(
             sds(total, model, dtype=LOW), sds(total, units, dtype=LOW), sds(total, 2 * units, dtype=LOW),
+            sds(total, model, dtype=LOW),
         ),
         in_specs=[vmem()] * 2 + [hbm()] * 4,
-        out_specs=[hbm()] + [vmem()] * 2,
+        out_specs=[hbm()] + [vmem()] * 3,
         scratch_shapes=[pltpu.VMEM((parts, rows, model), LOW)]
         + [pltpu.VMEM(w.shape, LOW) for w in weights]
         + [pltpu.VMEM((total, model), LOW)]
         + line_sems(parts)
         + [pltpu.SemaphoreType.DMA((4,)), pltpu.SemaphoreType.DMA((parts,))],
         compiler_params=comm_params(2),
-        cost_estimate=cost(6 * total * model * units, 120 * 2**20),
+        cost_estimate=cost(8 * total * model * units, 120 * 2**20),
         name="feed",
     )(residual, gain, *weights, out_grad)
 
@@ -977,7 +986,7 @@
     )(*lefts, *rights)
 
 
-def state_kernel(count, heads, backward, own_ref, out_ref, buf, send_sem, pass_sem, got_sem, own_sem):
+def state_kernel(count, heads, backward, own_ref, out_ref, buf, send_sem, pass_sem, got_sem):
     me = lax.axis_index("dp")
     core = lax.rem(me, 2)
     sibling = me + 1 - 2 * core
@@ -993,9 +1002,7 @@
 
     lax.fori_loop(1, half, hello, 0)
     pl.semaphore_signal(barrier, inc=1, device_id={"dp": sibling}, device_id_type=MESH)
-    local = pltpu.make_async_copy(own_ref, buf.at[me], own_sem)
-    local.start()
-    local.wait()
+    buf[me] = own_ref[...].astype(LOW)
     pl.semaphore_wait(barrier, half)
 
     def needed(source, target):
@@ -1053,7 +1060,7 @@
         @pl.when(needed(piece, me))
         def _():
             for h in range(heads):
-                both = buf[piece, h]
+                both = buf[piece, h].astype(F32)
                 if backward:
                     out_ref[h] = mm(both[:, 128:], out_ref[h], TN) + both[:, :128]
                 else:
@@ -1090,9 +1097,8 @@
         out_shape=sds(heads, 128, 128),
         in_specs=[vmem()],
         out_specs=vmem(),
-        scratch_shapes=[pltpu.VMEM((count, heads, 128, 256), F32)]
-        + [pltpu.SemaphoreType.DMA((count,))] * 3
-        + [pltpu.SemaphoreType.DMA],
+        scratch_shapes=[pltpu.VMEM((count, heads, 128, 256), LOW)]
+        + [pltpu.SemaphoreType.DMA((count,))] * 3,
         compiler_params=comm_params(number),
         cost_estimate=cost(count * heads * 6 * 128**3, count * heads * 256 * 128 * 4),
         name="exchange%d" % number,
@@ -1257,7 +1263,7 @@
 
     mixed_own = lax.all_to_all(mixed, "tensor", split_axis=0, concat_axis=1, tiled=True)
     residual = own_rows + dot(mixed_own, w_out_full)
-    mid_all, activated, grad_units = feed(
+    mid_all, activated, grad_units, mlp_part = feed(
         tensor_parts, residual, gain_mid_rows, (w_gate, w_up, w_down), out_grad
     )
     units = w_gate.shape[1]
@@ -1270,16 +1276,15 @@
     def added(values, back_by, got):
         return (piece_of(values, back_by).astype(F32) + got.astype(F32)).astype(LOW)
 
-    mlp_part = dot(activated, w_down).astype(LOW)
     mlp_run = lax.ppermute(piece_of(mlp_part, 1), "tensor", ring)
-    out_grad_2, activated_2, mlp_part = lax.optimization_barrier((out_grad, activated, mlp_part))
-    down_grad = contract_rows(out_grad_2, activated_2).astype(LOW)
+    down_grad = contract_rows(out_grad, activated).astype(LOW)
     units_grad = contract_rows(mid_all, after(grad_units, down_grad)).astype(LOW)
+    units_grad, mlp_run = lax.optimization_barrier((units_grad, mlp_run))
     down_grad_sum = lax.psum_scatter(down_grad, "dp", scatter_dimension=0, tiled=True)
     units_grad_sum = lax.psum_scatter(units_grad, "dp", scatter_dimension=0, tiled=True)
 
     grad_mid = scatter(
-        tensor_parts, [after(grad_units, units_grad, mlp_run)], [w_gate, w_up],
+        tensor_parts, [after(grad_units, units_grad)], [w_gate, w_up],
         ((0, 0, units), (0, units, units)), 4,
     )
     grad_res_norm, gain_mid_grad = norm_back(residual, gain_mid, grad_mid)
@@ -1290,9 +1295,8 @@
     grad_mixed = lax.all_to_all(
         grad_mixed_own, "tensor", split_axis=1, concat_axis=0, tiled=True
     )
-    mixer_pieces = [grad_mixer]
-    grad_mixer_1, mlp_run = lax.optimization_barrier((grad_mixer, mlp_run, grad_mixed))[:2]
-    mixer_pieces.append(lax.ppermute(grad_mixer_1, "tensor", ring))
+    grad_mixer_all, mlp_run = lax.optimization_barrier((grad_mixer, mlp_run, grad_mixed))[:2]
+    grad_mixer_all = lax.all_gather(grad_mixer_all, "tensor", axis=0, tiled=True)
     for back_by in range(2, tensor_parts - 1):
         mlp_run = lax.ppermute(added(mlp_part, back_by, mlp_run), "tensor", ring)
 
@@ -1300,39 +1304,29 @@
         grad_mixed, rows_out, gate_raw, gain_heads, qt, t, totals, heads
     )
     grad_end = exchange(dp_parts, ds_total, heads, True, 5)
-    grad_end, piece_1, mlp_run, _, _ = lax.optimization_barrier(
-        (grad_end, mixer_pieces[1], mlp_run, units_grad_sum, down_grad_sum)
-    )
-    mixer_pieces[1] = piece_1
-    mixer_pieces.append(lax.ppermute(piece_1, "tensor", ring))
-    mlp_run = lax.ppermute(added(mlp_part, tensor_parts - 1, mlp_run), "tensor", ring)
-    output = (residual + (piece_of(mlp_part, 0).astype(F32) + mlp_run.astype(F32))).astype(LOW)
+    grad_end, mlp_run, _, _ = lax.optimization_barrier(
+        (grad_end, mlp_run, units_grad_sum, down_grad_sum)
+    )
     grads, tails, rim_grad, taps_grad, params_grad = back(
         scalars, pieces, rims, narrow, taps, params, grad_end, do, v2, s, x, p, kg, w, u, qt, t,
-        docs, heads,
+        gate_low, docs, heads,
     )
     rim_back = lax.ppermute(rim_grad, "dp", [(i + 1, i) for i in range(dp_parts - 1)])
     tails = tails.at[HALO - 8 :].add(rim_back).astype(LOW)
     grads = lax.dynamic_update_slice(grads, tails, (group_rows - HALO, 0))
-    grads, piece_last, _ = lax.optimization_barrier((grads, mixer_pieces[-1], mlp_run))
-    for _ in range(3, tensor_parts):
-        piece_last = lax.ppermute(piece_last, "tensor", ring)
-        mixer_pieces.append(piece_last)
-    grads_w = contract_rows(normed_all, grads).astype(LOW)
-    gate_w = contract_rows(normed_all, gate_low).astype(LOW)
-    grad_mixer_all = jnp.zeros((group_rows, model), LOW)
-    for back_by, piece in enumerate(mixer_pieces):
-        index = lax.rem(tensor_index - back_by + tensor_parts, tensor_parts)
-        grad_mixer_all = lax.dynamic_update_slice_in_dim(
-            grad_mixer_all, piece, index * rows_own, 0
-        )
-    out_w = contract_rows(after(grad_mixer_all, grads_w, gate_w), mixed).astype(LOW)
-    mixer_grad = jnp.concatenate([grads_w, gate_w, out_w], axis=1)
+    mlp_run = lax.ppermute(
+        added(mlp_part, tensor_parts - 1, after(mlp_run, rim_grad)), "tensor", ring
+    )
+    out_w = contract_rows(after(grad_mixer_all, rim_grad), mixed).astype(LOW)
+    out_w_sum = lax.psum_scatter(out_w, "dp", scatter_dimension=0, tiled=True).astype(F32)
+    mixer_grad = contract_rows(normed_all, after(grads, out_w)).astype(LOW)
+    mixer_grad, mlp_run = lax.optimization_barrier((mixer_grad, mlp_run))
     mixer_sum = lax.psum_scatter(mixer_grad, "dp", scatter_dimension=0, tiled=True).astype(F32)
+    output = (residual + (piece_of(mlp_part, 0).astype(F32) + mlp_run.astype(F32))).astype(LOW)
     grad_normed = scatter(
-        tensor_parts, [after(grads, mixer_grad), gate_low],
+        tensor_parts, [after(grads, mixer_grad)],
         [w_query, w_key, w_value, w_narrow, w_gate_out],
-        ((0, 0, width), (0, width, width), (0, 2 * width, width), (0, 3 * width, 128), (1, 0, width)),
+        ((0, 0, width), (0, width, width), (0, 2 * width, width), (0, 3 * width, 128), (0, 3 * width + 128, width)),
         6,
     )
     grad_tokens, gain_in_grad = norm_back(own_rows, gain_in, grad_normed)
@@ -1362,14 +1356,14 @@
         mixer_sum[:, 2 * width : start],
         mixer_sum[:, start : start + heads],
         mixer_sum[:, start + heads : start + 2 * heads],
-        mixer_sum[:, start + 128 : start + 128 + width],
+        mixer_sum[:, start + 128 :],
         wide[0:4],
         wide[4:8],
         wide[8:12],
         by_head[1],
         by_head[0],
         wide[12],
-        mixer_sum[:, start + 128 + width :].T,
+        out_w_sum.T,
         gains[1],
         units_grad_sum[:, :units].astype(F32),
         units_grad_sum[:, units:].astype(F32),

time: 840 us -> 740 us (0.88)
  waiting for transfers between devices: 121 us -> 63.8 us
  Pallas kernels: 503 us -> 477 us
  blocking collectives: 0 us -> 23.9 us
  other arithmetic: 58.1 us -> 42.3 us
  local copies, waits for them, and re-layouts: 40 us -> 27.5 us
  starting transfers between devices: 25.2 us -> 15.8 us
    ppermute x4 -> x1, waiting for transfers between devices: 56.4 us -> 8.34 us  [local(): lax.ppermute(added(mlp_part, tensor_parts - 1, after(mlp_run, rim_grad)),...]
    all_to_all x0 -> x1, blocking collectives: none -> 23.9 us  [local(): lax.all_to_all(grad_mixed_own, 'tensor', split_axis=1, concat_axis=0, til...]
    pallas_call x2, Pallas kernels: 56.8 us -> 33.6 us  [exchange(): pl.pallas_call(functools.partial(state_kernel, count, heads, backward), o...]
    all_to_all x1 -> x0, waiting for transfers between devices: 19.1 us -> none  [local(): lax.all_to_all(grad_mixed_own, 'tensor', split_axis=1, concat_axis=0, til...]
    concatenate x1 -> x0, other arithmetic: 17.9 us -> none  [local(): mixer_grad = jnp.concatenate([grads_w, gate_w, out_w], axis=1)]
    ppermute x1, waiting for transfers between devices: 28.4 us -> 13.2 us  [local(): mlp_run = lax.ppermute(piece_of(mlp_part, 1), 'tensor', ring)]
    all_gather x1, waiting for transfers between devices: 5.06 us -> 16.6 us  [local(): out_mine = lax.all_gather(out_half, 'tensor', axis=0)]
    dot_general x2 -> x1, matrix products: 18.2 us -> 7.06 us  [dot(): return jnp.dot(left, right, preferred_element_type=F32)]
  transfers between devices with their start and end apart: 15 -> 13, of which waited for: 8 -> 7; matrix products, arithmetic and copies ran while one was open for 12% -> 14% of each run, Pallas kernels for 37% -> 44%
where the time goes in v3:
time: 740 us; the launch traced here: 729 us
  Pallas kernels  477 us (64%)
  matrix products  64 us (9%)
  waiting for transfers between devices  63.8 us (9%)
  other arithmetic  42.3 us (6%)
  local copies, waits for them, and re-layouts  27.5 us (4%)
  blocking collectives  23.9 us (3%)
  starting transfers between devices  15.8 us (2%)
  between operations  15 us (2%)
    pallas_call x2, Pallas kernels, scatter(): pl.pallas_call(kernel, out_shape=sds(rows, model), in_specs=[vmem()] * le...  166 us
    pallas_call x1, Pallas kernels, feed(): pl.pallas_call(functools.partial(feed_kernel, parts), out_shape=(sds(tota...  78.4 us
    pallas_call x1, Pallas kernels, project(): pl.pallas_call(functools.partial(project_kernel, parts), out_shape=(sds(t...  75.1 us
    dot_general x4, matrix products, contract_rows(): return lax.dot_general(left, right, TN, preferred_element_type=F32)  50.8 us
    pallas_call x1, Pallas kernels, back(): pl.pallas_call(functools.partial(back_kernel, docs, heads, chunks), out_s...  47.3 us
    pallas_call x1, Pallas kernels, intra(): pl.pallas_call(functools.partial(intra_kernel, docs, heads), out_shape=(t...  41 us
    pallas_call x2, Pallas kernels, exchange(): pl.pallas_call(functools.partial(state_kernel, count, heads, backward), o...  33.6 us
    all_to_all x1, blocking collectives, local(): lax.all_to_all(grad_mixed_own, 'tensor', split_axis=1, concat_axis=0, til...  23.9 us
  transfers between devices with their start and end apart: 13, of which 7 were waited for; matrix products, arithmetic and copies ran while one was open for 14% of the time, Pallas kernels for 44%

profile of v3, /device:TPU:12, one launch (start us, length us, event | category | flops | bytes accessed | tf_op | source)
XLA Modules:
  0.0 729.2 jit_solution(17739980156590174912)
XLA Ops:
  10.7 75.1 %project.1 = (bf16[1024,2048]{1,0:T(8,128)(2,1)}, bf16[1024,512]{1,0:T(8,128)(2,1)}, bf16[1024,512]{1,0:T(8,128)(2,1)}, bf16[1024,512]{1,0:T(8,128)(2,1)}, f32[1024,512]{1,0:T(8,128)}, /*index=5*/f32[1024,128]{1,0:T(8,128)}) custom-call(bf16[256,2048]{1,0:T(8,128)(2,1)} %tok_ref.1, f32[8,2048]{1,0:T(8,128)} %broadcast_in_dim.10.gain_ref, ...), custom_call_target="tpu_custom_call" | custom-call | flops 9126805504 | bytes 62914560 | tf_op jit(solution)/shard_map/project/pallas_call | solution.py:723
  95.4 41.0 %intra.1 = (f32[8,4,128,128]{3,2,1,0:T(8,128)}, f32[8,4,128,128]{3,2,1,0:T(8,128)}, f32[8,4,128,128]{3,2,1,0:T(8,128)}, f32[1024,512]{1,0:T(8,128)}, f32[1024,51...) custom-call(s32[5]{0:T(128)} %pad_add_fusion.scalars, ...), custom_call_target="tpu_custom_call" | custom-call | flops 24159191040 | bytes 62914560 | tf_op jit(solution)/shard_map/intra/pallas_call | solution.py:238
  136.4 16.0 %exchange3.1.s_in = f32[4,128,128]{2,1,0:T(8,128)} custom-call(f32[4,128,256]{2,1,0:T(8,128)} %get-tuple-element.111.own_ref.maps_ref), custom_call_target="tpu_custom_call" | custom-call | flops 402653184 | bytes 4194304 | tf_op jit(solution)/shard_map/exchange3/pallas_call | solution.py:1095
  152.4 16.6 %all-gather.6.cloned.1.call-done = bf16[1024,2048]{1,0:T(8,128)(2,1)} async-done(((bf16[256,2048]{1,0:T(8,128)(2,1)}), bf16[1024,2048]{1,0:T(8,128)(2,1)}) %all-gather.6.cloned.1.call-update) | async-done | bytes 4194320 | tf_op jit(solution)/shard_map/all_gather | solution.py:1247
  169.6 11.5 %outward.1 = (f32[1024,512]{1,0:T(8,128)}, f32[1024,512]{1,0:T(8,128)}, f32[8,4,128,128]{3,2,1,0:T(8,128)}, bf16[1024,512]{1,0:T(8,128)(2,1)}) custom-call(f32[4,128,128]{2,1,0:T(8,128)} %exchange3.1.s_in, f32[1024,512]{1,0:T(8,128)} %get-tuple-element.112.w_ref.refs_19_, f32[1024,512]{1,0:T(8,128)} %get-tuple-element.113.u_ref.refs_20_, ...), custom_call_target="tpu_custom_call" | custom-call | flops 1207959552 | bytes 23068672 | tf_op jit(solution)/shard_map/outward/pallas_call | solution.py:294
  183.4 6.5 all-to-all-start
  190.4 5.8 select_bitcast_fusion.1
  196.2 7.5 %pad_maximum_fusion = bf16[4,2,256,2048]{3,2,1,0:T(8,128)(2,1)} fusion(bf16[4,1,256,2048]{3,2,1,0:T(8,128)(2,1)} %get-tuple-element.223, bf16[4,1,256,2048]{3,2,1,0:T(8,128)(2,1)} %get-tuple-element.222), kind=kLoop, calls=%fused_computation.2 | loop fusion | flops 4194304 | bytes 16777216 | tf_op jit(solution)/shard_map/stack | solution.py:1258
  203.8 9.5 %all-to-all-done = bf16[4,256,512]{1,2,0:T(8,128)(2,1)S(1)} async-done(((bf16[4,256,512]{1,2,0:T(8,128)(2,1)}), bf16[4,256,512]{1,2,0:T(8,128)(2,1)S(1)}, u32[]{:S(2)}, u32[]{:S(2)}) %all-to-all-start) | async-done | bytes 1048608 | tf_op jit(solution)/shard_map/all_to_all | solution.py:1264
  213.3 7.1 multiply_reduce_fusion.2
  221.0 78.4 %feed.1 = (bf16[1024,2048]{1,0:T(8,128)(2,1)}, bf16[1024,1408]{1,0:T(8,128)(2,1)}, bf16[1024,2816]{1,0:T(8,128)(2,1)}, bf16[1024,2048]{1,0:T(8,128)(2,1)}) custom-call(f32[256,2048]{1,0:T(8,128)} %get-tuple-element.245.res_ref, f32[8,2048]{1,0:T(8,128)} %broadcast_in_dim.13.gain_ref, bf16[2048,1408]{1,0:T(8,128)(2,1)} %refs_1_.6, ...), custom_call_target="tpu_custom_call" | custom-call | flops 23622320128 | bytes 125829120 | tf_op jit(solution)/shard_map/feed/pallas_call | solution.py:804
  299.4 10.5 %fusion = bf16[2048,1408]{0,1:T(8,128)(2,1)} fusion(bf16[1024,1408]{1,0:T(8,128)(2,1)} %get-tuple-element.126, bf16[1024,2048]{1,0:T(8,128)(2,1)} %refs_3_.4), kind=kOutput, calls=%fused_computation.4 | convolution fusion | flops 5908463616 | bytes 12845056 | tf_op jit(solution)/shard_map/dot_general | solution.py:528
  312.5 18.6 %convolution_convert_fusion.1 = bf16[2048,2816]{1,0:T(8,128)(2,1)} fusion(bf16[1024,2048]{1,0:T(8,128)(2,1)} %get-tuple-element.125, bf16[1024,2816]{1,0:T(8,128)(2,1)} %get-tuple-element.129.refs_0_), kind=kOutput, calls=%fused_computation.1 | convolution fusion | flops 11816927232 | bytes 21495808 | tf_op jit(solution)/shard_map/dot_general | solution.py:528
  331.1 13.2 %collective-permute-done.2 = bf16[256,2048]{1,0:T(8,128)(2,1)S(1)} collective-permute-done((bf16[256,2048]{1,0:T(8,128)(2,1)S(1)}, bf16[256,2048]{1,0:T(8,128)(2,1)S(1)}, u32[]{:S(2)}, u32[]{:S(2)}) %collective-permute-start.2) | collective-permute-done | bytes 1048608 | tf_op jit(solution)/shard_map/ppermute | solution.py:1279
  345.3 82.7 %scatter4.1 = f32[256,2048]{1,0:T(8,128)} custom-call(bf16[1024,2816]{1,0:T(8,128)(2,1)} %get-tuple-element.129.refs_0_, bf16[2048,1408]{1,0:T(8,128)(2,1)} %refs_1_.6, bf16[2048,1408]{1,0:T(8,128)(2,1)} %refs_2_.6), custom_call_target="tpu_custom_call" | custom-call | flops 11811160064 | bytes 62914560 | tf_op jit(solution)/shard_map/scatter4/pallas_call | solution.py:973
  430.2 2.9 fusion.7
  433.2 6.2 convolution_convert_fusion.4
  439.5 23.9 %all_to_all.38 = bf16[256,4,512]{2,0,1:T(8,128)(2,1)} all-to-all(bf16[256,4,512]{2,0,1:T(8,128)(2,1)S(1)} %bitcast.70), channel_id=1, replica_groups=mesh['dp'=8,'tensor'=4] {'tensor'}, dimensions={1} | all-to-all | bytes 2097152 | tf_op jit(solution)/shard_map/all_to_all | solution.py:1295
  467.0 10.4 %inward.1 = (f32[1024,512]{1,0:T(8,128)}, bf16[1024,512]{1,0:T(8,128)(2,1)}, f32[8,512]{1,0:T(8,128)}, f32[4,128,256]{2,1,0:T(8,128)}) custom-call(bf16[1024,512]{1,0:T(8,128)(2,1)} %bitcast.69, f32[1024,512]{1,0:T(8,128)} %get-tuple-element.130.out_ref, f32[1024,512]{1,0:T(8,128)} %get-tuple-element.118.gate_ref, f32[8,512]{1,0:T(8,128)} %broadcast_in_dim.12.gain_ref, ...), custom_call_target="tpu_custom_call" | custom-call | flops 805306368 | bytes 14680064 | tf_op jit(solution)/shard_map/inward/pallas_call | solution.py:344
  477.4 17.6 %exchange5.1.refs_12_ = f32[4,128,128]{2,1,0:T(8,128)} custom-call(f32[4,128,256]{2,1,0:T(8,128)} %get-tuple-element.131.own_ref), custom_call_target="tpu_custom_call" | custom-call | flops 402653184 | bytes 4194304 | tf_op jit(solution)/shard_map/exchange5/pallas_call | solution.py:1095
  495.0 9.9 %collective-permute-done.3 = bf16[256,2048]{1,0:T(8,128)(2,1)} collective-permute-done((bf16[256,2048]{1,0:T(8,128)(2,1)}, bf16[256,2048]{1,0:T(8,128)(2,1)}, u32[]{:S(2)}, u32[]{:S(2)}) %collective-permute-start.3) | collective-permute-done | bytes 1048608 | tf_op jit(solution)/shard_map/ppermute | solution.py:1301
  504.9 47.3 %back.1 = (bf16[1024,2176]{1,0:T(8,128)(2,1)}, f32[16,1536]{1,0:T(8,128)}, f32[8,1536]{1,0:T(8,128)}, f32[12,8,512]{2,1,0:T(8,128)}, f32[16,128]{1,0:T(8,128)}) custom-call(s32[5]{0:T(128)} %pad_add_fusion.scalars, bf16[1024,512]{1,0:T(8,128)(2,1)} %get-tuple-element.107.refs_0_.refs_3_, bf16[1024,512]{1,0:T(8,128)(2,1)} %get-tuple-element.108.refs_1_.refs_4_, ...), custom_call_target="tpu_custom_call" | custom-call | flops 8053063680 | bytes 33554432 | tf_op jit(solution)/shard_map/back/pallas_call | solution.py:502
  554.1 3.5 all-gather.4.cloned.1.call-done
  557.7 6.2 convolution_convert_fusion.3
  563.9 2.9 add_convert_fusion.1
  566.9 3.0 collective-permute-start.5
  570.5 15.5 %convolution_convert_fusion = bf16[2048,2176]{1,0:T(8,128)(2,1)} fusion(bf16[1024,2048]{1,0:T(8,128)(2,1)} %get-tuple-element.123, bf16[1024,2176]{1,0:T(8,128)(2,1)} %convert_dynamic-update-slice_fusion.refs_0_), kind=kOutput, calls=%fused_computation | convolution fusion | flops 9131261952 | bytes 17563648 | tf_op jit(solution)/shard_map/dot_general | solution.py:528
  585.9 8.3 %collective-permute-done.5 = bf16[256,2048]{1,0:T(8,128)(2,1)} collective-permute-done((bf16[256,2048]{1,0:T(8,128)(2,1)}, bf16[256,2048]{1,0:T(8,128)(2,1)}, u32[]{:S(2)}, u32[]{:S(2)}) %collective-permute-start.5) | collective-permute-done | bytes 1048608 | tf_op jit(solution)/shard_map/ppermute | solution.py:1317
  597.1 82.9 %scatter6.1 = f32[256,2048]{1,0:T(8,128)} custom-call(bf16[1024,2176]{1,0:T(8,128)(2,1)} %convert_dynamic-update-slice_fusion.refs_0_, bf16[2048,512]{1,0:T(8,128)(2,1)} %refs_1_.7, bf16[2048,512]{1,0:T(8,128)(2,1)} %refs_2_.7, bf16[2048,512]{1,0:T(8,128)(2,1)} %refs_3_.5, bf16[2048,128]{1,0:T(8,128)(2,1)} %pad.18.narrow_w.refs_4_, bf16[2048,512]{1,0:T(8,128)(2,1)} %refs_5_.1), custom_call_target="tpu_custom_call" | custom-call | flops 9126805504 | bytes 62914560 | tf_op jit(solution)/shard_map/scatter6/pallas_call | solution.py:973
  684.8 3.1 slice_convert_fusion
  687.9 14.0 %totals.1 = (f32[16,2048]{1,0:T(8,128)}, f32[8,512]{1,0:T(8,128)}) custom-call(f32[24,512]{1,0:T(8,128)} %concatenate.21.own_ref), custom_call_target="tpu_custom_call" | custom-call | flops 98304 | bytes 393216 | tf_op jit(solution)/shard_map/totals/pallas_call | solution.py:1177
  709.1 5.8 fusion.4
  (120 shorter events, 50.7 us)
Async XLA Ops:
  7.2 78.7 %copy-start = (bf16[512,2048]{1,0:T(8,128)(2,1)S(1)}, bf16[512,2048]{1,0:T(8,128)(2,1)}, u32[]{:S(2)}) copy-start(bf16[512,2048]{1,0:T(8,128)(2,1)} %param.41) | copy-start | bytes 6291460
  7.2 161.8 %all-gather.6.cloned.1.call-start = ((), (), s32[]{:S(2)}) async-start(), calls=%async_computation.11 | async-start | bytes 5242880 | tf_op jit(solution)/shard_map/all_gather | solution.py:1247
  85.8 4.6 copy-start.19
  85.8 4.9 copy-start.11
  85.8 4.8 copy-start.12
  85.8 4.8 copy-start.13
  85.8 6.1 copy-start.17
  85.9 6.1 copy-start.18
  88.5 6.3 collective-permute-start
  92.2 3.2 copy-start.15
  95.4 73.6 %copy-start.16 = (f32[512]{0:T(512)S(1)}, f32[512]{0:T(512)}, u32[]{:S(2)}) copy-start(f32[512]{0:T(512)} %param.40) | copy-start | bytes 6148
  169.0 21.4 %collective-permute-start.1 = (bf16[4,256,2048]{2,1,0:T(8,128)(2,1)}, bf16[4,256,2048]{2,1,0:T(8,128)(2,1)}, u32[]{:S(2)}, u32[]{:S(2)}) collective-permute-start(bf16[4,256,2048]{2,1,0:T(8,128)(2,1)} %bitcast.67), channel_id=1, source_target_pairs={{0,4},{4,0},{8,12},{12,8},{16,20},{20,16},{24,28},{28,24},{1,5},{5... | collective-permute-start | bytes 12582920 | tf_op jit(solution)/shard_map/ppermute | solution.py:1257
  183.4 29.9 %all-to-all-start = ((bf16[4,256,512]{1,2,0:T(8,128)(2,1)}), bf16[4,256,512]{1,2,0:T(8,128)(2,1)S(1)}, u32[]{:S(2)}, u32[]{:S(2)}) async-start(bf16[4,256,512]{1,2,0:T(8,128)(2,1)} %copy.56), calls=%async_computation | async-start | bytes 2097152 | tf_op jit(solution)/shard_map/all_to_all | solution.py:1264
  189.9 315.0 %reduce-scatter.7.cloned.1.call-start = ((), (), s32[]{:S(2)}) async-start(), calls=%async_computation.7 | async-start | bytes 6488064 | tf_op jit(solution)/shard_map/reduce_scatter | solution.py:1283
  196.2 17.1 %copy-start.4 = (bf16[256,2048]{1,0:T(8,128)(2,1)S(1)}, bf16[256,2048]{1,0:T(8,128)(2,1)}, u32[]{:S(2)}) copy-start(bf16[256,2048]{1,0:T(8,128)(2,1)} %tok_ref.1) | copy-start | bytes 3145732
  213.3 7.1 copy-start.8
  309.9 195.0 %reduce-scatter.5.cloned.1.call-start = ((), (), s32[]{:S(2)}) async-start(), calls=%async_computation.6 | async-start | bytes 12976128 | tf_op jit(solution)/shard_map/reduce_scatter | solution.py:1284
  311.3 32.9 %collective-permute-start.2 = (bf16[256,2048]{1,0:T(8,128)(2,1)S(1)}, bf16[256,2048]{1,0:T(8,128)(2,1)S(1)}, u32[]{:S(2)}, u32[]{:S(2)}) collective-permute-start(bf16[256,2048]{1,0:T(8,128)(2,1)S(1)} %constant_dynamic-slice_fusion), channel_id=1, source_target_pairs={{0,1},{1,2},{2,3},{3,0},{4,5},{5,6},{6,7},{7,4},{8,9},{9,10},{10,1... | collective-permute-start | bytes 3145736 | tf_op jit(solution)/shard_map/ppermute | solution.py:1279
  345.2 212.4 %all-gather.4.cloned.1.call-start = ((), (), s32[]{:S(2)}) async-start(), calls=%async_computation.8 | async-start | bytes 5242880 | tf_op jit(solution)/shard_map/all_gather | solution.py:1299
  345.2 82.7 %copy-start.2 = (f32[256,2048]{1,0:T(8,128)S(1)}, f32[256,2048]{1,0:T(8,128)}, u32[]{:S(2)}) copy-start(f32[256,2048]{1,0:T(8,128)} %get-tuple-element.245.res_ref) | copy-start | bytes 6291460
  427.9 2.3 copy-start.3
  463.4 251.5 %reduce-scatter.11.cloned.1.call-start = ((), (), s32[]{:S(2)}) async-start(), calls=%async_computation.10 | async-start | bytes 2359296 | tf_op jit(solution)/shard_map/reduce_scatter | solution.py:1321
  466.4 38.5 %collective-permute-start.3 = (bf16[256,2048]{1,0:T(8,128)(2,1)}, bf16[256,2048]{1,0:T(8,128)(2,1)}, u32[]{:S(2)}, u32[]{:S(2)}) collective-permute-start(bf16[256,2048]{1,0:T(8,128)(2,1)} %add_convert_fusion.2), channel_id=1, source_target_pairs={{0,1},{1,2},{2,3},{3,0},{4,5},{5,6},{6,7},{7,4},{8,9},{9,10},{10,1... | collective-permute-start | bytes 3145736 | tf_op jit(solution)/shard_map/ppermute | solution.py:1301
  552.2 17.6 %collective-permute-start.4 = (f32[8,1536]{1,0:T(8,128)}, f32[8,1536]{1,0:T(8,128)S(1)}, u32[]{:S(2)}, u32[]{:S(2)}) collective-permute-start(f32[8,1536]{1,0:T(8,128)} %get-tuple-element.144), channel_id=1, source_target_pairs={{4,0},{8,4},{12,8},{16,12},{20,16},{24,20},{28,24},{5,1},{9,5},{13... | collective-permute-start | bytes 147464 | tf_op jit(solution)/shard_map/ppermute | solution.py:1314
  563.9 5.9 copy-start.6
  563.9 153.0 %reduce-scatter.9.cloned.1.call-start = ((), (), s32[]{:S(2)}) async-start(), calls=%async_computation.9 | async-start | bytes 10027008 | tf_op jit(solution)/shard_map/reduce_scatter | solution.py:1324
  566.9 27.4 %collective-permute-start.5 = (bf16[256,2048]{1,0:T(8,128)(2,1)}, bf16[256,2048]{1,0:T(8,128)(2,1)}, u32[]{:S(2)}, u32[]{:S(2)}) collective-permute-start(bf16[256,2048]{1,0:T(8,128)(2,1)} %add_convert_fusion.1), channel_id=1, source_target_pairs={{0,1},{1,2},{2,3},{3,0},{4,5},{5,6},{6,7},{7,4},{8,9},{9,10},{10,1... | collective-permute-start | bytes 3145736 | tf_op jit(solution)/shard_map/ppermute | solution.py:1317
  585.9 8.7 %copy-start.10 = (f32[8,512]{1,0:T(8,128)S(1)}, f32[8,512]{1,0:T(8,128)}, u32[]{:S(2)}) copy-start(f32[8,512]{1,0:T(8,128)} %get-tuple-element.154) | copy-start | bytes 49156
  594.3 2.7 copy-start.14
  594.3 2.7 copy-start.7
  597.1 82.9 %copy-start.9 = (f32[2048]{0:T(1024)S(1)}, f32[2048]{0:T(1024)}, u32[]{:S(2)}) copy-start(f32[2048]{0:T(1024)} %param.28) | copy-start | bytes 24580
  718.6 3.3 copy-start.1
  (1 other events, 1.0 us)
Sparse Core Ops, SparseCore 0:
  87.1 81.8 all-gather.5
  310.1 69.7 reduce-scatter.6
  383.7 86.7 reduce-scatter.4
  472.6 85.0 all-gather.3
  564.0 42.4 reduce-scatter.10
  609.9 73.7 reduce-scatter.8

commit v4 on v3

--- a/solution.py
+++ b/solution.py
@@ -22,6 +22,27 @@
     return lax.dot_general(
         left, right, dims, precision=lax.Precision.HIGH, preferred_element_type=F32
     )
+
+
+def halves(values):
+    high = values.astype(LOW)
+    return high, (values - high.astype(F32)).astype(LOW)
+
+
+def mm_split(left, right):
+    (lh, ll), (rh, rl) = left, right
+    return lax.dot_general(
+        jnp.concatenate([lh, ll, lh], axis=1),
+        jnp.concatenate([rh, rh, rl], axis=0),
+        NN,
+        preferred_element_type=F32,
+    )
+
+
+def mm_sum(left, right):
+    (lh, ll), (rh, rl) = left, right
+    one = functools.partial(lax.dot_general, dimension_numbers=NN, preferred_element_type=F32)
+    return one(lh, rh) + (one(ll, rh) + one(lh, rl))
 
 
 def mm_full(left, right, dims=NN):
@@ -304,7 +325,7 @@
     )(s_in, w, u, qt, ou, t, o, gate, gain)
 
 
-def inward_kernel(heads, gm_ref, out_ref, gate_ref, gain_ref, qt_ref, t_ref, maps_ref,
+def inward_kernel(heads, scalars, gm_ref, out_ref, gate_ref, gain_ref, qt_ref, t_ref, maps_ref,
                   do_ref, dgate_ref, dgain_ref, tot_ref, run):
     step = pl.program_id(0)
 
@@ -315,9 +336,13 @@
 
     hs = range(heads)
     grads = []
+    core = scalars[scalars.shape[0] - 1]
     for h in hs:
         out, gate = out_ref[:, lanes(h)], gate_ref[:, lanes(h)]
-        gm = gm_ref[:, lanes(h)].astype(F32)
+        other = (h + heads // 2) % heads
+        gm = jnp.where(
+            core == 0, gm_ref[:, lanes(h)].astype(F32), gm_ref[:, lanes(other)].astype(F32)
+        )
         gain = gain_ref[0:1, lanes(h)]
         scale = lax.rsqrt(jnp.mean(out * out, axis=-1, keepdims=True) + epsilon)
         normed = out * scale
@@ -337,21 +362,24 @@
         tot_ref[h] = jnp.concatenate([new, maps_ref[h, :, 128:]], axis=1)
 
 
-def inward(gm, out, gate, gain, qt, t, maps, heads):
+def inward(scalars, gm, out, gate, gain, qt, t, maps, heads):
     rows, width = gm.shape
     chunks = rows // CHUNK
     flat, tiles = rows_spec(width, chunks, True), tile_spec(heads, chunks, True)
     return pl.pallas_call(
         functools.partial(inward_kernel, heads),
         out_shape=(sds(rows, width), sds(rows, width, dtype=LOW), sds(8, width), sds(heads, 128, 256)),
-        grid=(chunks,),
-        in_specs=[flat, flat, flat, whole_spec(8, width), flat, tiles, whole_spec(heads, 128, 256)],
-        out_specs=[flat, flat, whole_spec(8, width), whole_spec(heads, 128, 256)],
-        scratch_shapes=[pltpu.VMEM((heads, 128, 128), F32)],
+        grid_spec=pltpu.PrefetchScalarGridSpec(
+            num_scalar_prefetch=1,
+            grid=(chunks,),
+            in_specs=[flat, flat, flat, whole_spec(8, width), flat, tiles, whole_spec(heads, 128, 256)],
+            out_specs=[flat, flat, whole_spec(8, width), whole_spec(heads, 128, 256)],
+            scratch_shapes=[pltpu.VMEM((heads, 128, 128), F32)],
+        ),
         compiler_params=pltpu.CompilerParams(**PARAMS),
         cost_estimate=cost(chunks * heads * 6 * 2 * 128**3, 7 * rows * width * 4),
         name="inward",
-    )(gm, out, gate, gain, qt, t, maps)
+    )(scalars, gm, out, gate, gain, qt, t, maps)
 
 
 def back_kernel(docs, heads, chunks, scalars, *refs):
@@ -823,11 +851,169 @@
 SUBS = 2
 
 
-def scatter_kernel(parts, given, count, splits, *refs):
-    lefts, rights_in, out_ref = refs[0:given], refs[given : given + count], refs[given + count]
-    refs = refs[given + count + 1 :]
+class Plain:
+    inputs, outputs = 0, 1
+
+    def __init__(self, parts):
+        self.parts = parts
+
+    def begin(self, given, scratch):
+        greet("tensor", self.parts)
+
+    def end(self, given, out, scratch):
+        pass
+
+    def shapes(self, rows, model):
+        return (sds(rows, model),)
+
+    def scratch(self, rows, model):
+        return []
+
+
+def each(total, me, action):
+    def body(k, _):
+        action(lax.rem(me + k, total))
+        return 0
+
+    lax.fori_loop(1, total, body, 0)
+
+
+class Exchange:
+    def __init__(self, axis, total, buf, send_sem, got_sem):
+        self.axis, self.total = axis, total
+        self.buf, self.send_sem, self.got_sem = buf, send_sem, got_sem
+
+    def copy(self, source, target):
+        return pltpu.make_async_remote_copy(
+            src_ref=self.buf.at[source],
+            dst_ref=self.buf.at[source],
+            send_sem=self.send_sem.at[target],
+            recv_sem=self.got_sem.at[source],
+            device_id={self.axis: target},
+            device_id_type=MESH,
+        )
+
+    def send(self):
+        me = lax.axis_index(self.axis)
+        each(self.total, me, lambda other: self.copy(me, other).start())
+
+    def receive(self):
+        me = lax.axis_index(self.axis)
+        each(self.total, me, lambda other: self.copy(other, me).wait_recv())
+
+    def drain(self):
+        me = lax.axis_index(self.axis)
+        each(self.total, me, lambda other: self.copy(me, other).wait_send())
+
+    def sum(self, at=slice(None)):
+        total = self.buf[0, at]
+        for i in range(1, self.total):
+            total = total + self.buf[i, at]
+        return total
+
+
+class Closing:
+    inputs, outputs = 4, 4
+
+    def __init__(self, count, parts, kept, flat):
+        self.count, self.parts, self.kept, self.flat = count, parts, kept, flat
+
+    def stages(self, scratch):
+        return (
+            Exchange("dp", self.count, *scratch[0:3]),
+            Exchange("tensor", self.parts, *scratch[3:6]),
+            Exchange("dp", self.count, *scratch[6:9]),
+            Exchange("tensor", self.parts, *scratch[9:12]),
+        )
+
+    def begin(self, given, scratch):
+        dp, z = lax.axis_index("dp"), lax.axis_index("tensor")
+        barrier = pltpu.get_barrier_semaphore()
+
+        def hello(axis):
+            def one(other):
+                pl.semaphore_signal(
+                    barrier, inc=1, device_id={axis: other}, device_id_type=MESH
+                )
+
+            return one
+
+        each(self.count, dp, hello("dp"))
+        each(self.parts, z, hello("tensor"))
+        first = self.stages(scratch)[0]
+        first.buf[dp] = given[3][...]
+        pl.semaphore_wait(barrier, self.count + self.parts - 2)
+        first.send()
+
+    def end(self, given, out, scratch):
+        tok_ref, gain_ref, res_ref, flat_ref = given
+        out_ref, wide_ref, rest_ref, gain_out = out
+        dp, z = lax.axis_index("dp"), lax.axis_index("tensor")
+        flat_dp, flat_z, gain_dp, gain_z = self.stages(scratch)
+        sums = scratch[12]
+        rows, model = out_ref.shape
+        flat_dp.receive()
+        flat_z.buf[z] = flat_dp.sum()
+        flat_z.send()
+        sums[...] = jnp.zeros_like(sums)
+
+        def body(i, _):
+            at = pl.ds(pl.multiple_of(i * 32, 32), 32)
+            values, grad = tok_ref[at, :].astype(F32), out_ref[at, :]
+            inv = lax.rsqrt(jnp.mean(values * values, axis=-1, keepdims=True) + epsilon)
+            scaled = grad * gain_ref[0:1, :]
+            inner = jnp.mean(scaled * values, axis=-1, keepdims=True)
+            out_ref[at, :] = (
+                res_ref[at, :] + inv * scaled - values * (inner * inv * inv * inv)
+            )
+            sums[...] += jnp.sum((grad * values * inv).reshape(4, 8, model), axis=0)
+            return 0
+
+        lax.fori_loop(0, rows // 32, body, 0)
+        total = jnp.sum(sums[...], axis=0, keepdims=True)
+        wide = model // 8
+        gain_dp.buf[dp] = jnp.concatenate(
+            [total[:, i * wide : (i + 1) * wide] for i in range(8)], axis=0
+        )
+        gain_dp.send()
+        flat_z.receive()
+        width = flat_ref.shape[1]
+        for i in range(self.parts):
+            wide_ref[:, i * width : (i + 1) * width] = flat_z.buf[i, : self.kept, :]
+        rest_ref[...] = flat_z.sum(slice(self.kept, None))
+        gain_dp.receive()
+        gain_z.buf[z] = gain_dp.sum()
+        gain_z.send()
+        gain_z.receive()
+        gain_out[...] = gain_z.sum()
+        for stage in (flat_dp, flat_z, gain_dp, gain_z):
+            stage.drain()
+
+    def shapes(self, rows, model):
+        height, width = self.flat
+        return (
+            sds(rows, model), sds(self.kept, width * self.parts), sds(height - self.kept, width),
+            sds(8, model // 8),
+        )
+
+    def scratch(self, rows, model):
+        out = []
+        for shape in (self.flat, (8, model // 8)):
+            for total in (self.count, self.parts):
+                out.append(pltpu.VMEM((total,) + shape, F32))
+                out.extend([pltpu.SemaphoreType.DMA((total,))] * 2)
+        return out + [pltpu.VMEM((8, model), F32)]
+
+
+def scatter_kernel(parts, given, count, splits, ending, *refs):
+    lefts, rights_in = refs[0:given], refs[given : given + count]
+    refs = refs[given + count :]
+    extra_in, refs = refs[: ending.inputs], refs[ending.inputs :]
+    extra_out, refs = refs[: ending.outputs], refs[ending.outputs :]
     rights, (part, send_r, send_l, got_l, got_r) = refs[0:count], refs[count : count + 5]
     sem_sr, sem_sl, sem_gl, sem_gr, load_sem = refs[count + 5 : count + 10]
+    extra = refs[count + 10 :]
+    out_ref = extra_out[0]
     me = lax.axis_index("tensor")
     rows, model = out_ref.shape
     size = rows // SUBS
@@ -836,7 +1022,7 @@
     ]
     for load in loads:
         load.start()
-    greet("tensor", parts)
+    ending.begin(extra_in, extra)
     for load in loads:
         load.wait()
 
@@ -947,6 +1133,8 @@
             leftward(slot).wait_recv()
             out_ref[at, :] = out_ref[at, :] + got_r[slot].astype(F32)
 
+    ending.end(extra_in, extra_out, extra)
+
     def finish(slot, _):
         piece = slot // SUBS
 
@@ -963,27 +1151,29 @@
     lax.fori_loop(0, parts * SUBS, finish, 0)
 
 
-def scatter(parts, lefts, rights, splits, number):
+def scatter(parts, lefts, rights, splits, number, ending=None, extra=()):
     total = lefts[0].shape[0]
     model = rights[0].shape[0]
     rows = total // parts
     count = len(rights)
+    ending = ending or Plain(parts)
     slots = pltpu.VMEM((parts * SUBS, rows // SUBS, model), LOW)
-    kernel = functools.partial(scatter_kernel, parts, len(lefts), count, splits)
+    shapes = ending.shapes(rows, model)
     return pl.pallas_call(
-        kernel,
-        out_shape=sds(rows, model),
-        in_specs=[vmem()] * len(lefts) + [hbm()] * count,
-        out_specs=vmem(),
+        functools.partial(scatter_kernel, parts, len(lefts), count, splits, ending),
+        out_shape=shapes,
+        in_specs=[vmem()] * len(lefts) + [hbm()] * count + [vmem()] * len(extra),
+        out_specs=[vmem()] * len(shapes),
         scratch_shapes=[pltpu.VMEM(w.shape, LOW) for w in rights]
         + [pltpu.VMEM((rows, model), F32)]
         + [slots] * 4
         + line_sems(parts * SUBS)
-        + [pltpu.SemaphoreType.DMA((count,))],
+        + [pltpu.SemaphoreType.DMA((count,))]
+        + ending.scratch(rows, model),
         compiler_params=comm_params(number),
         cost_estimate=cost(2 * total * model * sum(w.shape[1] for w in rights), 60 * 2**20),
         name="scatter%d" % number,
-    )(*lefts, *rights)
+    )(*lefts, *rights, *extra)
 
 
 def state_kernel(count, heads, backward, own_ref, out_ref, buf, send_sem, pass_sem, got_sem):
@@ -1102,89 +1292,6 @@
         compiler_params=comm_params(number),
         cost_estimate=cost(count * heads * 6 * 128**3, count * heads * 256 * 128 * 4),
         name="exchange%d" % number,
-    )(own)
-
-
-def totals_kernel(count, parts, kept, own_ref, wide_ref, flat_ref, buf, mid, send1, got1, send2, got2):
-    dp, z = lax.axis_index("dp"), lax.axis_index("tensor")
-    barrier = pltpu.get_barrier_semaphore()
-
-    def hello_dp(k, _):
-        pl.semaphore_signal(
-            barrier, inc=1, device_id={"dp": lax.rem(dp + k, count)}, device_id_type=MESH
-        )
-        return 0
-
-    def hello_z(k, _):
-        pl.semaphore_signal(
-            barrier, inc=1, device_id={"tensor": lax.rem(z + k, parts)}, device_id_type=MESH
-        )
-        return 0
-
-    lax.fori_loop(1, count, hello_dp, 0)
-    lax.fori_loop(1, parts, hello_z, 0)
-    buf[dp] = own_ref[...]
-    pl.semaphore_wait(barrier, count + parts - 2)
-
-    def over_dp(source, target):
-        return pltpu.make_async_remote_copy(
-            src_ref=buf.at[source],
-            dst_ref=buf.at[source],
-            send_sem=send1.at[target],
-            recv_sem=got1.at[source],
-            device_id={"dp": target},
-            device_id_type=MESH,
-        )
-
-    def over_z(source, target):
-        return pltpu.make_async_remote_copy(
-            src_ref=mid.at[source],
-            dst_ref=mid.at[source],
-            send_sem=send2.at[target],
-            recv_sem=got2.at[source],
-            device_id={"tensor": target},
-            device_id_type=MESH,
-        )
-
-    def each(total, me, action):
-        def body(k, _):
-            action(lax.rem(me + k, total))
-            return 0
-
-        lax.fori_loop(1, total, body, 0)
-
-    each(count, dp, lambda other: over_dp(dp, other).start())
-    each(count, dp, lambda other: over_dp(other, dp).wait_recv())
-    total = buf[0]
-    for i in range(1, count):
-        total = total + buf[i]
-    mid[z] = total
-    each(parts, z, lambda other: over_z(z, other).start())
-    each(parts, z, lambda other: over_z(other, z).wait_recv())
-    width = own_ref.shape[1]
-    flat = mid[0, kept:, :]
-    for i in range(parts):
-        wide_ref[:, i * width : (i + 1) * width] = mid[i, :kept, :]
-        if i:
-            flat = flat + mid[i, kept:, :]
-    flat_ref[...] = flat
-    each(count, dp, lambda other: over_dp(dp, other).wait_send())
-    each(parts, z, lambda other: over_z(z, other).wait_send())
-
-
-def totals_of(count, parts, own, kept, number):
-    rows, width = own.shape
-    return pl.pallas_call(
-        functools.partial(totals_kernel, count, parts, kept),
-        out_shape=(sds(kept, width * parts), sds(rows - kept, width)),
-        in_specs=[vmem()],
-        out_specs=[vmem(), vmem()],
-        scratch_shapes=[pltpu.VMEM((count, rows, width), F32), pltpu.VMEM((parts, rows, width), F32)]
-        + [pltpu.SemaphoreType.DMA((count,))] * 2
-        + [pltpu.SemaphoreType.DMA((parts,))] * 2,
-        compiler_params=comm_params(number),
-        cost_estimate=cost(count * rows * width, count * rows * width * 4),
-        name="totals",
     )(own)
 
 
@@ -1223,13 +1330,14 @@
     seq_total = group_rows * dp_parts
     heads = w_alpha.shape[1]
     width = w_query.shape[1]
+    core = lax.rem(dp_index, 2)
     docs = doc_lengths.shape[0] * doc_lengths.shape[1]
     starts = (
         jnp.cumsum(doc_lengths, axis=1)
         - doc_lengths
         + seq_total * lax.broadcasted_iota(jnp.int32, doc_lengths.shape, 0)
     ).reshape(-1)
-    scalars = jnp.concatenate([(dp_index * group_rows).reshape(1), starts]).astype(jnp.int32)
+    scalars = jnp.concatenate([(dp_index * group_rows).reshape(1), starts, core.reshape(1)]).astype(jnp.int32)
     taps = jnp.concatenate([conv_query, conv_key, conv_value, jnp.zeros((4, width), F32)])
     params = jnp.zeros((8, 128), F32).at[0, :heads].set(decay_bias).at[1, :heads].set(decay_log)
     gain_heads = jnp.broadcast_to(head_gain[None], (8, width))
@@ -1242,7 +1350,6 @@
         tensor_parts, tokens, gain_in_rows, w_narrow, (w_query, w_key, w_value, w_gate_out)
     )
     half = width // 2
-    core = lax.rem(dp_index, 2)
     out_half = lax.dynamic_slice_in_dim(after(w_out, narrow), core * half, half, 0)
     out_mine = lax.all_gather(out_half, "tensor", axis=0)
     forth = [(i, i + 1) for i in range(dp_parts - 1)]
@@ -1254,15 +1361,19 @@
         scalars, pieces, rims, narrow, taps, params, docs, heads
     )
     state_in = exchange(dp_parts, totals, heads, False, 3)
-    out_other = lax.ppermute(after(out_mine, state_in), "dp", [(i, i ^ 1) for i in range(dp_parts)])
-    w_out_full = jnp.stack(
-        [jnp.where(core == 0, out_mine, out_other), jnp.where(core == 0, out_other, out_mine)],
-        axis=1,
-    ).reshape(width * tensor_parts, model)
     rows_out, v2, s, mixed = outward(state_in, w, u, qt, ou, t, o, gate_raw, gain_heads, heads)
 
     mixed_own = lax.all_to_all(mixed, "tensor", split_axis=0, concat_axis=1, tiled=True)
-    residual = own_rows + dot(mixed_own, w_out_full)
+    out_mine, _ = lax.optimization_barrier((out_mine, mixed))
+    out_other = lax.ppermute(out_mine, "dp", [(i, i ^ 1) for i in range(dp_parts)])
+    out_mine = out_mine.reshape(tensor_parts * half, model)
+    out_other = out_other.reshape(tensor_parts * half, model)
+    split = mixed_own.reshape(rows_own, tensor_parts, 2, half)
+
+    def of_core(index):
+        return lax.dynamic_index_in_dim(split, index, 2, keepdims=False).reshape(rows_own, -1)
+
+    residual = own_rows + (dot(of_core(core), out_mine) + dot(of_core(1 - core), out_other))
     mid_all, activated, grad_units, mlp_part = feed(
         tensor_parts, residual, gain_mid_rows, (w_gate, w_up, w_down), out_grad
     )
@@ -1283,7 +1394,7 @@
     down_grad_sum = lax.psum_scatter(down_grad, "dp", scatter_dimension=0, tiled=True)
     units_grad_sum = lax.psum_scatter(units_grad, "dp", scatter_dimension=0, tiled=True)
 
-    grad_mid = scatter(
+    (grad_mid,) = scatter(
         tensor_parts, [after(grad_units, units_grad)], [w_gate, w_up],
         ((0, 0, units), (0, units, units)), 4,
     )
@@ -1291,66 +1402,66 @@
     grad_own = lax.dynamic_slice_in_dim(out_grad, tensor_index * rows_own, rows_own, 0)
     grad_residual = grad_own.astype(F32) + grad_res_norm
     grad_mixer = grad_residual.astype(LOW)
-    grad_mixed_own = contract_cols(grad_mixer, w_out_full).astype(LOW)
+    grad_mixed = jnp.concatenate(
+        [contract_cols(grad_mixer, weight).astype(LOW) for weight in (out_mine, out_other)], axis=1
+    ).reshape(rows_own, 2, tensor_parts, half)
     grad_mixed = lax.all_to_all(
-        grad_mixed_own, "tensor", split_axis=1, concat_axis=0, tiled=True
-    )
-    grad_mixer_all, mlp_run = lax.optimization_barrier((grad_mixer, mlp_run, grad_mixed))[:2]
-    grad_mixer_all = lax.all_gather(grad_mixer_all, "tensor", axis=0, tiled=True)
+        grad_mixed, "tensor", split_axis=2, concat_axis=0, tiled=True
+    ).reshape(group_rows, width)
+    mlp_run = after(mlp_run, grad_mixed)
+    out_w = contract_rows(after(grad_mixer, grad_mixed), mixed_own).astype(LOW)
+    out_w_sum = lax.psum_scatter(out_w, "dp", scatter_dimension=0, tiled=True)
     for back_by in range(2, tensor_parts - 1):
         mlp_run = lax.ppermute(added(mlp_part, back_by, mlp_run), "tensor", ring)
 
     do, gate_low, head_gain_part, ds_total = inward(
-        grad_mixed, rows_out, gate_raw, gain_heads, qt, t, totals, heads
+        scalars, grad_mixed, rows_out, gate_raw, gain_heads, qt, t, totals, heads
     )
     grad_end = exchange(dp_parts, ds_total, heads, True, 5)
     grad_end, mlp_run, _, _ = lax.optimization_barrier(
         (grad_end, mlp_run, units_grad_sum, down_grad_sum)
     )
+    mlp_run = lax.ppermute(added(mlp_part, tensor_parts - 1, mlp_run), "tensor", ring)
     grads, tails, rim_grad, taps_grad, params_grad = back(
         scalars, pieces, rims, narrow, taps, params, grad_end, do, v2, s, x, p, kg, w, u, qt, t,
         gate_low, docs, heads,
     )
+    grads, tails, rim_grad, taps_grad, params_grad, mlp_run = lax.optimization_barrier(
+        (grads, tails, rim_grad, taps_grad, params_grad, mlp_run)
+    )
     rim_back = lax.ppermute(rim_grad, "dp", [(i + 1, i) for i in range(dp_parts - 1)])
     tails = tails.at[HALO - 8 :].add(rim_back).astype(LOW)
     grads = lax.dynamic_update_slice(grads, tails, (group_rows - HALO, 0))
-    mlp_run = lax.ppermute(
-        added(mlp_part, tensor_parts - 1, after(mlp_run, rim_grad)), "tensor", ring
-    )
-    out_w = contract_rows(after(grad_mixer_all, rim_grad), mixed).astype(LOW)
-    out_w_sum = lax.psum_scatter(out_w, "dp", scatter_dimension=0, tiled=True).astype(F32)
-    mixer_grad = contract_rows(normed_all, after(grads, out_w)).astype(LOW)
-    mixer_grad, mlp_run = lax.optimization_barrier((mixer_grad, mlp_run))
+    out_w_sum = lax.psum_scatter(
+        out_w_sum, "tensor", scatter_dimension=1, tiled=True
+    )
+    mixer_grad = contract_rows(normed_all, grads).astype(LOW)
     mixer_sum = lax.psum_scatter(mixer_grad, "dp", scatter_dimension=0, tiled=True).astype(F32)
     output = (residual + (piece_of(mlp_part, 0).astype(F32) + mlp_run.astype(F32))).astype(LOW)
-    grad_normed = scatter(
-        tensor_parts, [after(grads, mixer_grad)],
-        [w_query, w_key, w_value, w_narrow, w_gate_out],
-        ((0, 0, width), (0, width, width), (0, 2 * width, width), (0, 3 * width, 128), (0, 3 * width + 128, width)),
-        6,
-    )
-    grad_tokens, gain_in_grad = norm_back(own_rows, gain_in, grad_normed)
-    input_grad = grad_residual + grad_tokens
-
     params_grad = params_grad.reshape(2, 8, 128).sum(1)
     flat = jnp.concatenate(
         [
             taps_grad.sum(1),
             head_gain_part.sum(0)[None],
             jnp.pad(params_grad, ((0, 1), (0, width - 128))),
-            gain_in_grad.reshape(-1, width),
-            gain_mid_grad.reshape(-1, width),
+            jnp.pad(gain_mid_grad.reshape(-1, width), ((0, 4), (0, 0))),
         ],
         axis=0,
     )
-    wide, gains = totals_of(dp_parts, tensor_parts, flat, 16, 7)
+    input_grad, wide, rest, gain_in_grad = scatter(
+        tensor_parts, [after(grads, mixer_grad)],
+        [w_query, w_key, w_value, w_narrow, w_gate_out],
+        ((0, 0, width), (0, width, width), (0, 2 * width, width), (0, 3 * width, 128), (0, 3 * width + 128, width)),
+        6, Closing(dp_parts, tensor_parts, 16, flat.shape),
+        (tokens, gain_in_rows, grad_residual, flat),
+    )
+    out_w_sum = after(out_w_sum, gain_in_grad).astype(F32)
     by_head = wide[13:15].reshape(2, tensor_parts, width)[:, :, :heads].reshape(2, -1)
-    gains = gains.reshape(2, model)
     start = 3 * width
     return (
         output,
         input_grad,
-        gains[0],
+        gain_in_grad.reshape(model),
         mixer_sum[:, :width],
         mixer_sum[:, width : 2 * width],
         mixer_sum[:, 2 * width : start],
@@ -1364,7 +1475,7 @@
         by_head[0],
         wide[12],
         out_w_sum.T,
-        gains[1],
+        rest[: model // width].reshape(model),
         units_grad_sum[:, :units].astype(F32),
         units_grad_sum[:, units:].astype(F32),
         down_grad_sum.T.astype(F32),

time: 740 us -> 724 us (0.978)
  waiting for transfers between devices: 63.8 us -> 45.6 us
  other arithmetic: 42.3 us -> 27.4 us
  local copies, waits for them, and re-layouts: 27.5 us -> 36 us
    all_to_all x1, waiting for transfers between devices: 9.52 us -> 23.2 us  [local(): lax.all_to_all(mixed, 'tensor', split_axis=0, concat_axis=1, tiled=True)]
    another operation x2 -> x0, other arithmetic: 13.4 us -> none  [local(): jnp.stack([jnp.where(core == 0, out_mine, out_other), jnp.where(core == 0...]
    all_gather x1, waiting for transfers between devices: 16.6 us -> 4.53 us  [local(): out_mine = lax.all_gather(out_half, 'tensor', axis=0)]
    ppermute x1, waiting for transfers between devices: 9.89 us -> 0.01 us  [local(): mlp_run = lax.ppermute(added(mlp_part, back_by, mlp_run), 'tensor', ring)]
    ppermute x2, waiting for transfers between devices: 8.34 us -> 0.01 us  [the longest x1 0.01 us: local(): lax.ppermute(out_mine, 'dp', [(i, i ^ 1) for i in range(dp_parts)])]
    pallas_call x3 -> x2, Pallas kernels: 180 us -> 181 us  [scatter(): pl.pallas_call(functools.partial(scatter_kernel, parts, len(lefts), count...]
  transfers between devices with their start and end apart: 13 -> 13, of which waited for: 7 -> 5; matrix products, arithmetic and copies ran while one was open for 14% -> 13% of each run, Pallas kernels for 44% -> 46%
where the time goes in v4:
time: 724 us; the launch traced here: 712 us
  Pallas kernels  484 us (67%)
  matrix products  63.9 us (9%)
  waiting for transfers between devices  45.6 us (6%)
  local copies, waits for them, and re-layouts  36 us (5%)
  other arithmetic  27.4 us (4%)
  blocking collectives  24 us (3%)
  starting transfers between devices  16.3 us (2%)
  between operations  15 us (2%)
    pallas_call x2, Pallas kernels, scatter(): pl.pallas_call(functools.partial(scatter_kernel, parts, len(lefts), count...  181 us
    pallas_call x1, Pallas kernels, feed(): pl.pallas_call(functools.partial(feed_kernel, parts), out_shape=(sds(tota...  78.4 us
    pallas_call x1, Pallas kernels, project(): pl.pallas_call(functools.partial(project_kernel, parts), out_shape=(sds(t...  75.1 us
    dot_general x4, matrix products, contract_rows(): return lax.dot_general(left, right, TN, preferred_element_type=F32)  50.2 us
    pallas_call x1, Pallas kernels, back(): pl.pallas_call(functools.partial(back_kernel, docs, heads, chunks), out_s...  47.5 us
    pallas_call x1, Pallas kernels, intra(): pl.pallas_call(functools.partial(intra_kernel, docs, heads), out_shape=(t...  41 us
    pallas_call x2, Pallas kernels, exchange(): pl.pallas_call(functools.partial(state_kernel, count, heads, backward), o...  38.1 us
    all_to_all x1, blocking collectives, local(): lax.all_to_all(grad_mixed, 'tensor', split_axis=2, concat_axis=0, tiled=T...  24 us
  transfers between devices with their start and end apart: 13, of which 5 were waited for; matrix products, arithmetic and copies ran while one was open for 13% of the time, Pallas kernels for 46%

profile of v4, /device:TPU:12, one launch (start us, length us, event | category | flops | bytes accessed | tf_op | source)
XLA Modules:
  0.0 712.4 jit_solution(7814902909060859921)
XLA Ops:
  10.7 75.1 %project.1 = (bf16[1024,2048]{1,0:T(8,128)(2,1)}, bf16[1024,512]{1,0:T(8,128)(2,1)}, bf16[1024,512]{1,0:T(8,128)(2,1)}, bf16[1024,512]{1,0:T(8,128)(2,1)}, f32[1024,512]{1,0:T(8,128)}, /*index=5*/f32[1024,128]{1,0:T(8,128)}) custom-call(bf16[256,2048]{1,0:T(8,128)(2,1)} %refs_6_.1, f32[8,2048]{1,0:T(8,128)} %broadcast_in_dim.10.gain_ref.refs_7_, ...), custom_call_target="tpu_custom_call" | custom-call | flops 9126805504 | bytes 62914560 | tf_op jit(solution)/shard_map/project/pallas_call | solution.py:751
  92.1 2.6 collective-permute-done
  95.3 41.0 %intra.1 = (f32[8,4,128,128]{3,2,1,0:T(8,128)}, f32[8,4,128,128]{3,2,1,0:T(8,128)}, f32[8,4,128,128]{3,2,1,0:T(8,128)}, f32[1024,512]{1,0:T(8,128)}, f32[1024,51...) custom-call(s32[6]{0:T(128)} %pad_add_fusion.scalars, ...), custom_call_target="tpu_custom_call" | custom-call | flops 24159191040 | bytes 62914560 | tf_op jit(solution)/shard_map/intra/pallas_call | solution.py:259
  136.3 16.0 %exchange3.1.s_in = f32[4,128,128]{2,1,0:T(8,128)} custom-call(f32[4,128,256]{2,1,0:T(8,128)} %get-tuple-element.115.own_ref.maps_ref), custom_call_target="tpu_custom_call" | custom-call | flops 402653184 | bytes 4194304 | tf_op jit(solution)/shard_map/exchange3/pallas_call | solution.py:1285
  152.9 11.5 %outward.1 = (f32[1024,512]{1,0:T(8,128)}, f32[1024,512]{1,0:T(8,128)}, f32[8,4,128,128]{3,2,1,0:T(8,128)}, bf16[1024,512]{1,0:T(8,128)(2,1)}) custom-call(f32[4,128,128]{2,1,0:T(8,128)} %exchange3.1.s_in, f32[1024,512]{1,0:T(8,128)} %get-tuple-element.116.w_ref.refs_19_, f32[1024,512]{1,0:T(8,128)} %get-tuple-element.117.u_ref.refs_20_, ...), custom_call_target="tpu_custom_call" | custom-call | flops 1207959552 | bytes 23068672 | tf_op jit(solution)/shard_map/outward/pallas_call | solution.py:315
  164.4 4.5 all-gather.3.cloned.1.call-done
  169.0 2.3 copy.62
  171.2 6.5 all-to-all-start
  178.0 23.2 %all-to-all-done = bf16[4,256,512]{1,2,0:T(8,128)(2,1)S(1)} async-done(((bf16[4,256,512]{1,2,0:T(8,128)(2,1)}), bf16[4,256,512]{1,2,0:T(8,128)(2,1)S(1)}, u32[]{:S(2)}, u32[]{:S(2)}) %all-to-all-start) | async-done | bytes 1048608 | tf_op jit(solution)/shard_map/all_to_all | solution.py:1366
  201.2 3.5 fusion.8
  204.8 4.9 multiply_reduce_fusion.2
  210.4 78.4 %feed.1 = (bf16[1024,2048]{1,0:T(8,128)(2,1)}, bf16[1024,1408]{1,0:T(8,128)(2,1)}, bf16[1024,2816]{1,0:T(8,128)(2,1)}, bf16[1024,2048]{1,0:T(8,128)(2,1)}) custom-call(f32[256,2048]{1,0:T(8,128)} %get-tuple-element.269.res_ref, f32[8,2048]{1,0:T(8,128)} %broadcast_in_dim.13.gain_ref, bf16[2048,1408]{1,0:T(8,128)(2,1)} %refs_1_.6, ...), custom_call_target="tpu_custom_call" | custom-call | flops 23622320128 | bytes 125829120 | tf_op jit(solution)/shard_map/feed/pallas_call | solution.py:832
  288.7 10.5 %fusion = bf16[2048,1408]{0,1:T(8,128)(2,1)} fusion(bf16[1024,1408]{1,0:T(8,128)(2,1)} %get-tuple-element.129, bf16[1024,2048]{1,0:T(8,128)(2,1)} %refs_3_.4), kind=kOutput, calls=%fused_computation.4 | convolution fusion | flops 5908463616 | bytes 12845056 | tf_op jit(solution)/shard_map/dot_general | solution.py:556
  302.1 18.5 %convolution_convert_fusion.1 = bf16[2048,2816]{1,0:T(8,128)(2,1)} fusion(bf16[1024,2048]{1,0:T(8,128)(2,1)} %get-tuple-element.128, bf16[1024,2816]{1,0:T(8,128)(2,1)} %get-tuple-element.132.refs_0_), kind=kOutput, calls=%fused_computation.1 | convolution fusion | flops 11816927232 | bytes 21495808 | tf_op jit(solution)/shard_map/dot_general | solution.py:556
  320.6 13.2 %collective-permute-done.2 = bf16[256,2048]{1,0:T(8,128)(2,1)S(1)} collective-permute-done((bf16[256,2048]{1,0:T(8,128)(2,1)S(1)}, bf16[256,2048]{1,0:T(8,128)(2,1)S(1)}, u32[]{:S(2)}, u32[]{:S(2)}) %collective-permute-start.2) | collective-permute-done | bytes 1048608 | tf_op jit(solution)/shard_map/ppermute | solution.py:1390
  334.8 82.7 %scatter4.1 = f32[256,2048]{1,0:T(8,128)} custom-call(bf16[1024,2816]{1,0:T(8,128)(2,1)} %get-tuple-element.132.refs_0_, bf16[2048,1408]{1,0:T(8,128)(2,1)} %refs_1_.6, bf16[2048,1408]{1,0:T(8,128)(2,1)} %refs_2_.6), custom_call_target="tpu_custom_call" | custom-call | flops 11811160064 | bytes 62914560 | tf_op jit(solution)/shard_map/scatter4/pallas_call | solution.py:1162
  417.5 2.3 multiply_reduce_fusion
  419.9 3.2 fusion.3
  423.1 3.9 convolution_convert_fusion.4
  429.4 2.6 reshape.214
  434.1 24.0 %all_to_all.34 = bf16[256,2,4,256]{3,1,0,2:T(2,128)(2,1)S(1)} all-to-all(bf16[256,2,4,256]{3,1,0,2:T(2,128)(2,1)S(1)} %copy.63), channel_id=1, replica_groups=mesh['dp'=8,'tensor'=4] {'tensor'}, dimensions={2} | all-to-all | bytes 2097152 | tf_op jit(solution)/shard_map/all_to_all | solution.py:1408
  459.3 5.6 convolution_convert_fusion.2
  466.1 2.6 add_convert_fusion.2
  469.3 12.3 %inward.1 = (f32[1024,512]{1,0:T(8,128)}, bf16[1024,512]{1,0:T(8,128)(2,1)}, f32[8,512]{1,0:T(8,128)}, f32[4,128,256]{2,1,0:T(8,128)}) custom-call(s32[6]{0:T(128)} %pad_add_fusion.scalars, bf16[1024,512]{1,0:T(8,128)(2,1)} %bitcast.69, f32[1024,512]{1,0:T(8,128)} %get-tuple-element.133.out_ref, f32[1024,512]{1,0:T(8,128)} %get-tuple-element.122.gate_ref, ...), custom_call_target="tpu_custom_call" | custom-call | flops 805306368 | bytes 14680064 | tf_op jit(solution)/shard_map/inward/pallas_call | solution.py:369
  481.6 22.1 %exchange5.1.refs_12_ = f32[4,128,128]{2,1,0:T(8,128)} custom-call(f32[4,128,256]{2,1,0:T(8,128)} %get-tuple-element.134.own_ref), custom_call_target="tpu_custom_call" | custom-call | flops 402653184 | bytes 4194304 | tf_op jit(solution)/shard_map/exchange5/pallas_call | solution.py:1285
  507.6 47.5 %back.1 = (bf16[1024,2176]{1,0:T(8,128)(2,1)}, f32[16,1536]{1,0:T(8,128)}, f32[8,1536]{1,0:T(8,128)}, f32[12,8,512]{2,1,0:T(8,128)}, f32[16,128]{1,0:T(8,128)}) custom-call(s32[6]{0:T(128)} %pad_add_fusion.scalars, bf16[1024,512]{1,0:T(8,128)(2,1)} %get-tuple-element.111.refs_0_.refs_3_, bf16[1024,512]{1,0:T(8,128)(2,1)} %get-tuple-element.112.refs_1_.refs_4_, ...), custom_call_target="tpu_custom_call" | custom-call | flops 8053063680 | bytes 33554432 | tf_op jit(solution)/shard_map/back/pallas_call | solution.py:530
  556.1 3.3 collective-permute-start.5
  564.4 15.5 %convolution_convert_fusion = bf16[2048,2176]{1,0:T(8,128)(2,1)} fusion(bf16[1024,2048]{1,0:T(8,128)(2,1)} %get-tuple-element.155, bf16[1024,2176]{1,0:T(8,128)(2,1)} %convert_dynamic-update-slice_fusion.refs_0_), kind=kOutput, calls=%fused_computation | convolution fusion | flops 9131261952 | bytes 17563648 | tf_op jit(solution)/shard_map/dot_general | solution.py:556
  580.8 2.3 convert_bitcast_fusion
  587.2 3.0 add_convert_fusion
  590.2 97.8 %scatter6.1 = (f32[256,2048]{1,0:T(8,128)}, f32[16,2048]{1,0:T(8,128)}, f32[8,512]{1,0:T(8,128)}, f32[8,256]{1,0:T(8,128)}) custom-call(bf16[1024,2176]{1,0:T(8,128)(2,1)} %convert_dynamic-update-slice_fusion.refs_0_, bf16[2048,512]{1,0:T(8,128)(2,1)} %refs_1_.7, bf16[2048,512]{1,0:T(8,128)(2,1)} %refs_2_.7, bf16[2048,512]{1,0:T(8,128)(2,1)} %refs_3_.5, ...), custom_call_target="tpu_custom_call" | custom-call | flops 9126805504 | bytes 62914560 | tf_op jit(solution)/shard_map/scatter6/pallas_call | solution.py:1162
  700.1 2.8 fusion.4
  (122 shorter events, 52.1 us)
Async XLA Ops:
  7.2 78.6 %copy-start = (bf16[512,2048]{1,0:T(8,128)(2,1)S(1)}, bf16[512,2048]{1,0:T(8,128)(2,1)}, u32[]{:S(2)}) copy-start(bf16[512,2048]{1,0:T(8,128)(2,1)} %param.41) | copy-start | bytes 6291460
  7.2 161.8 %all-gather.3.cloned.1.call-start = ((), (), s32[]{:S(2)}) async-start(), calls=%async_computation.12 | async-start | bytes 5242880 | tf_op jit(solution)/shard_map/all_gather | solution.py:1354
  85.7 4.6 copy-start.21
  85.8 4.9 copy-start.13
  85.8 4.8 copy-start.14
  85.8 4.8 copy-start.15
  85.8 6.1 copy-start.18
  85.8 6.1 copy-start.19
  88.4 6.3 collective-permute-start
  92.1 3.2 copy-start.16
  95.3 57.0 %copy-start.17 = (f32[512]{0:T(512)S(1)}, f32[512]{0:T(512)}, u32[]{:S(2)}) copy-start(f32[512]{0:T(512)} %param.40) | copy-start | bytes 6148
  169.0 35.8 %collective-permute-start.1 = (bf16[4,256,2048]{2,1,0:T(8,128)(2,1)}, bf16[4,256,2048]{2,1,0:T(8,128)(2,1)}, u32[]{:S(2)}, u32[]{:S(2)}) collective-permute-start(bf16[4,256,2048]{2,1,0:T(8,128)(2,1)} %bitcast.81), channel_id=1, source_target_pairs={{0,4},{4,0},{8,12},{12,8},{16,20},{20,16},{24,28},{28,24},{1,5},{5... | collective-permute-start | bytes 12582920 | tf_op jit(solution)/shard_map/ppermute | solution.py:1368
  171.2 29.9 %all-to-all-start = ((bf16[4,256,512]{1,2,0:T(8,128)(2,1)}), bf16[4,256,512]{1,2,0:T(8,128)(2,1)S(1)}, u32[]{:S(2)}, u32[]{:S(2)}) async-start(bf16[4,256,512]{1,2,0:T(8,128)(2,1)} %copy.62), calls=%async_computation | async-start | bytes 2097152 | tf_op jit(solution)/shard_map/all_to_all | solution.py:1366
  177.7 326.0 %reduce-scatter.8.cloned.1.call-start = ((), (), s32[]{:S(2)}) async-start(), calls=%async_computation.8 | async-start | bytes 6488064 | tf_op jit(solution)/shard_map/reduce_scatter | solution.py:1394
  201.2 3.6 copy-start.11
  204.8 5.0 copy-start.12
  299.3 204.5 %reduce-scatter.6.cloned.1.call-start = ((), (), s32[]{:S(2)}) async-start(), calls=%async_computation.7 | async-start | bytes 12976128 | tf_op jit(solution)/shard_map/reduce_scatter | solution.py:1395
  300.7 33.2 %collective-permute-start.2 = (bf16[256,2048]{1,0:T(8,128)(2,1)S(1)}, bf16[256,2048]{1,0:T(8,128)(2,1)S(1)}, u32[]{:S(2)}, u32[]{:S(2)}) collective-permute-start(bf16[256,2048]{1,0:T(8,128)(2,1)S(1)} %constant_dynamic-slice_fusion), channel_id=1, source_target_pairs={{0,1},{1,2},{2,3},{3,0},{4,5},{5,6},{6,7},{7,4},{8,9},{9,10},{10,1... | collective-permute-start | bytes 3145736 | tf_op jit(solution)/shard_map/ppermute | solution.py:1390
  334.8 224.6 %reduce-scatter.12.cloned.1.call-start = ((), (), s32[]{:S(2)}) async-start(), calls=%async_computation.10 | async-start | bytes 9437184 | tf_op jit(solution)/shard_map/reduce_scatter | solution.py:1413
  334.8 82.7 %copy-start.2 = (f32[256,2048]{1,0:T(8,128)S(1)}, f32[256,2048]{1,0:T(8,128)}, u32[]{:S(2)}) copy-start(f32[256,2048]{1,0:T(8,128)} %get-tuple-element.269.res_ref) | copy-start | bytes 6291460
  417.5 2.3 copy-start.3
  423.1 3.9 copy-start.4
  423.1 3.9 copy-start.20
  434.1 25.2 %copy-start.5 = (bf16[256,2048]{1,0:T(8,128)(2,1)S(1)}, bf16[256,2048]{1,0:T(8,128)(2,1)}, u32[]{:S(2)}) copy-start(bf16[256,2048]{1,0:T(8,128)(2,1)} %copy-done.4) | copy-start | bytes 3145732
  465.0 229.2 %reduce-scatter.14.cloned.1.call-start = ((), (), s32[]{:S(2)}) async-start(), calls=%async_computation.11 | async-start | bytes 1310720 | tf_op jit(solution)/shard_map/reduce_scatter | solution.py:1435
  468.7 35.0 %collective-permute-start.3 = (bf16[256,2048]{1,0:T(8,128)(2,1)}, bf16[256,2048]{1,0:T(8,128)(2,1)S(1)}, u32[]{:S(2)}, u32[]{:S(2)}) collective-permute-start(bf16[256,2048]{1,0:T(8,128)(2,1)} %add_convert_fusion.2), channel_id=1, source_target_pairs={{0,1},{1,2},{2,3},{3,0},{4,5},{5,6},{6,7},{7,4},{8,9},{9,10},{10,1... | collective-permute-start | bytes 3145736 | tf_op jit(solution)/shard_map/ppermute | solution.py:1415
  505.4 49.7 %collective-permute-start.4 = (bf16[256,2048]{1,0:T(8,128)(2,1)S(1)}, bf16[256,2048]{1,0:T(8,128)(2,1)S(1)}, u32[]{:S(2)}, u32[]{:S(2)}) collective-permute-start(bf16[256,2048]{1,0:T(8,128)(2,1)S(1)} %add_convert_fusion.1), channel_id=1, source_target_pairs={{0,1},{1,2},{2,3},{3,0},{4,5},{5,6},{6,7},{7,4},{8,9},{9,10},{10,1... | collective-permute-start | bytes 3145736 | tf_op jit(solution)/shard_map/ppermute | solution.py:1424
  556.1 5.3 collective-permute-start.5
  559.5 138.3 %reduce-scatter.10.cloned.1.call-start = ((), (), s32[]{:S(2)}) async-start(), calls=%async_computation.9 | async-start | bytes 10027008 | tf_op jit(solution)/shard_map/reduce_scatter | solution.py:1439
  579.9 3.2 copy-start.7
  700.1 2.8 copy-start.6
  702.9 2.3 copy-start.1
  (3 other events, 3.2 us)
Sparse Core Ops, SparseCore 0:
  87.1 81.8 all-gather.2
  299.4 69.7 reduce-scatter.7
  373.1 86.7 reduce-scatter.5
  465.1 75.9 reduce-scatter.11
  559.6 25.1 reduce-scatter.13
  588.7 74.4 reduce-scatter.9

commit v5 on v4

--- a/solution.py
+++ b/solution.py
@@ -22,27 +22,6 @@
     return lax.dot_general(
         left, right, dims, precision=lax.Precision.HIGH, preferred_element_type=F32
     )
-
-
-def halves(values):
-    high = values.astype(LOW)
-    return high, (values - high.astype(F32)).astype(LOW)
-
-
-def mm_split(left, right):
-    (lh, ll), (rh, rl) = left, right
-    return lax.dot_general(
-        jnp.concatenate([lh, ll, lh], axis=1),
-        jnp.concatenate([rh, rh, rl], axis=0),
-        NN,
-        preferred_element_type=F32,
-    )
-
-
-def mm_sum(left, right):
-    (lh, ll), (rh, rl) = left, right
-    one = functools.partial(lax.dot_general, dimension_numbers=NN, preferred_element_type=F32)
-    return one(lh, rh) + (one(ll, rh) + one(lh, rl))
 
 
 def mm_full(left, right, dims=NN):
@@ -146,12 +125,25 @@
     return lax.rsqrt(jnp.sum(values * values, axis=-1, keepdims=True) + epsilon)
 
 
-def load_pieces(step, mains, priors, rims):
-    pieces = [m[...].astype(F32) for m in mains]
+GROUP = 2
+
+
+def chunk_inputs(step, position, mains, priors, rims, narrow_ref, taps, params, scalars, docs, heads):
+    out = []
+    whole = [m[...].astype(F32) for m in mains]
     befores = [
         jnp.where(step == 0, r[...].astype(F32), p[...].astype(F32)) for p, r in zip(priors, rims)
     ]
-    return pieces, befores
+    for j in range(GROUP):
+        rows = slice(j * CHUNK, j * CHUNK + CHUNK)
+        masks = chunk_masks(position + j * CHUNK, scalars, docs)
+        pieces = [w[rows] for w in whole]
+        if j:
+            befores = [w[j * CHUNK - HALO : j * CHUNK] for w in whole]
+        feats = features(pieces, befores, taps, masks, heads)
+        gate = gates(narrow_ref[rows, :], params, masks)
+        out.append((rows, masks, feats, gate))
+    return out
 
 
 def intra_kernel(docs, heads, scalars, *refs):
@@ -160,80 +152,84 @@
     x_ref, p_ref, kg_ref, w_ref, u_ref, qt_ref, ou_ref, t_ref, o_ref, tot_ref = refs[12:22]
     run = refs[22]
     step = pl.program_id(0)
-    position = scalars[0] + step * CHUNK
-    masks = chunk_masks(position, scalars, docs)
-    pieces, befores = load_pieces(step, mains, priors, rims)
-    feats = features(pieces, befores, taps_ref[...], masks, heads)
-    _, _, _, beta, total, total_row = gates(narrow_ref[...], params_ref[...], masks)
+    position = scalars[0] + step * (CHUNK * GROUP)
+    inputs = chunk_inputs(
+        step, position, mains, priors, rims, narrow_ref, taps_ref[...], params_ref[...], scalars,
+        docs, heads,
+    )
+    masks = inputs[0][1]
     eye = jnp.where(masks["row"] == masks["col"], 1.0, 0.0)
-    conv = [pre * sg for _, pre, sg in feats]
-    hs = range(heads)
-    q, k, v, terms, b = [], [], [], [], []
-    for h in hs:
-        cq, ck = conv[0][:, lanes(h)], conv[1][:, lanes(h)]
-        q.append(cq * (unit(cq) * (1.0 / math.sqrt(128.0))))
-        k.append(ck * unit(ck))
-        v.append(conv[2][:, lanes(h)])
+    items = [(j, h) for j in range(GROUP) for h in range(heads)]
+    every = range(len(items))
+    q, k, v, terms, b, strict = [], [], [], [], [], []
+    for j, h in items:
+        _, masks, feats, (_, _, _, beta, total, total_row) = inputs[j]
+        conv = [pre[:, lanes(h)] * sg[:, lanes(h)] for _, pre, sg in feats]
+        q.append(conv[0] * (unit(conv[0]) * (1.0 / math.sqrt(128.0))))
+        k.append(conv[1] * unit(conv[1]))
+        v.append(conv[2])
         terms.append(decay_terms(h, total, total_row, masks))
         b.append(beta[:, heads + h : heads + h + 1])
-    kg = [jnp.where(masks["strict"], mm(k[h], k[h], NT) * terms[h][0], 0.0) for h in hs]
-    p = [mm(q[h], k[h], NT) * terms[h][0] for h in hs]
-    a = [b[h] * kg[h] for h in hs]
+        strict.append(masks["strict"])
+    kg = [jnp.where(strict[i], mm(k[i], k[i], NT) * terms[i][0], 0.0) for i in every]
+    p = [mm(q[i], k[i], NT) * terms[i][0] for i in every]
+    a = [b[i] * kg[i] for i in every]
     pair = (masks["row"] >> 1) == (masks["col"] >> 1)
-    x = [eye - jnp.where(pair, a[h], 0.0) for h in hs]
+    x = [eye - jnp.where(pair, a[i], 0.0) for i in every]
     for level in range(1, 7):
         wide = (masks["row"] >> (level + 1)) == (masks["col"] >> (level + 1))
         off = wide & ((masks["row"] >> level) != (masks["col"] >> level))
-        lx = [mm(jnp.where(off, a[h], 0.0), x[h]) for h in hs]
-        x = [x[h] - mm(x[h], lx[h]) for h in hs]
+        lx = [mm(jnp.where(off, a[i], 0.0), x[i]) for i in every]
+        x = [x[i] - mm(x[i], lx[i]) for i in every]
     wu = [
-        mm(x[h], jnp.concatenate([(b[h] * terms[h][1]) * k[h], b[h] * v[h]], axis=1)) for h in hs
+        mm(x[i], jnp.concatenate([(b[i] * terms[i][1]) * k[i], b[i] * v[i]], axis=1)) for i in every
     ]
-    pwu = [mm(p[h], wu[h]) for h in hs]
-    kwu = [mm(terms[h][2] * k[h], wu[h], TN) for h in hs]
+    pwu = [mm(p[i], wu[i]) for i in every]
+    kwu = [mm(terms[i][2] * k[i], wu[i], TN) for i in every]
 
     @pl.when(step == 0)
     def _():
-        for h in hs:
+        for h in range(heads):
             run[h] = jnp.concatenate([jnp.zeros((128, 128), F32), eye], axis=1)
 
-    for h in hs:
-        x_ref[0, h] = x[h]
-        p_ref[0, h] = p[h]
-        kg_ref[0, h] = kg[h]
-        w_ref[:, lanes(h)] = wu[h][:, :128]
-        u_ref[:, lanes(h)] = wu[h][:, 128:]
-        qt_ref[:, lanes(h)] = terms[h][1] * q[h] - pwu[h][:, :128]
-        ou_ref[:, lanes(h)] = pwu[h][:, 128:]
-        transfer = terms[h][3] * eye - kwu[h][:, :128]
-        offset = kwu[h][:, 128:]
-        t_ref[0, h] = transfer
-        o_ref[0, h] = offset
+    for i, (j, h) in enumerate(items):
+        rows = inputs[j][0]
+        x_ref[j, h] = x[i]
+        p_ref[j, h] = p[i]
+        kg_ref[j, h] = kg[i]
+        w_ref[rows, lanes(h)] = wu[i][:, :128]
+        u_ref[rows, lanes(h)] = wu[i][:, 128:]
+        qt_ref[rows, lanes(h)] = terms[i][1] * q[i] - pwu[i][:, :128]
+        ou_ref[rows, lanes(h)] = pwu[i][:, 128:]
+        transfer = terms[i][3] * eye - kwu[i][:, :128]
+        offset = kwu[i][:, 128:]
+        t_ref[j, h] = transfer
+        o_ref[j, h] = offset
         new = mm(transfer, run[h])
         new = jnp.concatenate([new[:, :128] + offset, new[:, 128:]], axis=1)
         run[h] = new
         tot_ref[h] = new
 
 
-def rows_spec(width, chunks, reverse=False):
-    if reverse:
-        return pl.BlockSpec((CHUNK, width), lambda c, *_: (chunks - 1 - c, 0))
-    return pl.BlockSpec((CHUNK, width), lambda c, *_: (c, 0))
-
-
-def halo_spec(width, chunks, reverse=False):
-    per = CHUNK // HALO
-    if reverse:
-        return pl.BlockSpec(
-            (HALO, width), lambda c, *_: (jnp.maximum((chunks - 1 - c) * per - 1, 0), 0)
-        )
-    return pl.BlockSpec((HALO, width), lambda c, *_: (jnp.maximum(c * per - 1, 0), 0))
-
-
-def tile_spec(heads, chunks, reverse=False):
-    if reverse:
-        return pl.BlockSpec((1, heads, 128, 128), lambda c, *_: (chunks - 1 - c, 0, 0, 0))
-    return pl.BlockSpec((1, heads, 128, 128), lambda c, *_: (c, 0, 0, 0))
+def at_step(chunks, reverse, group):
+    steps = chunks // group
+    return (lambda c: steps - 1 - c) if reverse else (lambda c: c)
+
+
+def rows_spec(width, chunks, reverse=False, group=1):
+    at = at_step(chunks, reverse, group)
+    return pl.BlockSpec((CHUNK * group, width), lambda c, *_: (at(c), 0))
+
+
+def halo_spec(width, chunks, reverse=False, group=1):
+    per = CHUNK * group // HALO
+    at = at_step(chunks, reverse, group)
+    return pl.BlockSpec((HALO, width), lambda c, *_: (jnp.maximum(at(c) * per - 1, 0), 0))
+
+
+def tile_spec(heads, chunks, reverse=False, group=1):
+    at = at_step(chunks, reverse, group)
+    return pl.BlockSpec((group, heads, 128, 128), lambda c, *_: (at(c), 0, 0, 0))
 
 
 def whole_spec(*shape):
@@ -261,14 +257,14 @@
         out_shape=(tiles, tiles, tiles, flat, flat, flat, flat, tiles, tiles, sds(heads, 128, 256)),
         grid_spec=pltpu.PrefetchScalarGridSpec(
             num_scalar_prefetch=1,
-            grid=(chunks,),
-            in_specs=[rows_spec(width, chunks)] * 3
-            + [halo_spec(width, chunks)] * 3
+            grid=(chunks // GROUP,),
+            in_specs=[rows_spec(width, chunks, False, GROUP)] * 3
+            + [halo_spec(width, chunks, False, GROUP)] * 3
             + [whole_spec(HALO, width)] * 3
-            + [rows_spec(128, chunks), whole_spec(16, width), whole_spec(8, 128)],
-            out_specs=[tile_spec(heads, chunks)] * 3
-            + [rows_spec(width, chunks)] * 4
-            + [tile_spec(heads, chunks)] * 2
+            + [rows_spec(128, chunks, False, GROUP), whole_spec(16, width), whole_spec(8, 128)],
+            out_specs=[tile_spec(heads, chunks, False, GROUP)] * 3
+            + [rows_spec(width, chunks, False, GROUP)] * 4
+            + [tile_spec(heads, chunks, False, GROUP)] * 2
             + [whole_spec(heads, 128, 256)],
             scratch_shapes=[pltpu.VMEM((heads, 128, 256), F32)],
         ),
@@ -382,15 +378,15 @@
     )(scalars, gm, out, gate, gain, qt, t, maps)
 
 
-def back_kernel(docs, heads, chunks, scalars, *refs):
+def back_kernel(docs, heads, steps, scalars, *refs):
     mains, priors, rims = refs[0:3], refs[3:6], refs[6:9]
     narrow_ref, taps_ref, params_ref, ds_in = refs[9:13]
     (do_ref, v2_ref, s_ref, x_ref, p_ref, kg_ref, w_ref, u_ref, qt_ref, t_ref) = refs[13:23]
     dgate_ref, grads_ref, tail_ref, rim_ref, gtaps_ref, gparams_ref = refs[23:29]
     run, after = refs[29:31]
     rev = pl.program_id(0)
-    step = chunks - 1 - rev
-    position = scalars[0] + step * CHUNK
+    step = steps - 1 - rev
+    position = scalars[0] + step * (CHUNK * GROUP)
 
     @pl.when(rev == 0)
     def _():
@@ -399,149 +395,162 @@
         gtaps_ref[...] = jnp.zeros_like(gtaps_ref)
         gparams_ref[...] = jnp.zeros_like(gparams_ref)
 
-    masks = chunk_masks(position, scalars, docs)
-    pieces, befores = load_pieces(step, mains, priors, rims)
     taps = taps_ref[...]
-    feats = features(pieces, befores, taps, masks, heads)
-    shifted, rate, decays, beta, total, total_row = gates(narrow_ref[...], params_ref[...], masks)
-    conv = [pre * sg for _, pre, sg in feats]
-    lane = masks["col"]
-    hs = range(heads)
-    q, k, v, uq, uk, terms, b = [], [], [], [], [], [], []
+    inputs = chunk_inputs(
+        step, position, mains, priors, rims, narrow_ref, taps, params_ref[...], scalars, docs, heads
+    )
+    lane, row = inputs[0][1]["col"], inputs[0][1]["row"]
+    items = [(j, h) for j in reversed(range(GROUP)) for h in range(heads)]
+    every = range(len(items))
+    q, k, v, uq, uk, cq, ck, terms, b, rows, masks = [], [], [], [], [], [], [], [], [], [], []
     root = 1.0 / math.sqrt(128.0)
-    for h in hs:
-        cq, ck = conv[0][:, lanes(h)], conv[1][:, lanes(h)]
-        uq.append(unit(cq))
-        uk.append(unit(ck))
-        q.append(cq * (uq[h] * root))
-        k.append(ck * uk[h])
-        v.append(conv[2][:, lanes(h)])
-        terms.append(decay_terms(h, total, total_row, masks))
+    for i, (j, h) in enumerate(items):
+        rows_j, masks_j, feats, (_, _, _, beta, total, total_row) = inputs[j]
+        conv = [pre[:, lanes(h)] * sg[:, lanes(h)] for _, pre, sg in feats]
+        cq.append(conv[0])
+        ck.append(conv[1])
+        uq.append(unit(conv[0]))
+        uk.append(unit(conv[1]))
+        q.append(conv[0] * (uq[i] * root))
+        k.append(conv[1] * uk[i])
+        v.append(conv[2])
+        terms.append(decay_terms(h, total, total_row, masks_j))
         b.append(beta[:, heads + h : heads + h + 1])
-    do = [do_ref[:, lanes(h)] for h in hs]
-    v2 = [v2_ref[:, lanes(h)] for h in hs]
-    dsn = [run[h] for h in hs]
-    kt = [terms[h][2] * k[h] for h in hs]
-    dv2 = [mm(p_ref[0, h], do[h], TN) + mm(kt[h], dsn[h]) for h in hs]
-    for h in hs:
-        left = jnp.concatenate([qt_ref[:, lanes(h)], t_ref[0, h]], axis=0)
-        run[h] = mm(left, jnp.concatenate([do[h], dsn[h]], axis=0), TN)
-    states = [s_ref[0, h] for h in hs]
-    both = [mm(jnp.concatenate([do[h], dv2[h]], axis=0), states[h], NT) for h in hs]
-    dp = [jnp.where(masks["inside"], mm(do[h], v2[h], NT), 0.0) for h in hs]
-    dkt = [mm(v2[h], dsn[h], NT) for h in hs]
-    dx = [mm(x_ref[0, h], jnp.concatenate([-both[h][128:], dv2[h]], axis=1), TN) for h in hs]
+        rows.append(rows_j)
+        masks.append(masks_j)
+    do = [do_ref[rows[i], lanes(h)] for i, (j, h) in enumerate(items)]
+    dsn = []
+    for i, (j, h) in enumerate(items):
+        dsn.append(run[h])
+        left = jnp.concatenate([qt_ref[rows[i], lanes(h)], t_ref[j, h]], axis=0)
+        run[h] = mm(left, jnp.concatenate([do[i], dsn[i]], axis=0), TN)
+    v2 = [v2_ref[rows[i], lanes(h)] for i, (j, h) in enumerate(items)]
+    kt = [terms[i][2] * k[i] for i in every]
+    dv2 = [mm(p_ref[j, h], do[i], TN) + mm(kt[i], dsn[i]) for i, (j, h) in enumerate(items)]
+    states = [s_ref[j, h] for j, h in items]
+    both = [mm(jnp.concatenate([do[i], dv2[i]], axis=0), states[i], NT) for i in every]
+    dp = [jnp.where(masks[i]["inside"], mm(do[i], v2[i], NT), 0.0) for i in every]
+    dkt = [mm(v2[i], dsn[i], NT) for i in every]
+    dx = [
+        mm(x_ref[j, h], jnp.concatenate([-both[i][128:], dv2[i]], axis=1), TN)
+        for i, (j, h) in enumerate(items)
+    ]
     da = [
         jnp.where(
-            masks["strict"],
-            -mm(dx[h], jnp.concatenate([w_ref[:, lanes(h)], u_ref[:, lanes(h)]], axis=1), NT),
+            masks[i]["strict"],
+            -mm(
+                dx[i],
+                jnp.concatenate([w_ref[rows[i], lanes(h)], u_ref[rows[i], lanes(h)]], axis=1),
+                NT,
+            ),
             0.0,
         )
-        for h in hs
+        for i, (j, h) in enumerate(items)
     ]
-    gdecay = jnp.zeros((CHUNK, CHUNK), F32)
-    gbeta = jnp.zeros((CHUNK, CHUNK), F32)
-    minus = jnp.zeros((CHUNK, CHUNK), F32)
+    zero = jnp.zeros((CHUNK, CHUNK), F32)
+    gdecay, gbeta, minus = [zero] * GROUP, [zero] * GROUP, [zero] * GROUP
     dq, dk, dv = [], [], []
-    for h in hs:
-        spread, start, to_last, keep = terms[h]
-        doq = both[h][:128]
-        dqk = dp[h] * spread
-        kgh = kg_ref[0, h]
-        z = da[h] * kgh
-        dkk = b[h] * da[h] * spread
-        dxk, dxv = dx[h][:, :128], dx[h][:, 128:]
+    for i, (j, h) in enumerate(items):
+        spread, start, to_last, keep = terms[i]
+        doq = both[i][:128]
+        dqk = dp[i] * spread
+        z = da[i] * kg_ref[j, h]
+        dkk = b[i] * da[i] * spread
+        dxk, dxv = dx[i][:, :128], dx[i][:, 128:]
         stacked = jnp.concatenate([dqk, dkk], axis=0)
-        forward = mm(stacked, k[h])
-        backward = mm(stacked, jnp.concatenate([q[h], k[h]], axis=0), TN)
-        kx = jnp.sum(k[h] * dxk, axis=-1, keepdims=True)
+        forward = mm(stacked, k[i])
+        backward = mm(stacked, jnp.concatenate([q[i], k[i]], axis=0), TN)
+        kx = jnp.sum(k[i] * dxk, axis=-1, keepdims=True)
         dq.append(start * doq + forward[:128])
-        dk.append(
-            backward + forward[128:] + to_last * dkt[h] + (b[h] * start) * dxk
-        )
-        dv.append(b[h] * dxv)
+        dk.append(backward + forward[128:] + to_last * dkt[i] + (b[i] * start) * dxk)
+        dv.append(b[i] * dxv)
         gb = (
             jnp.sum(z, axis=-1, keepdims=True)
-            + jnp.sum(v[h] * dxv, axis=-1, keepdims=True)
+            + jnp.sum(v[i] * dxv, axis=-1, keepdims=True)
             + start * kx
         )
-        gamgrad = b[h] * z + dp[h] * p_ref[0, h]
-        dstart = jnp.sum(q[h] * doq, axis=-1, keepdims=True) + b[h] * kx
-        dlast = jnp.sum(k[h] * dkt[h], axis=-1, keepdims=True) * to_last
-        dkeep = jnp.sum(states[h] * dsn[h], keepdims=True) * keep
+        gamgrad = b[i] * z + dp[i] * p_ref[j, h]
+        dstart = jnp.sum(q[i] * doq, axis=-1, keepdims=True) + b[i] * kx
+        dlast = jnp.sum(k[i] * dkt[i], axis=-1, keepdims=True) * to_last
+        dkeep = jnp.sum(states[i] * dsn[i], keepdims=True) * keep
         gcol = jnp.sum(gamgrad, axis=-1, keepdims=True) + dstart * start - dlast
         end = jnp.sum(dlast, keepdims=True) + dkeep
-        gcol = gcol + jnp.where(masks["row"][:, :1] == CHUNK - 1, end, 0.0)
+        gcol = gcol + jnp.where(row[:, :1] == CHUNK - 1, end, 0.0)
         grow = jnp.sum(gamgrad, axis=0, keepdims=True)
-        gdecay = jnp.where(lane == h, gcol, gdecay)
-        gbeta = jnp.where(lane == heads + h, gb, gbeta)
-        minus = jnp.where(masks["row"] == h, grow, minus)
-    gdecay = gdecay - minus.T
-    upper = jnp.where(masks["row"] <= masks["col"], 1.0, 0.0)
-    dg = mm_full(upper, gdecay)
-    galpha = dg * rate * jax.nn.sigmoid(shifted)
-    width = pieces[0].shape[1]
+        gdecay[j] = jnp.where(lane == h, gcol, gdecay[j])
+        gbeta[j] = jnp.where(lane == heads + h, gb, gbeta[j])
+        minus[j] = jnp.where(row == h, grow, minus[j])
+    upper = jnp.where(row <= lane, 1.0, 0.0)
+    width = mains[0].shape[1]
     grads_ref[:, 3 * width + 128 :] = dgate_ref[...]
-    grads_ref[:, 3 * width : 3 * width + 128] = jnp.where(
-        lane < heads, galpha, gbeta * beta * (1.0 - beta)
-    ).astype(LOW)
-    gparams_ref[0:8, :] += jnp.sum((galpha).reshape(CHUNK // 8, 8, 128), axis=0)
-    gparams_ref[8:16, :] += jnp.sum((dg * decays).reshape(CHUNK // 8, 8, 128), axis=0)
-
-    for i in range(3):
-        rows, pre, sg = feats[i]
-        pieces_d = []
-        for h in hs:
-            if i == 2:
-                pieces_d.append(dv[h])
-            else:
-                inv = uq[h] if i == 0 else uk[h]
-                grad = dq[h] * root if i == 0 else dk[h]
-                normal = conv[i][:, lanes(h)] * inv
-                pieces_d.append(
-                    inv * (grad - normal * jnp.sum(grad * normal, axis=-1, keepdims=True))
+    for j in reversed(range(GROUP)):
+        rows_j, masks_j, feats, (shifted, rate, decays, beta, _, _) = inputs[j]
+        dg = mm_full(upper, gdecay[j] - minus[j].T)
+        galpha = dg * rate * jax.nn.sigmoid(shifted)
+        grads_ref[rows_j, 3 * width : 3 * width + 128] = jnp.where(
+            lane < heads, galpha, gbeta[j] * beta * (1.0 - beta)
+        ).astype(LOW)
+        gparams_ref[0:8, :] += jnp.sum((galpha).reshape(CHUNK // 8, 8, 128), axis=0)
+        gparams_ref[8:16, :] += jnp.sum((dg * decays).reshape(CHUNK // 8, 8, 128), axis=0)
+        for i in range(3):
+            shift_rows, pre, sg = feats[i]
+            pieces_d = []
+            for h in range(heads):
+                at = items.index((j, h))
+                if i == 2:
+                    pieces_d.append(dv[at])
+                else:
+                    inv = uq[at] if i == 0 else uk[at]
+                    grad = dq[at] * root if i == 0 else dk[at]
+                    normal = (cq[at] if i == 0 else ck[at]) * inv
+                    pieces_d.append(
+                        inv * (grad - normal * jnp.sum(grad * normal, axis=-1, keepdims=True))
+                    )
+            dc = jnp.concatenate(pieces_d, axis=1)
+            ds = dc * (sg * (1.0 + pre * (1.0 - sg)))
+            grad = ds * taps[4 * i + 3 : 4 * i + 4, :]
+            rim = jnp.zeros((8, ds.shape[1]), F32)
+            gtaps_ref[4 * i + 3] += jnp.sum((ds * shift_rows[0]).reshape(CHUNK // 8, 8, -1), axis=0)
+            for s in range(1, 4):
+                tap = taps[4 * i + 3 - s : 4 * i + 4 - s, :]
+                masked = jnp.where(masks_j["back"][s], ds, 0.0)
+                gtaps_ref[4 * i + 3 - s] += jnp.sum(
+                    (ds * shift_rows[s]).reshape(CHUNK // 8, 8, -1), axis=0
                 )
-        dc = jnp.concatenate(pieces_d, axis=1)
-        ds = dc * (sg * (1.0 + pre * (1.0 - sg)))
-        grad = ds * taps[4 * i + 3 : 4 * i + 4, :]
-        rim = jnp.zeros((8, ds.shape[1]), F32)
-        gtaps_ref[4 * i + 3] += jnp.sum((ds * rows[0]).reshape(CHUNK // 8, 8, -1), axis=0)
-        for s in range(1, 4):
-            tap = taps[4 * i + 3 - s : 4 * i + 4 - s, :]
-            masked = jnp.where(masks["back"][s], ds, 0.0)
-            gtaps_ref[4 * i + 3 - s] += jnp.sum((ds * rows[s]).reshape(CHUNK // 8, 8, -1), axis=0)
-            ext = jnp.concatenate([masked, after[3 * i + s - 1]], axis=0)
-            grad = grad + pltpu.roll(ext, CHUNK + 8 - s, 0)[:CHUNK] * tap
-            after[3 * i + s - 1] = masked[:8]
-            front = jnp.concatenate([jnp.zeros_like(masked[:8]), masked[:8]], axis=0)
-            rim = rim + pltpu.roll(front, 16 - s, 0)[:8] * tap
-        grads_ref[:, i * width : (i + 1) * width] = grad.astype(LOW)
-        rim_ref[:, i * width : (i + 1) * width] = rim
-
-        @pl.when(rev == 0)
-        def _():
-            tail_ref[:, i * width : (i + 1) * width] = grad[CHUNK - HALO :]
+                ext = jnp.concatenate([masked, after[3 * i + s - 1]], axis=0)
+                grad = grad + pltpu.roll(ext, CHUNK + 8 - s, 0)[:CHUNK] * tap
+                after[3 * i + s - 1] = masked[:8]
+                front = jnp.concatenate([jnp.zeros_like(masked[:8]), masked[:8]], axis=0)
+                rim = rim + pltpu.roll(front, 16 - s, 0)[:8] * tap
+            grads_ref[rows_j, i * width : (i + 1) * width] = grad.astype(LOW)
+            if j == 0:
+                rim_ref[:, i * width : (i + 1) * width] = rim
+            if j == GROUP - 1:
+
+                @pl.when(rev == 0)
+                def _():
+                    tail_ref[:, i * width : (i + 1) * width] = grad[CHUNK - HALO :]
 
 
 def back(scalars, pieces, rims, narrow, taps, params, ds_in, do, v2, s, x, p, kg, w, u, qt, t, dgate, docs, heads):
     rows, width = pieces[0].shape
     chunks = rows // CHUNK
-    flat, tiles = rows_spec(width, chunks, True), tile_spec(heads, chunks, True)
+    flat, tiles = rows_spec(width, chunks, True, GROUP), tile_spec(heads, chunks, True, GROUP)
     return pl.pallas_call(
-        functools.partial(back_kernel, docs, heads, chunks),
+        functools.partial(back_kernel, docs, heads, chunks // GROUP),
         out_shape=(
             sds(rows, 4 * width + 128, dtype=LOW), sds(HALO, 3 * width), sds(8, 3 * width),
             sds(12, 8, width), sds(16, 128),
         ),
         grid_spec=pltpu.PrefetchScalarGridSpec(
             num_scalar_prefetch=1,
-            grid=(chunks,),
+            grid=(chunks // GROUP,),
             in_specs=[flat] * 3
-            + [halo_spec(width, chunks, True)] * 3
+            + [halo_spec(width, chunks, True, GROUP)] * 3
             + [whole_spec(HALO, width)] * 3
-            + [rows_spec(128, chunks, True), whole_spec(16, width), whole_spec(8, 128)]
+            + [rows_spec(128, chunks, True, GROUP), whole_spec(16, width), whole_spec(8, 128)]
             + [whole_spec(heads, 128, 128), flat, flat, tiles, tiles, tiles, tiles, flat, flat, flat, tiles, flat],
-            out_specs=[rows_spec(4 * width + 128, chunks, True)]
+            out_specs=[rows_spec(4 * width + 128, chunks, True, GROUP)]
             + [whole_spec(HALO, 3 * width), whole_spec(8, 3 * width)]
             + [whole_spec(12, 8, width), whole_spec(16, 128)],
             scratch_shapes=[pltpu.VMEM((heads, 128, 128), F32), pltpu.VMEM((9, 8, width), F32)],
@@ -648,14 +657,16 @@
         def _():
             first()
 
-        @pl.when(low >= 0)
-        def _():
-            use(low)
-
-        @pl.when((step > 0) & (high < parts))
-        def _():
-            use(high)
-
+        def visit(side, _):
+            piece = me + step * (2 * side - 1)
+
+            @pl.when((piece >= 0) & (piece < parts) & ((step > 0) | (side == 0)))
+            def _():
+                use(piece)
+
+            return 0
+
+        lax.fori_loop(0, 2, visit, 0)
         return 0
 
     lax.fori_loop(0, parts, body, 0)
@@ -763,13 +774,20 @@
     )(tokens, gain, narrow_w, *weights)
 
 
+SUBS = 2
+FEED_SUBS = 4
+
+
 def feed_kernel(parts, res_ref, gain_ref, *refs):
     weights_in, og_in = refs[0:3], refs[3]
-    all_ref, act_ref, gu_ref, mlp_ref = refs[4:8]
-    buf, weights, og = refs[8], refs[9:12], refs[12]
-    sems, load_sem, store_sem = refs[13:17], refs[17], refs[18]
+    mlp_ref, out_ref, grads_ref = refs[4:7]
+    buf, weights, og, sent, got = refs[7], refs[8:11], refs[11], refs[12], refs[13]
+    sems, load_sem = refs[14:18], refs[18]
+    sem_sr, sem_sl, sem_gl, sem_gr = refs[19:23]
+    act_ref, gu_ref, stage, stage_sem = refs[23:27]
     me = lax.axis_index("tensor")
-    rows = res_ref.shape[0]
+    rows, model = res_ref.shape
+    size = rows // FEED_SUBS
     units = weights_in[0].shape[1]
     loads = [
         pltpu.make_async_copy(src, dst, load_sem.at[i])
@@ -785,12 +803,31 @@
         for load in loads:
             load.wait()
 
-    def stored(piece):
-        at = pl.ds(pl.multiple_of(piece * rows, rows), rows)
-        return pltpu.make_async_copy(buf.at[piece], all_ref.at[at, :], store_sem.at[piece])
-
-    def tile(at, piece, column, size):
-        cols = pl.ds(pl.multiple_of(column, 128), size)
+    def rightward(piece, sub):
+        slot = piece * FEED_SUBS + sub
+        return pltpu.make_async_remote_copy(
+            src_ref=sent.at[slot],
+            dst_ref=got.at[slot],
+            send_sem=sem_sr.at[slot],
+            recv_sem=sem_gl.at[slot],
+            device_id={"tensor": me + 1},
+            device_id_type=MESH,
+        )
+
+    def leftward(piece, sub, to):
+        slot = piece * FEED_SUBS + sub
+        landing = jnp.where(piece == to, parts * FEED_SUBS + sub, slot)
+        return pltpu.make_async_remote_copy(
+            src_ref=sent.at[slot],
+            dst_ref=got.at[landing],
+            send_sem=sem_sl.at[slot],
+            recv_sem=sem_gr.at[slot],
+            device_id={"tensor": me - 1},
+            device_id_type=MESH,
+        )
+
+    def tile(at, piece, column, wide):
+        cols = pl.ds(pl.multiple_of(column, 128), wide)
         values = buf[piece]
         gate = dot(values, wg[:, cols])
         up = dot(values, wu[:, cols])
@@ -799,11 +836,10 @@
         act = gate * sg
         act_ref[at, cols] = (act * up).astype(LOW)
         gu_ref[at, cols] = (grad * up * sg * (1.0 + gate * (1.0 - sg))).astype(LOW)
-        gu_ref[at, pl.ds(pl.multiple_of(units + column, 128), size)] = (grad * act).astype(LOW)
+        gu_ref[at, pl.ds(pl.multiple_of(units + column, 128), wide)] = (grad * act).astype(LOW)
 
     def use(piece):
         at = pl.ds(pl.multiple_of(piece * rows, rows), rows)
-        stored(piece).start()
 
         def body(i, _):
             tile(at, piece, i * 256, 256)
@@ -813,42 +849,176 @@
         if units % 256:
             tile(at, piece, units - units % 256, units % 256)
 
-        def down(i, _):
-            cols = pl.ds(pl.multiple_of(i * 256, 256), 256)
-            mlp_ref[at, cols] = dot(act_ref[at, :], wd[:, cols]).astype(LOW)
+        def product(j, _):
+            cols = pl.ds(pl.multiple_of(j * 256, 256), 256)
+            total = contract_cols(gu_ref[at, :units], wg[cols, :])
+            total = total + contract_cols(gu_ref[at, units:], wu[cols, :])
+
+            @pl.when(piece == me)
+            def _():
+                out_ref[:, cols] = total
+
+            @pl.when(piece != me)
+            def _():
+                for sub in range(FEED_SUBS):
+                    sent[piece * FEED_SUBS + sub, :, cols] = total[sub * size : sub * size + size].astype(LOW)
+
             return 0
 
-        lax.fori_loop(0, mlp_ref.shape[1] // 256, down, 0)
+        lax.fori_loop(0, model // 256, product, 0)
+
+        @pl.when((piece > me) & (me == 0))
+        def _():
+            for sub in range(FEED_SUBS):
+                rightward(piece, sub).start()
+
+        @pl.when((piece < me) & (me == parts - 1))
+        def _():
+            for sub in range(FEED_SUBS):
+                leftward(piece, sub, me - 1).start()
 
     line_gather(parts, buf, sems, first, use)
-    for piece in range(parts):
-        stored(piece).wait()
+
+    def down(item, _):
+        piece, i = item // (model // 256), item % (model // 256)
+        at = pl.ds(pl.multiple_of(piece * rows, rows), rows)
+        cols = pl.ds(pl.multiple_of(i * 256, 256), 256)
+        mlp_ref[at, cols] = dot(act_ref[at, :], wd[:, cols]).astype(LOW)
+        return 0
+
+    lax.fori_loop(0, parts * (model // 256), down, 0)
+    talls = model // 256
+    tiles = 3 * talls
+
+    def staged(tile):
+        at = pl.ds(pl.multiple_of((tile % talls) * 256, 256), 256)
+        cols = pl.ds(pl.multiple_of((tile // talls) * units, 128), units)
+        return pltpu.make_async_copy(
+            stage.at[tile % 2], grads_ref.at[at, cols], stage_sem.at[tile % 2]
+        )
+
+    def grad_tile(tile):
+        column = tile // talls
+        over = pl.ds(pl.multiple_of((tile % talls) * 256, 256), 256)
+
+        @pl.when(tile >= 2)
+        def _():
+            staged(tile - 2).wait()
+
+        def summed(left, right):
+            total = None
+            for p in range(parts):
+                term = contract_rows(left(p), right(slice(p * rows, p * rows + rows)))
+                total = term if total is None else total + term
+            stage[tile % 2] = total.astype(LOW)
+
+        @pl.when(column < 2)
+        def _():
+            cols = pl.ds(pl.multiple_of(column * units, 128), units)
+            summed(lambda p: buf[p, :, over], lambda at: gu_ref[at, cols])
+
+        @pl.when(column == 2)
+        def _():
+            summed(lambda p: og[p * rows : p * rows + rows, over], lambda at: act_ref[at, :])
+
+        staged(tile).start()
+
+    turns = 2 * (parts - 1) * FEED_SUBS
+    per_turn = -(-tiles // turns)
+    right_first = 2 * me < parts
+
+    def pass_on(item, _):
+        turn = item // ((parts - 1) * FEED_SUBS)
+        rest = item % ((parts - 1) * FEED_SUBS)
+        step, sub = 1 + rest // FEED_SUBS, rest % FEED_SUBS
+        right = (turn == 0) == right_first
+        going_right = right & (me + step < parts) & (me > 0)
+        going_left = jnp.logical_not(right) & (me - step >= 0) & (me < parts - 1)
+
+        @pl.when(going_right)
+        def _():
+            piece = me + step
+            slot = piece * FEED_SUBS + sub
+            rightward(piece, sub).wait_recv()
+            sent[slot] = (sent[slot].astype(F32) + got[slot].astype(F32)).astype(LOW)
+            rightward(piece, sub).start()
+
+        @pl.when(going_left)
+        def _():
+            piece = me - step
+            slot = piece * FEED_SUBS + sub
+            leftward(piece, sub, me).wait_recv()
+            sent[slot] = (sent[slot].astype(F32) + got[slot].astype(F32)).astype(LOW)
+            leftward(piece, sub, me - 1).start()
+
+        for i in range(per_turn):
+            tile = item * per_turn + i
+            if per_turn * turns == tiles:
+                grad_tile(tile)
+            else:
+                pl.when(tile < tiles)(functools.partial(grad_tile, tile))
+        return 0
+
+    lax.fori_loop(0, turns, pass_on, 0)
+    for sub in range(FEED_SUBS):
+        at = slice(sub * size, sub * size + size)
+
+        @pl.when(me > 0)
+        def _():
+            rightward(me, sub).wait_recv()
+            out_ref[at, :] = out_ref[at, :] + got[me * FEED_SUBS + sub].astype(F32)
+
+        @pl.when(me < parts - 1)
+        def _():
+            leftward(me, sub, me).wait_recv()
+            out_ref[at, :] = out_ref[at, :] + got[parts * FEED_SUBS + sub].astype(F32)
+
+    def finish(slot, _):
+        piece, sub = slot // FEED_SUBS, slot % FEED_SUBS
+
+        @pl.when(piece > me)
+        def _():
+            rightward(piece, sub).wait_send()
+
+        @pl.when(piece < me)
+        def _():
+            leftward(piece, sub, me - 1).wait_send()
+
+        return 0
+
+    lax.fori_loop(0, parts * FEED_SUBS, finish, 0)
+    for slot in range(2):
+        staged(tiles - 2 + slot).wait()
 
 
 def feed(parts, residual, gain, weights, out_grad):
     rows, model = residual.shape
     units = weights[0].shape[1]
     total = rows * parts
+    low = sds(total, model, dtype=LOW)
     return pl.pallas_call(
         functools.partial(feed_kernel, parts),
-        out_shape=(
-            sds(total, model, dtype=LOW), sds(total, units, dtype=LOW), sds(total, 2 * units, dtype=LOW),
-            sds(total, model, dtype=LOW),
-        ),
+        out_shape=(low, sds(rows, model), sds(model, 3 * units, dtype=LOW)),
         in_specs=[vmem()] * 2 + [hbm()] * 4,
-        out_specs=[hbm()] + [vmem()] * 3,
+        out_specs=[vmem()] * 2 + [hbm()],
         scratch_shapes=[pltpu.VMEM((parts, rows, model), LOW)]
         + [pltpu.VMEM(w.shape, LOW) for w in weights]
         + [pltpu.VMEM((total, model), LOW)]
+        + [pltpu.VMEM((parts * FEED_SUBS, rows // FEED_SUBS, model), LOW)]
+        + [pltpu.VMEM((parts * FEED_SUBS + FEED_SUBS, rows // FEED_SUBS, model), LOW)]
         + line_sems(parts)
-        + [pltpu.SemaphoreType.DMA((4,)), pltpu.SemaphoreType.DMA((parts,))],
+        + [pltpu.SemaphoreType.DMA((4,))]
+        + line_sems(parts * FEED_SUBS)
+        + [
+            pltpu.VMEM((total, units), LOW),
+            pltpu.VMEM((total, 2 * units), LOW),
+            pltpu.VMEM((2, 256, units), LOW),
+            pltpu.SemaphoreType.DMA((2,)),
+        ],
         compiler_params=comm_params(2),
-        cost_estimate=cost(8 * total * model * units, 120 * 2**20),
+        cost_estimate=cost(18 * total * model * units, 120 * 2**20),
         name="feed",
     )(residual, gain, *weights, out_grad)
-
-
-SUBS = 2
 
 
 class Plain:
@@ -1062,13 +1232,22 @@
 
     half = part.at[pl.ds(0, size), :]
 
-    def go_right(piece, sub):
+    right_first = 2 * me < parts
+
+    def body(item, _):
+        step, sub = item // (2 * SUBS), (item // 2) % SUBS
+        right = (item % 2 == 0) == right_first
+        piece = jnp.where(right, parts - 1 - step, step)
         slot = piece * SUBS + sub
-
-        @pl.when(piece > me)
+        go_right = right & (piece > me)
+        go_left = jnp.logical_not(right) & (piece < me)
+
+        @pl.when(go_right | go_left)
         def _():
             product(piece * rows + sub * size, size, half)
 
+        @pl.when(go_right)
+        def _():
             @pl.when(me > 0)
             def _():
                 rightward(slot).wait_recv()
@@ -1080,13 +1259,8 @@
 
             rightward(slot).start()
 
-    def go_left(piece, sub):
-        slot = piece * SUBS + sub
-
-        @pl.when(piece < me)
-        def _():
-            product(piece * rows + sub * size, size, half)
-
+        @pl.when(go_left)
+        def _():
             @pl.when(me < parts - 1)
             def _():
                 leftward(slot).wait_recv()
@@ -1098,25 +1272,9 @@
 
             leftward(slot).start()
 
-    right_first = 2 * me < parts
-
-    def body(item, _):
-        step, sub = item // SUBS, item % SUBS
-        right, left = parts - 1 - step, step
-
-        @pl.when(right_first)
-        def _():
-            go_right(right, sub)
-
-        go_left(left, sub)
-
-        @pl.when(jnp.logical_not(right_first))
-        def _():
-            go_right(right, sub)
-
         return 0
 
-    lax.fori_loop(0, (parts - 1) * SUBS, body, 0)
+    lax.fori_loop(0, (parts - 1) * SUBS * 2, body, 0)
     product(me * rows, rows, part)
     for sub in range(SUBS):
         at = slice(sub * size, sub * size + size)
@@ -1374,7 +1532,7 @@
         return lax.dynamic_index_in_dim(split, index, 2, keepdims=False).reshape(rows_own, -1)
 
     residual = own_rows + (dot(of_core(core), out_mine) + dot(of_core(1 - core), out_other))
-    mid_all, activated, grad_units, mlp_part = feed(
+    mlp_part, grad_mid, units_grad = feed(
         tensor_parts, residual, gain_mid_rows, (w_gate, w_up, w_down), out_grad
     )
     units = w_gate.shape[1]
@@ -1387,17 +1545,7 @@
     def added(values, back_by, got):
         return (piece_of(values, back_by).astype(F32) + got.astype(F32)).astype(LOW)
 
-    mlp_run = lax.ppermute(piece_of(mlp_part, 1), "tensor", ring)
-    down_grad = contract_rows(out_grad, activated).astype(LOW)
-    units_grad = contract_rows(mid_all, after(grad_units, down_grad)).astype(LOW)
-    units_grad, mlp_run = lax.optimization_barrier((units_grad, mlp_run))
-    down_grad_sum = lax.psum_scatter(down_grad, "dp", scatter_dimension=0, tiled=True)
     units_grad_sum = lax.psum_scatter(units_grad, "dp", scatter_dimension=0, tiled=True)
-
-    (grad_mid,) = scatter(
-        tensor_parts, [after(grad_units, units_grad)], [w_gate, w_up],
-        ((0, 0, units), (0, units, units)), 4,
-    )
     grad_res_norm, gain_mid_grad = norm_back(residual, gain_mid, grad_mid)
     grad_own = lax.dynamic_slice_in_dim(out_grad, tensor_index * rows_own, rows_own, 0)
     grad_residual = grad_own.astype(F32) + grad_res_norm
@@ -1408,36 +1556,32 @@
     grad_mixed = lax.all_to_all(
         grad_mixed, "tensor", split_axis=2, concat_axis=0, tiled=True
     ).reshape(group_rows, width)
-    mlp_run = after(mlp_run, grad_mixed)
+    mlp_run = lax.ppermute(piece_of(after(mlp_part, grad_mixed), 1), "tensor", ring)
     out_w = contract_rows(after(grad_mixer, grad_mixed), mixed_own).astype(LOW)
     out_w_sum = lax.psum_scatter(out_w, "dp", scatter_dimension=0, tiled=True)
+    do, gate_low, head_gain_part, ds_total = inward(
+        scalars, grad_mixed, rows_out, gate_raw, gain_heads, qt, t, totals, heads
+    )
+    grad_end = exchange(dp_parts, ds_total, heads, True, 5)
+    grad_end, mlp_run = lax.optimization_barrier((grad_end, mlp_run))
     for back_by in range(2, tensor_parts - 1):
         mlp_run = lax.ppermute(added(mlp_part, back_by, mlp_run), "tensor", ring)
-
-    do, gate_low, head_gain_part, ds_total = inward(
-        scalars, grad_mixed, rows_out, gate_raw, gain_heads, qt, t, totals, heads
-    )
-    grad_end = exchange(dp_parts, ds_total, heads, True, 5)
-    grad_end, mlp_run, _, _ = lax.optimization_barrier(
-        (grad_end, mlp_run, units_grad_sum, down_grad_sum)
-    )
-    mlp_run = lax.ppermute(added(mlp_part, tensor_parts - 1, mlp_run), "tensor", ring)
     grads, tails, rim_grad, taps_grad, params_grad = back(
         scalars, pieces, rims, narrow, taps, params, grad_end, do, v2, s, x, p, kg, w, u, qt, t,
         gate_low, docs, heads,
     )
-    grads, tails, rim_grad, taps_grad, params_grad, mlp_run = lax.optimization_barrier(
-        (grads, tails, rim_grad, taps_grad, params_grad, mlp_run)
-    )
+    grads, tails, rim_grad, taps_grad, params_grad, mlp_run, units_grad_sum = (
+        lax.optimization_barrier(
+            (grads, tails, rim_grad, taps_grad, params_grad, mlp_run, units_grad_sum)
+        )
+    )
+    mlp_run = lax.ppermute(added(mlp_part, tensor_parts - 1, mlp_run), "tensor", ring)
     rim_back = lax.ppermute(rim_grad, "dp", [(i + 1, i) for i in range(dp_parts - 1)])
     tails = tails.at[HALO - 8 :].add(rim_back).astype(LOW)
     grads = lax.dynamic_update_slice(grads, tails, (group_rows - HALO, 0))
-    out_w_sum = lax.psum_scatter(
-        out_w_sum, "tensor", scatter_dimension=1, tiled=True
-    )
     mixer_grad = contract_rows(normed_all, grads).astype(LOW)
+    mixer_grad, mlp_run = lax.optimization_barrier((mixer_grad, mlp_run))
     mixer_sum = lax.psum_scatter(mixer_grad, "dp", scatter_dimension=0, tiled=True).astype(F32)
-    output = (residual + (piece_of(mlp_part, 0).astype(F32) + mlp_run.astype(F32))).astype(LOW)
     params_grad = params_grad.reshape(2, 8, 128).sum(1)
     flat = jnp.concatenate(
         [
@@ -1455,7 +1599,17 @@
         6, Closing(dp_parts, tensor_parts, 16, flat.shape),
         (tokens, gain_in_rows, grad_residual, flat),
     )
-    out_w_sum = after(out_w_sum, gain_in_grad).astype(F32)
+    out_w_sum, mlp_run, _ = lax.optimization_barrier((out_w_sum, mlp_run, gain_in_grad))
+    output = (residual + (piece_of(mlp_part, 0).astype(F32) + mlp_run.astype(F32))).astype(LOW)
+    def out_piece(ahead):
+        index = lax.rem(tensor_index + ahead, tensor_parts)
+        return lax.dynamic_slice_in_dim(out_w_dp, index * width, width, 1)
+
+    out_w_dp = out_w_sum
+    out_w_sum = out_piece(0).astype(F32)
+    for ahead in range(1, tensor_parts):
+        shift = [(i, (i + ahead) % tensor_parts) for i in range(tensor_parts)]
+        out_w_sum = out_w_sum + lax.ppermute(out_piece(ahead), "tensor", shift).astype(F32)
     by_head = wide[13:15].reshape(2, tensor_parts, width)[:, :, :heads].reshape(2, -1)
     start = 3 * width
     return (
@@ -1477,8 +1631,8 @@
         out_w_sum.T,
         rest[: model // width].reshape(model),
         units_grad_sum[:, :units].astype(F32),
-        units_grad_sum[:, units:].astype(F32),
-        down_grad_sum.T.astype(F32),
+        units_grad_sum[:, units : 2 * units].astype(F32),
+        units_grad_sum[:, 2 * units :].T.astype(F32),
     )
 
 

time: 724 us -> 688 us (0.950)
  matrix products: 63.9 us -> 35.5 us
  Pallas kernels: 484 us -> 463 us
  waiting for transfers between devices: 45.6 us -> 57.9 us
    pallas_call x2 -> x1, Pallas kernels: 181 us -> 93.1 us  [scatter(): pl.pallas_call(functools.partial(scatter_kernel, parts, len(lefts), count...]
    pallas_call x2, Pallas kernels: 126 us -> 191 us  [the longest x1 145 us: feed(): pl.pallas_call(functools.partial(feed_kernel, parts), out_shape=(low, sds...]
    dot_general x4 -> x2, matrix products: 50.2 us -> 21 us  [contract_rows(): return lax.dot_general(left, right, TN, preferred_element_type=F32)]
    ppermute x1, waiting for transfers between devices: 0.01 us -> 7.89 us  [local(): lax.ppermute(added(mlp_part, tensor_parts - 1, mlp_run), 'tensor', ring)]
    pallas_call x2, Pallas kernels: 38.1 us -> 45.6 us  [exchange(): pl.pallas_call(functools.partial(state_kernel, count, heads, backward), o...]
  transfers between devices with their start and end apart: 13 -> 14, of which waited for: 5 -> 7; matrix products, arithmetic and copies ran while one was open for 13% -> 12% of each run, Pallas kernels for 46% -> 36%
where the time goes in v5:
time: 688 us; the launch traced here: 677 us
  Pallas kernels  463 us (67%)
  waiting for transfers between devices  57.9 us (8%)
  local copies, waits for them, and re-layouts  38.5 us (6%)
  matrix products  35.5 us (5%)
  other arithmetic  25.2 us (4%)
  blocking collectives  23.8 us (3%)
  starting transfers between devices  19 us (3%)
  between operations  14.4 us (2%)
    pallas_call x1, Pallas kernels, feed(): pl.pallas_call(functools.partial(feed_kernel, parts), out_shape=(low, sds...  145 us
    pallas_call x1, Pallas kernels, scatter(): pl.pallas_call(functools.partial(scatter_kernel, parts, len(lefts), count...  93.1 us
    pallas_call x1, Pallas kernels, project(): pl.pallas_call(functools.partial(project_kernel, parts), out_shape=(sds(t...  75.1 us
    pallas_call x2, Pallas kernels, exchange(): pl.pallas_call(functools.partial(state_kernel, count, heads, backward), o...  45.6 us
    pallas_call x1, Pallas kernels, back(): pl.pallas_call(functools.partial(back_kernel, docs, heads, chunks // GROU...  45.2 us
    pallas_call x1, Pallas kernels, intra(): pl.pallas_call(functools.partial(intra_kernel, docs, heads), out_shape=(t...  35.4 us
    all_to_all x1, blocking collectives, local(): lax.all_to_all(grad_mixed, 'tensor', split_axis=2, concat_axis=0, tiled=T...  23.8 us
    all_to_all x1, waiting for transfers between devices, local(): lax.all_to_all(mixed, 'tensor', split_axis=0, concat_axis=1, tiled=True)  23.4 us
  transfers between devices with their start and end apart: 14, of which 7 were waited for; matrix products, arithmetic and copies ran while one was open for 12% of the time, Pallas kernels for 36%

profile of v5, /device:TPU:12, one launch (start us, length us, event | category | flops | bytes accessed | tf_op | source)
XLA Modules:
  0.0 677.1 jit_solution(10856679055170346037)
XLA Ops:
  10.7 75.1 %project.1 = (bf16[1024,2048]{1,0:T(8,128)(2,1)}, bf16[1024,512]{1,0:T(8,128)(2,1)}, bf16[1024,512]{1,0:T(8,128)(2,1)}, bf16[1024,512]{1,0:T(8,128)(2,1)}, f32[1024,512]{1,0:T(8,128)}, /*index=5*/f32[1024,128]{1,0:T(8,128)}) custom-call(bf16[256,2048]{1,0:T(8,128)(2,1)} %refs_6_.1, f32[8,2048]{1,0:T(8,128)} %broadcast_in_dim.10.gain_ref.refs_7_, ...), custom_call_target="tpu_custom_call" | custom-call | flops 9126805504 | bytes 62914560 | tf_op jit(solution)/shard_map/project/pallas_call | solution.py:762
  88.5 2.1 collective-permute-start
  92.4 2.4 collective-permute-done
  95.4 35.4 %intra.1 = (f32[8,4,128,128]{3,2,1,0:T(8,128)}, f32[8,4,128,128]{3,2,1,0:T(8,128)}, f32[8,4,128,128]{3,2,1,0:T(8,128)}, f32[1024,512]{1,0:T(8,128)}, f32[1024,51...) custom-call(s32[6]{0:T(128)} %pad_add_fusion.scalars, ...), custom_call_target="tpu_custom_call" | custom-call | flops 24159191040 | bytes 62914560 | tf_op jit(solution)/shard_map/intra/pallas_call | solution.py:255
  130.8 16.2 %exchange3.1.s_in = f32[4,128,128]{2,1,0:T(8,128)} custom-call(f32[4,128,256]{2,1,0:T(8,128)} %get-tuple-element.114.own_ref.maps_ref), custom_call_target="tpu_custom_call" | custom-call | flops 402653184 | bytes 4194304 | tf_op jit(solution)/shard_map/exchange3/pallas_call | solution.py:1443
  147.6 11.5 %outward.1 = (f32[1024,512]{1,0:T(8,128)}, f32[1024,512]{1,0:T(8,128)}, f32[8,4,128,128]{3,2,1,0:T(8,128)}, bf16[1024,512]{1,0:T(8,128)(2,1)}) custom-call(f32[4,128,128]{2,1,0:T(8,128)} %exchange3.1.s_in, f32[1024,512]{1,0:T(8,128)} %get-tuple-element.115.w_ref.refs_19_, f32[1024,512]{1,0:T(8,128)} %get-tuple-element.116.u_ref.refs_20_, ...), custom_call_target="tpu_custom_call" | custom-call | flops 1207959552 | bytes 23068672 | tf_op jit(solution)/shard_map/outward/pallas_call | solution.py:311
  159.1 9.9 %all-gather.3.cloned.1.call-done = bf16[1024,2048]{1,0:T(8,128)(2,1)} async-done(((bf16[256,2048]{1,0:T(8,128)(2,1)}), bf16[1024,2048]{1,0:T(8,128)(2,1)}) %all-gather.3.cloned.1.call-update) | async-done | bytes 4194320 | tf_op jit(solution)/shard_map/all_gather | solution.py:1512
  169.1 2.3 copy.65
  171.3 6.5 all-to-all-start
  177.8 23.4 %all-to-all-done = bf16[4,256,512]{1,2,0:T(8,128)(2,1)S(1)} async-done(((bf16[4,256,512]{1,2,0:T(8,128)(2,1)}), bf16[4,256,512]{1,2,0:T(8,128)(2,1)S(1)}, u32[]{:S(2)}, u32[]{:S(2)}) %all-to-all-start) | async-done | bytes 1048608 | tf_op jit(solution)/shard_map/all_to_all | solution.py:1524
  201.3 3.5 fusion.7
  204.9 4.9 multiply_reduce_fusion.2
  210.4 145.5 %feed.1 = (bf16[1024,2048]{1,0:T(8,128)(2,1)}, f32[256,2048]{1,0:T(8,128)}, bf16[2048,4224]{1,0:T(8,128)(2,1)}) custom-call(f32[256,2048]{1,0:T(8,128)} %get-tuple-element.271.res_ref, f32[8,2048]{1,0:T(8,128)} %broadcast_in_dim.13.gain_ref, bf16[2048,1408]{1,0:T(8,128)(2,1)} %refs_0_.3, bf16[2048,1408]{1,0:T(8,128)(2,1)} %refs_1_.4, ...), custom_call_target="tpu_custom_call" | custom-call | flops 53150220288 | bytes 125829120 | tf_op jit(solution)/shard_map/feed/pallas_call | solution.py:999
  357.5 2.3 multiply_reduce_fusion
  359.8 3.2 fusion.2
  363.0 4.8 convolution_convert_fusion.2
  370.8 2.8 reshape.214
  373.6 2.3 copy.66
  375.9 23.8 %all_to_all.34 = bf16[256,2,4,256]{3,1,0,2:T(2,128)(2,1)S(1)} all-to-all(bf16[256,2,4,256]{3,1,0,2:T(2,128)(2,1)S(1)} %copy.66), channel_id=1, replica_groups=mesh['dp'=8,'tensor'=4] {'tensor'}, dimensions={2} | all-to-all | bytes 2097152 | tf_op jit(solution)/shard_map/all_to_all | solution.py:1556
  400.9 5.7 convolution_convert_fusion.1
  408.6 11.4 %inward.1 = (f32[1024,512]{1,0:T(8,128)}, bf16[1024,512]{1,0:T(8,128)(2,1)}, f32[8,512]{1,0:T(8,128)}, f32[4,128,256]{2,1,0:T(8,128)}) custom-call(s32[6]{0:T(128)} %pad_add_fusion.scalars, bf16[1024,512]{1,0:T(8,128)(2,1)} %bitcast.63, f32[1024,512]{1,0:T(8,128)} %get-tuple-element.129.out_ref, f32[1024,512]{1,0:T(8,128)} %get-tuple-element.121.gate_ref, ...), custom_call_target="tpu_custom_call" | custom-call | flops 805306368 | bytes 14680064 | tf_op jit(solution)/shard_map/inward/pallas_call | solution.py:365
  420.1 29.4 %exchange5.1.refs_12_ = f32[4,128,128]{2,1,0:T(8,128)} custom-call(f32[4,128,256]{2,1,0:T(8,128)} %get-tuple-element.130.own_ref), custom_call_target="tpu_custom_call" | custom-call | flops 402653184 | bytes 4194304 | tf_op jit(solution)/shard_map/exchange5/pallas_call | solution.py:1443
  449.5 3.0 add_convert_fusion.2
  454.3 45.2 %back.1 = (bf16[1024,2176]{1,0:T(8,128)(2,1)}, f32[16,1536]{1,0:T(8,128)}, f32[8,1536]{1,0:T(8,128)}, f32[12,8,512]{2,1,0:T(8,128)}, f32[16,128]{1,0:T(8,128)}) custom-call(s32[6]{0:T(128)} %pad_add_fusion.scalars, bf16[1024,512]{1,0:T(8,128)(2,1)} %get-tuple-element.110.refs_0_.refs_3_, bf16[1024,512]{1,0:T(8,128)(2,1)} %get-tuple-element.111.refs_1_.refs_4_, ...), custom_call_target="tpu_custom_call" | custom-call | flops 8053063680 | bytes 33554432 | tf_op jit(solution)/shard_map/back/pallas_call | solution.py:539
  501.6 2.8 add_convert_fusion.1
  507.2 15.3 %convolution_convert_fusion = bf16[2048,2176]{1,0:T(8,128)(2,1)} fusion(bf16[1024,2048]{1,0:T(8,128)(2,1)} %get-tuple-element.128, bf16[1024,2176]{1,0:T(8,128)(2,1)} %convert_dynamic-update-slice_fusion.refs_0_), kind=kOutput, calls=%fused_computation | convolution fusion | flops 9131261952 | bytes 17563648 | tf_op jit(solution)/shard_map/dot_general | solution.py:565
  522.4 7.9 %collective-permute-done.5 = bf16[256,2048]{1,0:T(8,128)(2,1)S(1)} collective-permute-done((bf16[256,2048]{1,0:T(8,128)(2,1)}, bf16[256,2048]{1,0:T(8,128)(2,1)S(1)}, u32[]{:S(2)}, u32[]{:S(2)}) %collective-permute-start.5) | collective-permute-done | bytes 1048608 | tf_op jit(solution)/shard_map/ppermute | solution.py:1578
  532.0 3.4 convert_bitcast_fusion
  539.0 93.1 %scatter6.1 = (f32[256,2048]{1,0:T(8,128)}, f32[16,2048]{1,0:T(8,128)}, f32[8,512]{1,0:T(8,128)}, f32[8,256]{1,0:T(8,128)}) custom-call(bf16[1024,2176]{1,0:T(8,128)(2,1)} %convert_dynamic-update-slice_fusion.refs_0_, bf16[2048,512]{1,0:T(8,128)(2,1)} %refs_1_.5, bf16[2048,512]{1,0:T(8,128)(2,1)} %refs_2_.5, bf16[2048,512]{1,0:T(8,128)(2,1)} %refs_3_.5, ...), custom_call_target="tpu_custom_call" | custom-call | flops 9126805504 | bytes 62914560 | tf_op jit(solution)/shard_map/scatter6/pallas_call | solution.py:1320
  643.4 2.6 add_convert_fusion
  646.7 11.3 %collective-permute-done.6 = bf16[256,512]{1,0:T(8,128)(2,1)S(1)} collective-permute-done((bf16[256,512]{1,0:T(8,128)(2,1)S(1)}, bf16[256,512]{1,0:T(8,128)(2,1)S(1)}, u32[]{:S(2)}, u32[]{:S(2)}) %collective-permute-start.6) | collective-permute-done | bytes 262176 | tf_op jit(solution)/shard_map/ppermute | solution.py:1612
  665.3 2.8 fusion.3
  (124 shorter events, 50.9 us)
Async XLA Ops:
  7.2 78.7 %copy-start = (bf16[512,2048]{1,0:T(8,128)(2,1)S(1)}, bf16[512,2048]{1,0:T(8,128)(2,1)}, u32[]{:S(2)}) copy-start(bf16[512,2048]{1,0:T(8,128)(2,1)} %param.41) | copy-start | bytes 6291460
  7.2 161.9 %all-gather.3.cloned.1.call-start = ((), (), s32[]{:S(2)}) async-start(), calls=%async_computation.8 | async-start | bytes 5242880 | tf_op jit(solution)/shard_map/all_gather | solution.py:1512
  85.8 4.8 copy-start.23
  85.8 5.1 copy-start.15
  85.8 5.1 copy-start.16
  85.8 5.1 copy-start.17
  85.9 6.3 copy-start.20
  85.9 6.3 copy-start.21
  88.5 6.3 collective-permute-start
  95.4 51.6 %copy-start.19 = (f32[512]{0:T(512)S(1)}, f32[512]{0:T(512)}, u32[]{:S(2)}) copy-start(f32[512]{0:T(512)} %param.40) | copy-start | bytes 6148
  169.1 35.8 %collective-permute-start.1 = (bf16[4,256,2048]{2,1,0:T(8,128)(2,1)}, bf16[4,256,2048]{2,1,0:T(8,128)(2,1)}, u32[]{:S(2)}, u32[]{:S(2)}) collective-permute-start(bf16[4,256,2048]{2,1,0:T(8,128)(2,1)} %bitcast.75), channel_id=1, source_target_pairs={{0,4},{4,0},{8,12},{12,8},{16,20},{20,16},{24,28},{28,24},{1,5},{5... | collective-permute-start | bytes 12582920 | tf_op jit(solution)/shard_map/ppermute | solution.py:1526
  171.3 29.9 %all-to-all-start = ((bf16[4,256,512]{1,2,0:T(8,128)(2,1)}), bf16[4,256,512]{1,2,0:T(8,128)(2,1)S(1)}, u32[]{:S(2)}, u32[]{:S(2)}) async-start(bf16[4,256,512]{1,2,0:T(8,128)(2,1)} %copy.65), calls=%async_computation | async-start | bytes 2097152 | tf_op jit(solution)/shard_map/all_to_all | solution.py:1524
  177.8 321.7 %reduce-scatter.6.cloned.1.call-start = ((), (), s32[]{:S(2)}) async-start(), calls=%async_computation.6 | async-start | bytes 19464192 | tf_op jit(solution)/shard_map/reduce_scatter | solution.py:1548
  201.3 3.6 copy-start.9
  204.8 4.9 copy-start.13
  355.9 282.5 %reduce-scatter.4.cloned.1.call-start = ((), (), s32[]{:S(2)}) async-start(), calls=%async_computation.5 | async-start | bytes 9437184 | tf_op jit(solution)/shard_map/reduce_scatter | solution.py:1561
  363.0 4.8 copy-start.4
  363.0 5.5 copy-start.22
  375.9 25.0 %copy-start.5 = (bf16[256,2048]{1,0:T(8,128)(2,1)S(1)}, bf16[256,2048]{1,0:T(8,128)(2,1)}, u32[]{:S(2)}) copy-start(bf16[256,2048]{1,0:T(8,128)(2,1)} %copy-done.4) | copy-start | bytes 3145732
  406.6 256.3 %reduce-scatter.8.cloned.1.call-start = ((), (), s32[]{:S(2)}) async-start(), calls=%async_computation.7 | async-start | bytes 10027008 | tf_op jit(solution)/shard_map/reduce_scatter | solution.py:1584
  408.1 41.4 %collective-permute-start.2 = (bf16[256,2048]{1,0:T(8,128)(2,1)S(1)}, bf16[256,2048]{1,0:T(8,128)(2,1)}, u32[]{:S(2)}, u32[]{:S(2)}) collective-permute-start(bf16[256,2048]{1,0:T(8,128)(2,1)S(1)} %constant_dynamic-slice_fusion.3), channel_id=1, source_target_pairs={{0,1},{1,2},{2,3},{3,0},{4,5},{5,6},{6,7},{7,4},{8,9},{9,10},{10,1... | collective-permute-start | bytes 3145736 | tf_op jit(solution)/shard_map/ppermute | solution.py:1559
  452.5 47.0 %collective-permute-start.3 = (bf16[256,2048]{1,0:T(8,128)(2,1)}, bf16[256,2048]{1,0:T(8,128)(2,1)S(1)}, u32[]{:S(2)}, u32[]{:S(2)}) collective-permute-start(bf16[256,2048]{1,0:T(8,128)(2,1)} %add_convert_fusion.2), channel_id=1, source_target_pairs={{0,1},{1,2},{2,3},{3,0},{4,5},{5,6},{6,7},{7,4},{8,9},{9,10},{10,1... | collective-permute-start | bytes 3145736 | tf_op jit(solution)/shard_map/ppermute | solution.py:1568
  499.5 7.0 %copy-start.10 = (f32[16,1536]{1,0:T(8,128)S(1)}, f32[16,1536]{1,0:T(8,128)}, u32[]{:S(2)}) copy-start(f32[16,1536]{1,0:T(8,128)} %get-tuple-element.148) | copy-start | bytes 294916
  499.5 7.0 %collective-permute-start.4 = (f32[8,1536]{1,0:T(8,128)}, f32[8,1536]{1,0:T(8,128)S(1)}, u32[]{:S(2)}, u32[]{:S(2)}) collective-permute-start(f32[8,1536]{1,0:T(8,128)} %get-tuple-element.149), channel_id=1, source_target_pairs={{4,0},{8,4},{12,8},{16,12},{20,16},{24,20},{28,24},{5,1},{9,5},{13... | collective-permute-start | bytes 147464 | tf_op jit(solution)/shard_map/ppermute | solution.py:1579
  504.4 25.9 %collective-permute-start.5 = (bf16[256,2048]{1,0:T(8,128)(2,1)}, bf16[256,2048]{1,0:T(8,128)(2,1)S(1)}, u32[]{:S(2)}, u32[]{:S(2)}) collective-permute-start(bf16[256,2048]{1,0:T(8,128)(2,1)} %add_convert_fusion.1), channel_id=1, source_target_pairs={{0,1},{1,2},{2,3},{3,0},{4,5},{5,6},{6,7},{7,4},{8,9},{9,10},{10,1... | collective-permute-start | bytes 3145736 | tf_op jit(solution)/shard_map/ppermute | solution.py:1578
  522.4 8.9 %copy-start.14 = (f32[8,512]{1,0:T(8,128)S(1)}, f32[8,512]{1,0:T(8,128)}, u32[]{:S(2)}) copy-start(f32[8,512]{1,0:T(8,128)} %get-tuple-element.155) | copy-start | bytes 49156
  522.4 8.9 %copy-start.11 = (f32[12,8,512]{2,1,0:T(8,128)S(1)}, f32[12,8,512]{2,1,0:T(8,128)}, u32[]{:S(2)}) copy-start(f32[12,8,512]{2,1,0:T(8,128)} %get-tuple-element.154) | copy-start | bytes 589828
  632.2 11.2 %copy-start.8 = (bf16[256,2048]{1,0:T(8,128)(2,1)S(1)}, bf16[256,2048]{1,0:T(8,128)(2,1)}, u32[]{:S(2)}) copy-start(bf16[256,2048]{1,0:T(8,128)(2,1)} %copy-done.7) | copy-start | bytes 3145732
  639.6 18.4 %collective-permute-start.6 = (bf16[256,512]{1,0:T(8,128)(2,1)S(1)}, bf16[256,512]{1,0:T(8,128)(2,1)S(1)}, u32[]{:S(2)}, u32[]{:S(2)}) collective-permute-start(bf16[256,512]{1,0:T(8,128)(2,1)S(1)} %get-tuple-element.257), channel_id=1, source_target_pairs={{0,1},{1,2},{2,3},{3,0},{4,5},{5,6},{6,7},{7,4},{8,9},{9,10},{10,1... | collective-permute-start | bytes 786440 | tf_op jit(solution)/shard_map/ppermute | solution.py:1612
  640.3 18.6 %collective-permute-start.8 = (bf16[256,512]{1,0:T(8,128)(2,1)S(1)}, bf16[256,512]{1,0:T(8,128)(2,1)S(1)}, u32[]{:S(2)}, u32[]{:S(2)}) collective-permute-start(bf16[256,512]{1,0:T(8,128)(2,1)S(1)} %get-tuple-element.258), channel_id=1, source_target_pairs={{0,3},{1,0},{2,1},{3,2},{4,7},{5,4},{6,5},{7,6},{8,11},{9,8},{10,9... | collective-permute-start | bytes 786440 | tf_op jit(solution)/shard_map/ppermute | solution.py:1612
  641.7 4.4 copy-start.12
  641.7 19.2 %collective-permute-start.7 = (bf16[256,512]{1,0:T(8,128)(2,1)S(1)}, bf16[256,512]{1,0:T(8,128)(2,1)S(1)}, u32[]{:S(2)}, u32[]{:S(2)}) collective-permute-start(bf16[256,512]{1,0:T(8,128)(2,1)S(1)} %get-tuple-element.259), channel_id=1, source_target_pairs={{0,2},{1,3},{2,0},{3,1},{4,6},{5,7},{6,4},{7,5},{8,10},{9,11},{10,... | collective-permute-start | bytes 786440 | tf_op jit(solution)/shard_map/ppermute | solution.py:1612
  (6 other events, 13.0 us)
Sparse Core Ops, SparseCore 0:
  87.1 81.8 all-gather.2
  356.0 128.8 reduce-scatter.5
  488.8 73.5 reduce-scatter.3
  565.8 75.1 reduce-scatter.7

commit v6 on v5

--- a/solution.py
+++ b/solution.py
@@ -1030,6 +1030,12 @@
     def begin(self, given, scratch):
         greet("tensor", self.parts)
 
+    def tile(self, at, cols, total, given, scratch):
+        pass
+
+    def middle(self, given, scratch):
+        pass
+
     def end(self, given, out, scratch):
         pass
 
@@ -1111,21 +1117,36 @@
         each(self.count, dp, hello("dp"))
         each(self.parts, z, hello("tensor"))
         first = self.stages(scratch)[0]
-        first.buf[dp] = given[3][...]
+        first.buf[dp] = given[2][...]
+        scratch[12][...] = jnp.zeros_like(scratch[12])
         pl.semaphore_wait(barrier, self.count + self.parts - 2)
         first.send()
 
-    def end(self, given, out, scratch):
-        tok_ref, gain_ref, res_ref, flat_ref = given
-        out_ref, wide_ref, rest_ref, gain_out = out
+    def tile(self, at, cols, total, given, scratch):
+        terms = total * given[3][at, cols].astype(F32)
+        scratch[12][:, cols] += jnp.sum(terms.reshape(terms.shape[0] // 8, 8, -1), axis=0)
+
+    def middle(self, given, scratch):
         dp, z = lax.axis_index("dp"), lax.axis_index("tensor")
         flat_dp, flat_z, gain_dp, gain_z = self.stages(scratch)
-        sums = scratch[12]
-        rows, model = out_ref.shape
+        total = jnp.sum(scratch[12][...], axis=0, keepdims=True) / given[1][0:1, :]
+        wide = total.shape[1] // 8
+        gain_dp.buf[dp] = jnp.concatenate(
+            [total[:, i * wide : (i + 1) * wide] for i in range(8)], axis=0
+        )
+        gain_dp.send()
         flat_dp.receive()
         flat_z.buf[z] = flat_dp.sum()
         flat_z.send()
-        sums[...] = jnp.zeros_like(sums)
+        gain_dp.receive()
+        gain_z.buf[z] = gain_dp.sum()
+        gain_z.send()
+
+    def end(self, given, out, scratch):
+        tok_ref, gain_ref, flat_ref, _ = given
+        out_ref, wide_ref, rest_ref, gain_out = out
+        flat_dp, flat_z, gain_dp, gain_z = self.stages(scratch)
+        rows, model = out_ref.shape
 
         def body(i, _):
             at = pl.ds(pl.multiple_of(i * 32, 32), 32)
@@ -1133,27 +1154,15 @@
             inv = lax.rsqrt(jnp.mean(values * values, axis=-1, keepdims=True) + epsilon)
             scaled = grad * gain_ref[0:1, :]
             inner = jnp.mean(scaled * values, axis=-1, keepdims=True)
-            out_ref[at, :] = (
-                res_ref[at, :] + inv * scaled - values * (inner * inv * inv * inv)
-            )
-            sums[...] += jnp.sum((grad * values * inv).reshape(4, 8, model), axis=0)
+            out_ref[at, :] = inv * scaled - values * (inner * inv * inv * inv)
             return 0
 
         lax.fori_loop(0, rows // 32, body, 0)
-        total = jnp.sum(sums[...], axis=0, keepdims=True)
-        wide = model // 8
-        gain_dp.buf[dp] = jnp.concatenate(
-            [total[:, i * wide : (i + 1) * wide] for i in range(8)], axis=0
-        )
-        gain_dp.send()
         flat_z.receive()
         width = flat_ref.shape[1]
         for i in range(self.parts):
             wide_ref[:, i * width : (i + 1) * width] = flat_z.buf[i, : self.kept, :]
         rest_ref[...] = flat_z.sum(slice(self.kept, None))
-        gain_dp.receive()
-        gain_z.buf[z] = gain_dp.sum()
-        gain_z.send()
         gain_z.receive()
         gain_out[...] = gain_z.sum()
         for stage in (flat_dp, flat_z, gain_dp, gain_z):
@@ -1226,6 +1235,7 @@
                 term = contract_cols(lefts[index][at, first : first + wide], rights[i][cols, :])
                 total = term if total is None else total + term
             target[:, cols] = total
+            ending.tile(at, cols, total, extra_in, extra)
             return 0
 
         lax.fori_loop(0, model // 256, body, 0)
@@ -1276,6 +1286,7 @@
 
     lax.fori_loop(0, (parts - 1) * SUBS * 2, body, 0)
     product(me * rows, rows, part)
+    ending.middle(extra_in, extra)
     for sub in range(SUBS):
         at = slice(sub * size, sub * size + size)
         slot = me * SUBS + sub
@@ -1502,8 +1513,8 @@
     w_narrow = jnp.pad(jnp.concatenate([w_alpha, w_beta], axis=1), ((0, 0), (0, 128 - 2 * heads)))
 
     own_rows = tokens.astype(F32)
-    gain_in_rows = jnp.broadcast_to(gain_in[None], (8, model))
-    gain_mid_rows = jnp.broadcast_to(gain_mid[None], (8, model))
+    gain_in_rows = gain_in[None]
+    gain_mid_rows = gain_mid[None]
     normed_all, *pieces, gate_raw, narrow = project(
         tensor_parts, tokens, gain_in_rows, w_narrow, (w_query, w_key, w_value, w_gate_out)
     )
@@ -1536,14 +1547,12 @@
         tensor_parts, residual, gain_mid_rows, (w_gate, w_up, w_down), out_grad
     )
     units = w_gate.shape[1]
-    ring = [(i, (i + 1) % tensor_parts) for i in range(tensor_parts)]
-
-    def piece_of(values, back_by):
-        index = lax.rem(tensor_index - back_by + tensor_parts, tensor_parts)
+    right = [(i, (i + 1) % tensor_parts) for i in range(tensor_parts)]
+    left = [(i, (i - 1) % tensor_parts) for i in range(tensor_parts)]
+
+    def part_for(values, ahead):
+        index = lax.rem(tensor_index + ahead + tensor_parts, tensor_parts)
         return lax.dynamic_slice_in_dim(values, index * rows_own, rows_own, 0)
-
-    def added(values, back_by, got):
-        return (piece_of(values, back_by).astype(F32) + got.astype(F32)).astype(LOW)
 
     units_grad_sum = lax.psum_scatter(units_grad, "dp", scatter_dimension=0, tiled=True)
     grad_res_norm, gain_mid_grad = norm_back(residual, gain_mid, grad_mid)
@@ -1551,36 +1560,48 @@
     grad_residual = grad_own.astype(F32) + grad_res_norm
     grad_mixer = grad_residual.astype(LOW)
     grad_mixed = jnp.concatenate(
-        [contract_cols(grad_mixer, weight).astype(LOW) for weight in (out_mine, out_other)], axis=1
-    ).reshape(rows_own, 2, tensor_parts, half)
+        [
+            lax.dot_general(
+                grad_mixer, weight.reshape(tensor_parts, half, model), (((1,), (2,)), ((), ())),
+                preferred_element_type=F32,
+            ).astype(LOW).swapaxes(0, 1)
+            for weight in (out_mine, out_other)
+        ],
+        axis=2,
+    )
     grad_mixed = lax.all_to_all(
-        grad_mixed, "tensor", split_axis=2, concat_axis=0, tiled=True
+        grad_mixed, "tensor", split_axis=0, concat_axis=0, tiled=True
     ).reshape(group_rows, width)
-    mlp_run = lax.ppermute(piece_of(after(mlp_part, grad_mixed), 1), "tensor", ring)
-    out_w = contract_rows(after(grad_mixer, grad_mixed), mixed_own).astype(LOW)
+    mlp_late = after(mlp_part, grad_mixed)
+    mlp_run = part_for(mlp_late, tensor_parts - 2)
+    for ahead in range(tensor_parts - 2, 1, -1):
+        mlp_run = lax.ppermute(mlp_run, "tensor", right)
+        if ahead > 2:
+            mlp_run = (mlp_run.astype(F32) + part_for(mlp_part, ahead - 1).astype(F32)).astype(LOW)
+    mlp_left = lax.ppermute(part_for(mlp_late, -1), "tensor", left)
+    out_w = contract_rows(grad_mixer, mixed_own).astype(LOW)
     out_w_sum = lax.psum_scatter(out_w, "dp", scatter_dimension=0, tiled=True)
     do, gate_low, head_gain_part, ds_total = inward(
         scalars, grad_mixed, rows_out, gate_raw, gain_heads, qt, t, totals, heads
     )
     grad_end = exchange(dp_parts, ds_total, heads, True, 5)
     grad_end, mlp_run = lax.optimization_barrier((grad_end, mlp_run))
-    for back_by in range(2, tensor_parts - 1):
-        mlp_run = lax.ppermute(added(mlp_part, back_by, mlp_run), "tensor", ring)
+    mlp_right = lax.ppermute(
+        (mlp_run.astype(F32) + part_for(mlp_part, 1).astype(F32)).astype(LOW), "tensor", right
+    )
     grads, tails, rim_grad, taps_grad, params_grad = back(
         scalars, pieces, rims, narrow, taps, params, grad_end, do, v2, s, x, p, kg, w, u, qt, t,
         gate_low, docs, heads,
     )
-    grads, tails, rim_grad, taps_grad, params_grad, mlp_run, units_grad_sum = (
+    grads, tails, rim_grad, taps_grad, params_grad, mlp_right, mlp_left, units_grad_sum = (
         lax.optimization_barrier(
-            (grads, tails, rim_grad, taps_grad, params_grad, mlp_run, units_grad_sum)
+            (grads, tails, rim_grad, taps_grad, params_grad, mlp_right, mlp_left, units_grad_sum)
         )
     )
-    mlp_run = lax.ppermute(added(mlp_part, tensor_parts - 1, mlp_run), "tensor", ring)
     rim_back = lax.ppermute(rim_grad, "dp", [(i + 1, i) for i in range(dp_parts - 1)])
     tails = tails.at[HALO - 8 :].add(rim_back).astype(LOW)
     grads = lax.dynamic_update_slice(grads, tails, (group_rows - HALO, 0))
     mixer_grad = contract_rows(normed_all, grads).astype(LOW)
-    mixer_grad, mlp_run = lax.optimization_barrier((mixer_grad, mlp_run))
     mixer_sum = lax.psum_scatter(mixer_grad, "dp", scatter_dimension=0, tiled=True).astype(F32)
     params_grad = params_grad.reshape(2, 8, 128).sum(1)
     flat = jnp.concatenate(
@@ -1592,36 +1613,52 @@
         ],
         axis=0,
     )
-    input_grad, wide, rest, gain_in_grad = scatter(
+    grad_tokens, wide, rest, gain_in_grad = scatter(
         tensor_parts, [after(grads, mixer_grad)],
         [w_query, w_key, w_value, w_narrow, w_gate_out],
         ((0, 0, width), (0, width, width), (0, 2 * width, width), (0, 3 * width, 128), (0, 3 * width + 128, width)),
         6, Closing(dp_parts, tensor_parts, 16, flat.shape),
-        (tokens, gain_in_rows, grad_residual, flat),
-    )
-    out_w_sum, mlp_run, _ = lax.optimization_barrier((out_w_sum, mlp_run, gain_in_grad))
-    output = (residual + (piece_of(mlp_part, 0).astype(F32) + mlp_run.astype(F32))).astype(LOW)
-    def out_piece(ahead):
-        index = lax.rem(tensor_index + ahead, tensor_parts)
-        return lax.dynamic_slice_in_dim(out_w_dp, index * width, width, 1)
-
-    out_w_dp = out_w_sum
-    out_w_sum = out_piece(0).astype(F32)
+        (tokens, gain_in_rows, flat, normed_all),
+    )
+    out_w_dp, units_grad_sum, mlp_right, mlp_left, _ = lax.optimization_barrier(
+        (out_w_sum, units_grad_sum, mlp_right, mlp_left, gain_in_grad)
+    )
+    out_pieces = [
+        lax.dynamic_slice_in_dim(
+            out_w_dp, lax.rem(tensor_index + ahead, tensor_parts) * width, width, 1
+        )
+        for ahead in range(tensor_parts)
+    ]
+    wide, rest, units_grad_sum, mlp_right, *out_pieces = lax.optimization_barrier(
+        (wide, rest, units_grad_sum, mlp_right, *out_pieces)
+    )
     for ahead in range(1, tensor_parts):
         shift = [(i, (i + ahead) % tensor_parts) for i in range(tensor_parts)]
-        out_w_sum = out_w_sum + lax.ppermute(out_piece(ahead), "tensor", shift).astype(F32)
-    by_head = wide[13:15].reshape(2, tensor_parts, width)[:, :, :heads].reshape(2, -1)
+        out_pieces[ahead] = lax.ppermute(out_pieces[ahead], "tensor", shift)
+    output = residual + part_for(mlp_part, 0).astype(F32)
+    output = (output + (mlp_right.astype(F32) + mlp_left.astype(F32))).astype(LOW)
     start = 3 * width
-    return (
+    ready = [
         output,
-        input_grad,
-        gain_in_grad.reshape(model),
+        grad_residual + grad_tokens,
         mixer_sum[:, :width],
         mixer_sum[:, width : 2 * width],
         mixer_sum[:, 2 * width : start],
         mixer_sum[:, start : start + heads],
         mixer_sum[:, start + heads : start + 2 * heads],
         mixer_sum[:, start + 128 :],
+        units_grad_sum[:, :units].astype(F32),
+        units_grad_sum[:, units : 2 * units].astype(F32),
+        units_grad_sum[:, 2 * units :].T.astype(F32),
+    ]
+    ready, out_pieces = lax.optimization_barrier((ready, out_pieces))
+    out_w_sum = sum(piece.astype(F32) for piece in out_pieces)
+    by_head = wide[13:15].reshape(2, tensor_parts, width)[:, :, :heads].reshape(2, -1)
+    return (
+        ready[0],
+        ready[1],
+        gain_in_grad.reshape(model),
+        *ready[2:8],
         wide[0:4],
         wide[4:8],
         wide[8:12],
@@ -1630,9 +1667,7 @@
         wide[12],
         out_w_sum.T,
         rest[: model // width].reshape(model),
-        units_grad_sum[:, :units].astype(F32),
-        units_grad_sum[:, units : 2 * units].astype(F32),
-        units_grad_sum[:, 2 * units :].T.astype(F32),
+        *ready[8:11],
     )
 
 

time: 688 us -> 668 us (0.971)
  blocking collectives: 23.8 us -> 0 us
  waiting for transfers between devices: 57.9 us -> 67 us
    all_to_all x1 -> x0, blocking collectives: 23.8 us -> none  [local(): lax.all_to_all(grad_mixed, 'tensor', split_axis=2, concat_axis=0, tiled=T...]
    all_to_all x0 -> x1, waiting for transfers between devices: none -> 20.3 us  [local(): lax.all_to_all(grad_mixed, 'tensor', split_axis=0, concat_axis=0, tiled=T...]
    ppermute x6, waiting for transfers between devices: 22.1 us -> 8.68 us  [the longest x3 8.67 us: local(): out_pieces[ahead] = lax.ppermute(out_pieces[ahead], 'tensor', shift)]
  transfers between devices with their start and end apart: 14 -> 15, of which waited for: 7 -> 8; matrix products, arithmetic and copies ran while one was open for 12% -> 12% of each run, Pallas kernels for 36% -> 37%
where the time goes in v6:
time: 668 us; the launch traced here: 664 us
  Pallas kernels  464 us (69%)
  waiting for transfers between devices  67 us (10%)
  matrix products  40.5 us (6%)
  local copies, waits for them, and re-layouts  31.8 us (5%)
  other arithmetic  22.9 us (3%)
  starting transfers between devices  22.8 us (3%)
  between operations  14.7 us (2%)
    pallas_call x1, Pallas kernels, feed(): pl.pallas_call(functools.partial(feed_kernel, parts), out_shape=(low, sds...  145 us
    pallas_call x1, Pallas kernels, scatter(): pl.pallas_call(functools.partial(scatter_kernel, parts, len(lefts), count...  93.9 us
    pallas_call x1, Pallas kernels, project(): pl.pallas_call(functools.partial(project_kernel, parts), out_shape=(sds(t...  75 us
    pallas_call x1, Pallas kernels, back(): pl.pallas_call(functools.partial(back_kernel, docs, heads, chunks // GROU...  45.9 us
    pallas_call x2, Pallas kernels, exchange(): pl.pallas_call(functools.partial(state_kernel, count, heads, backward), o...  45.8 us
    pallas_call x1, Pallas kernels, intra(): pl.pallas_call(functools.partial(intra_kernel, docs, heads), out_shape=(t...  35.4 us
    all_to_all x1, waiting for transfers between devices, local(): lax.all_to_all(mixed, 'tensor', split_axis=0, concat_axis=1, tiled=True)  23.4 us
    dot_general x2, matrix products, contract_rows(): return lax.dot_general(left, right, TN, preferred_element_type=F32)  22.2 us
  transfers between devices with their start and end apart: 15, of which 8 were waited for; matrix products, arithmetic and copies ran while one was open for 12% of the time, Pallas kernels for 37%

profile of v6, /device:TPU:12, one launch (start us, length us, event | category | flops | bytes accessed | tf_op | source)
XLA Modules:
  0.0 663.9 jit_solution(3211587938230160685)
XLA Ops:
  9.3 75.0 %project.1 = (bf16[1024,2048]{1,0:T(8,128)(2,1)}, bf16[1024,512]{1,0:T(8,128)(2,1)}, bf16[1024,512]{1,0:T(8,128)(2,1)}, bf16[1024,512]{1,0:T(8,128)(2,1)}, f32[1024,512]{1,0:T(8,128)}, /*index=5*/f32[1024,128]{1,0:T(8,128)}) custom-call(bf16[256,2048]{1,0:T(8,128)(2,1)} %refs_6_.1, f32[1,2048]{1,0:T(1,128)} %bitcast.79, ...), custom_call_target="tpu_custom_call" | custom-call | flops 9126805504 | bytes 62914560 | tf_op jit(solution)/shard_map/project/pallas_call | solution.py:762
  87.0 2.4 collective-permute-start
  94.0 35.4 %intra.1 = (f32[8,4,128,128]{3,2,1,0:T(8,128)}, f32[8,4,128,128]{3,2,1,0:T(8,128)}, f32[8,4,128,128]{3,2,1,0:T(8,128)}, f32[1024,512]{1,0:T(8,128)}, f32[1024,51...) custom-call(s32[6]{0:T(128)} %pad_add_fusion.scalars, ...), custom_call_target="tpu_custom_call" | custom-call | flops 24159191040 | bytes 62914560 | tf_op jit(solution)/shard_map/intra/pallas_call | solution.py:255
  129.4 16.4 %exchange3.1.s_in = f32[4,128,128]{2,1,0:T(8,128)} custom-call(f32[4,128,256]{2,1,0:T(8,128)} %get-tuple-element.137.own_ref.maps_ref), custom_call_target="tpu_custom_call" | custom-call | flops 402653184 | bytes 4194304 | tf_op jit(solution)/shard_map/exchange3/pallas_call | solution.py:1454
  146.4 11.5 %outward.1 = (f32[1024,512]{1,0:T(8,128)}, f32[1024,512]{1,0:T(8,128)}, f32[8,4,128,128]{3,2,1,0:T(8,128)}, bf16[1024,512]{1,0:T(8,128)(2,1)}) custom-call(f32[4,128,128]{2,1,0:T(8,128)} %exchange3.1.s_in, f32[1024,512]{1,0:T(8,128)} %get-tuple-element.138.w_ref.refs_19_, f32[1024,512]{1,0:T(8,128)} %get-tuple-element.139.u_ref.refs_20_, ...), custom_call_target="tpu_custom_call" | custom-call | flops 1207959552 | bytes 23068672 | tf_op jit(solution)/shard_map/outward/pallas_call | solution.py:311
  157.9 9.7 %all-gather.3.cloned.1.call-done = bf16[1024,2048]{1,0:T(8,128)(2,1)} async-done(((bf16[256,2048]{1,0:T(8,128)(2,1)}), bf16[1024,2048]{1,0:T(8,128)(2,1)}) %all-gather.3.cloned.1.call-update) | async-done | bytes 4194320 | tf_op jit(solution)/shard_map/all_gather | solution.py:1523
  167.6 2.3 copy.65
  169.8 6.5 all-to-all-start
  176.3 23.4 %all-to-all-done = bf16[4,256,512]{1,2,0:T(8,128)(2,1)S(1)} async-done(((bf16[4,256,512]{1,2,0:T(8,128)(2,1)}), bf16[4,256,512]{1,2,0:T(8,128)(2,1)S(1)}, u32[]{:S(2)}, u32[]{:S(2)}) %all-to-all-start) | async-done | bytes 1048608 | tf_op jit(solution)/shard_map/all_to_all | solution.py:1535
  199.8 3.5 fusion.13
  203.4 5.0 multiply_reduce_fusion.2
  208.4 145.1 %feed.1 = (bf16[1024,2048]{1,0:T(8,128)(2,1)}, f32[256,2048]{1,0:T(8,128)}, bf16[2048,4224]{1,0:T(8,128)(2,1)}) custom-call(f32[256,2048]{1,0:T(8,128)} %get-tuple-element.318.res_ref, f32[1,2048]{1,0:T(1,128)} %bitcast.69, bf16[2048,1408]{1,0:T(8,128)(2,1)} %refs_0_.3, bf16[2048,1408]{1,0:T(8,128)(2,1)} %refs_1_.4, bf16[1408,2048]{1,0:T(8,128)(2,1)} %refs_2_.4, ...), custom_call_target="tpu_custom_call" | custom-call | flops 53150220288 | bytes 125829120 | tf_op jit(solution)/shard_map/feed/pallas_call | solution.py:999
  355.1 2.3 multiply_reduce_fusion
  360.6 7.0 %convolution_convert_fusion.1 = bf16[2048,2048]{1,0:T(8,128)(2,1)} fusion(bf16[256,2048]{0,1:T(8,128)(2,1)S(1)} %bitcast.64, f32[256,2048]{1,0:T(8,128)S(1)} %subtract_add_fusion), kind=kOutput, calls=%fused_computation.1 | convolution fusion | flops 2152202240 | bytes 11534336 | tf_op jit(solution)/shard_map/dot_general | solution.py:565
  367.6 5.5 fusion.1
  373.1 4.3 fusion.2
  378.5 3.5 all-to-all-start.1
  382.1 20.3 %all-to-all-done.1 = bf16[4,256,512]{1,2,0:T(8,128)(2,1)S(1)} async-done(((bf16[4,256,512]{1,2,0:T(8,128)(2,1)}), bf16[4,256,512]{1,2,0:T(8,128)(2,1)S(1)}, u32[]{:S(2)}, u32[]{:S(2)}) %all-to-all-start.1) | async-done | bytes 1048608 | tf_op jit(solution)/shard_map/all_to_all | solution.py:1572
  403.7 3.3 constant_dynamic-slice_fusion.4
  409.4 11.4 %inward.1 = (f32[1024,512]{1,0:T(8,128)}, bf16[1024,512]{1,0:T(8,128)(2,1)}, f32[8,512]{1,0:T(8,128)}, f32[4,128,256]{2,1,0:T(8,128)}) custom-call(s32[6]{0:T(128)} %pad_add_fusion.scalars, bf16[1024,512]{1,0:T(8,128)(2,1)} %bitcast.65, f32[1024,512]{1,0:T(8,128)} %get-tuple-element.150.out_ref, f32[1024,512]{1,0:T(8,128)} %get-tuple-element.144.gate_ref, ...), custom_call_target="tpu_custom_call" | custom-call | flops 805306368 | bytes 14680064 | tf_op jit(solution)/shard_map/inward/pallas_call | solution.py:365
  420.9 29.4 %exchange5.1.refs_12_ = f32[4,128,128]{2,1,0:T(8,128)} custom-call(f32[4,128,256]{2,1,0:T(8,128)} %get-tuple-element.151.own_ref), custom_call_target="tpu_custom_call" | custom-call | flops 402653184 | bytes 4194304 | tf_op jit(solution)/shard_map/exchange5/pallas_call | solution.py:1454
  453.5 45.9 %back.1 = (bf16[1024,2176]{1,0:T(8,128)(2,1)}, f32[16,1536]{1,0:T(8,128)}, f32[8,1536]{1,0:T(8,128)}, f32[12,8,512]{2,1,0:T(8,128)}, f32[16,128]{1,0:T(8,128)}) custom-call(s32[6]{0:T(128)} %pad_add_fusion.scalars, bf16[1024,512]{1,0:T(8,128)(2,1)} %get-tuple-element.133.refs_0_.refs_3_, bf16[1024,512]{1,0:T(8,128)(2,1)} %get-tuple-element.134.refs_1_.refs_4_, ...), custom_call_target="tpu_custom_call" | custom-call | flops 8053063680 | bytes 33554432 | tf_op jit(solution)/shard_map/back/pallas_call | solution.py:539
  499.4 2.2 collective-permute-start.5
  506.4 15.3 %convolution_convert_fusion = bf16[2048,2176]{1,0:T(8,128)(2,1)} fusion(bf16[1024,2048]{1,0:T(8,128)(2,1)} %get-tuple-element.171.refs_9_, bf16[1024,2176]{1,0:T(8,128)(2,1)} %convert_dynamic-update-slice_fusion.refs_0_), kind=kOutput, calls=%fused_computation | convolution fusion | flops 9131261952 | bytes 17563648 | tf_op jit(solution)/shard_map/dot_general | solution.py:565
  523.3 93.9 %scatter6.1 = (f32[256,2048]{1,0:T(8,128)}, f32[16,2048]{1,0:T(8,128)}, f32[8,512]{1,0:T(8,128)}, f32[8,256]{1,0:T(8,128)}) custom-call(bf16[1024,2176]{1,0:T(8,128)(2,1)} %convert_dynamic-update-slice_fusion.refs_0_, bf16[2048,512]{1,0:T(8,128)(2,1)} %refs_1_.5, bf16[2048,512]{1,0:T(8,128)(2,1)} %refs_2_.5, bf16[2048,512]{1,0:T(8,128)(2,1)} %refs_3_.5, ...), custom_call_target="tpu_custom_call" | custom-call | flops 9126805504 | bytes 62914560 | tf_op jit(solution)/shard_map/scatter6/pallas_call | solution.py:1331
  617.3 2.4 constant_dynamic-slice_fusion
  622.0 3.3 add.166
  625.2 4.3 collective-permute-start.7
  632.7 3.3 add_convert_fusion
  640.4 2.6 fusion.9
  643.0 5.2 collective-permute-done.7
  648.3 3.4 collective-permute-done.8
  (124 shorter events, 44.3 us)
Async XLA Ops:
  7.2 77.2 %copy-start = (bf16[512,2048]{1,0:T(8,128)(2,1)S(1)}, bf16[512,2048]{1,0:T(8,128)(2,1)}, u32[]{:S(2)}) copy-start(bf16[512,2048]{1,0:T(8,128)(2,1)} %param.41) | copy-start | bytes 6291460
  7.2 160.4 %all-gather.3.cloned.1.call-start = ((), (), s32[]{:S(2)}) async-start(), calls=%async_computation.8 | async-start | bytes 5242880 | tf_op jit(solution)/shard_map/all_gather | solution.py:1523
  84.4 5.1 copy-start.25
  84.4 5.3 copy-start.15
  84.4 5.3 copy-start.16
  84.4 5.3 copy-start.17
  84.4 6.6 copy-start.23
  84.4 6.6 copy-start.24
  87.0 6.3 collective-permute-start
  94.0 51.8 %copy-start.22 = (f32[512]{0:T(512)S(1)}, f32[512]{0:T(512)}, u32[]{:S(2)}) copy-start(f32[512]{0:T(512)} %param.40) | copy-start | bytes 6148
  167.6 35.8 %collective-permute-start.1 = (bf16[4,256,2048]{2,1,0:T(8,128)(2,1)}, bf16[4,256,2048]{2,1,0:T(8,128)(2,1)}, u32[]{:S(2)}, u32[]{:S(2)}) collective-permute-start(bf16[4,256,2048]{2,1,0:T(8,128)(2,1)} %bitcast.77), channel_id=1, source_target_pairs={{0,4},{4,0},{8,12},{12,8},{16,20},{20,16},{24,28},{28,24},{1,5},{5... | collective-permute-start | bytes 12582920 | tf_op jit(solution)/shard_map/ppermute | solution.py:1537
  169.8 29.9 %all-to-all-start = ((bf16[4,256,512]{1,2,0:T(8,128)(2,1)}), bf16[4,256,512]{1,2,0:T(8,128)(2,1)S(1)}, u32[]{:S(2)}, u32[]{:S(2)}) async-start(bf16[4,256,512]{1,2,0:T(8,128)(2,1)} %copy.65), calls=%async_computation | async-start | bytes 2097152 | tf_op jit(solution)/shard_map/all_to_all | solution.py:1535
  176.3 323.1 %reduce-scatter.4.cloned.1.call-start = ((), (), s32[]{:S(2)}) async-start(), calls=%async_computation.5 | async-start | bytes 19464192 | tf_op jit(solution)/shard_map/reduce_scatter | solution.py:1557
  199.8 3.6 copy-start.8
  353.6 263.7 %reduce-scatter.6.cloned.1.call-start = ((), (), s32[]{:S(2)}) async-start(), calls=%async_computation.6 | async-start | bytes 9437184 | tf_op jit(solution)/shard_map/reduce_scatter | solution.py:1583
  367.6 5.5 copy-start.4
  378.5 23.9 %all-to-all-start.1 = ((bf16[4,256,512]{1,2,0:T(8,128)(2,1)}), bf16[4,256,512]{1,2,0:T(8,128)(2,1)S(1)}, u32[]{:S(2)}, u32[]{:S(2)}) async-start(bf16[4,256,512]{1,2,0:T(8,128)(2,1)} %pad_maximum_fusion), calls=%async_computation.1 | async-start | bytes 2097152 | tf_op jit(solution)/shard_map/all_to_all | solution.py:1572
  382.0 256.8 %reduce-scatter.8.cloned.1.call-start = ((), (), s32[]{:S(2)}) async-start(), calls=%async_computation.7 | async-start | bytes 10027008 | tf_op jit(solution)/shard_map/reduce_scatter | solution.py:1605
  407.0 43.3 %collective-permute-start.2 = (bf16[256,2048]{1,0:T(8,128)(2,1)}, bf16[256,2048]{1,0:T(8,128)(2,1)}, u32[]{:S(2)}, u32[]{:S(2)}) collective-permute-start(bf16[256,2048]{1,0:T(8,128)(2,1)} %get-tuple-element.293), channel_id=1, source_target_pairs={{0,1},{1,2},{2,3},{3,0},{4,5},{5,6},{6,7},{7,4},{8,9},{9,10},{10,1... | collective-permute-start | bytes 3145736 | tf_op jit(solution)/shard_map/ppermute | solution.py:1578
  407.4 91.9 %collective-permute-start.4 = (bf16[256,2048]{1,0:T(8,128)(2,1)}, bf16[256,2048]{1,0:T(8,128)(2,1)S(1)}, u32[]{:S(2)}, u32[]{:S(2)}) collective-permute-start(bf16[256,2048]{1,0:T(8,128)(2,1)} %get-tuple-element.292), channel_id=1, source_target_pairs={{0,3},{1,0},{2,1},{3,2},{4,7},{5,4},{6,5},{7,6},{8,11},{9,8},{10,9... | collective-permute-start | bytes 3145736 | tf_op jit(solution)/shard_map/ppermute | solution.py:1581
  452.2 47.2 %collective-permute-start.3 = (bf16[256,2048]{1,0:T(8,128)(2,1)S(1)}, bf16[256,2048]{1,0:T(8,128)(2,1)}, u32[]{:S(2)}, u32[]{:S(2)}) collective-permute-start(bf16[256,2048]{1,0:T(8,128)(2,1)S(1)} %add_convert_fusion.1), channel_id=1, source_target_pairs={{0,1},{1,2},{2,3},{3,0},{4,5},{5,6},{6,7},{7,4},{8,9},{9,10},{10,1... | collective-permute-start | bytes 3145736 | tf_op jit(solution)/shard_map/ppermute | solution.py:1589
  499.4 4.0 collective-permute-start.5
  617.3 4.7 copy-start.5
  622.0 8.8 %copy-start.21 = (f32[8,512]{1,0:T(8,128)S(1)}, f32[8,512]{1,0:T(8,128)}, u32[]{:S(2)}) copy-start(f32[8,512]{1,0:T(8,128)} %get-tuple-element.206) | copy-start | bytes 49156
  622.0 9.4 %copy-start.19 = (f32[8,256]{1,0:T(8,128)S(1)}, f32[8,256]{1,0:T(8,128)}, u32[]{:S(2)}) copy-start(f32[8,256]{1,0:T(8,128)} %get-tuple-element.181) | copy-start | bytes 24580
  622.0 10.0 %copy-start.12 = (f32[16,2048]{1,0:T(8,128)S(1)}, f32[16,2048]{1,0:T(8,128)}, u32[]{:S(2)}) copy-start(f32[16,2048]{1,0:T(8,128)} %get-tuple-element.201) | copy-start | bytes 393220
  625.2 17.8 %collective-permute-start.6 = (bf16[256,512]{1,0:T(8,128)(2,1)}, bf16[256,512]{1,0:T(8,128)(2,1)}, u32[]{:S(2)}, u32[]{:S(2)}) collective-permute-start(bf16[256,512]{1,0:T(8,128)(2,1)} %get-tuple-element.190), channel_id=1, source_target_pairs={{0,1},{1,2},{2,3},{3,0},{4,5},{5,6},{6,7},{7,4},{8,9},{9,10},{10,1... | collective-permute-start | bytes 786440 | tf_op jit(solution)/shard_map/ppermute | solution.py:1637
  625.2 23.0 %collective-permute-start.7 = (bf16[256,512]{1,0:T(8,128)(2,1)}, bf16[256,512]{1,0:T(8,128)(2,1)}, u32[]{:S(2)}, u32[]{:S(2)}) collective-permute-start(bf16[256,512]{1,0:T(8,128)(2,1)} %get-tuple-element.191), channel_id=1, source_target_pairs={{0,2},{1,3},{2,0},{3,1},{4,6},{5,7},{6,4},{7,5},{8,10},{9,11},{10,... | collective-permute-start | bytes 786440 | tf_op jit(solution)/shard_map/ppermute | solution.py:1637
  629.6 22.1 %collective-permute-start.8 = (bf16[256,512]{1,0:T(8,128)(2,1)}, bf16[256,512]{1,0:T(8,128)(2,1)}, u32[]{:S(2)}, u32[]{:S(2)}) collective-permute-start(bf16[256,512]{1,0:T(8,128)(2,1)} %get-tuple-element.192), channel_id=1, source_target_pairs={{0,3},{1,0},{2,1},{3,2},{4,7},{5,4},{6,5},{7,6},{8,11},{9,8},{10,9... | collective-permute-start | bytes 786440 | tf_op jit(solution)/shard_map/ppermute | solution.py:1637
  632.7 3.3 copy-start.7
  651.7 5.3 copy-start.1
  653.2 3.0 copy-start.9
  (9 other events, 14.7 us)
Sparse Core Ops, SparseCore 0:
  85.7 81.8 all-gather.2
  353.7 128.8 reduce-scatter.3
  486.5 74.8 reduce-scatter.5
  564.9 73.8 reduce-scatter.7

commit v7 on v6

--- a/solution.py
+++ b/solution.py
@@ -702,9 +702,9 @@
 
 def project_kernel(parts, tok_ref, gain_ref, narrow_w, *refs):
     weights_in, all_ref = refs[0:4], refs[4]
-    q_ref, k_ref, v_ref, gate_ref, narrow_ref = refs[5:10]
-    buf, weights = refs[10], refs[11:15]
-    sems, load_sem, store_sem = refs[15:19], refs[19], refs[20]
+    q_ref, k_ref, v_ref, gate_ref, narrow_ref, tails_ref = refs[5:11]
+    buf, weights = refs[11], refs[12:16]
+    sems, load_sem, store_sem = refs[16:20], refs[20], refs[21]
     me = lax.axis_index("tensor")
     rows = tok_ref.shape[0]
     loads = [
@@ -732,6 +732,8 @@
         narrow_ref[at, :] = dot(values, narrow_w[...])
 
     line_gather(parts, buf, sems, first, use)
+    for i, out in enumerate((q_ref, k_ref, v_ref)):
+        tails_ref[i] = out[rows * parts - HALO :, :]
     for piece in range(parts):
         stored(piece).wait()
 
@@ -761,9 +763,12 @@
     low = sds(total, width, dtype=LOW)
     return pl.pallas_call(
         functools.partial(project_kernel, parts),
-        out_shape=(sds(total, model, dtype=LOW), low, low, low, sds(total, width), sds(total, 128)),
+        out_shape=(
+            sds(total, model, dtype=LOW), low, low, low, sds(total, width), sds(total, 128),
+            sds(3, HALO, width, dtype=LOW),
+        ),
         in_specs=[vmem()] * 3 + [hbm()] * 4,
-        out_specs=[hbm()] + [vmem()] * 5,
+        out_specs=[hbm()] + [vmem()] * 6,
         scratch_shapes=[pltpu.VMEM((parts, rows, model), LOW)]
         + [pltpu.VMEM((model, width), LOW)] * 4
         + line_sems(parts)
@@ -886,7 +891,6 @@
         mlp_ref[at, cols] = dot(act_ref[at, :], wd[:, cols]).astype(LOW)
         return 0
 
-    lax.fori_loop(0, parts * (model // 256), down, 0)
     talls = model // 256
     tiles = 3 * talls
 
@@ -960,6 +964,7 @@
         return 0
 
     lax.fori_loop(0, turns, pass_on, 0)
+    lax.fori_loop(0, parts * (model // 256), down, 0)
     for sub in range(FEED_SUBS):
         at = slice(sub * size, sub * size + size)
 
@@ -1515,16 +1520,14 @@
     own_rows = tokens.astype(F32)
     gain_in_rows = gain_in[None]
     gain_mid_rows = gain_mid[None]
-    normed_all, *pieces, gate_raw, narrow = project(
+    normed_all, *pieces, gate_raw, narrow, rims = project(
         tensor_parts, tokens, gain_in_rows, w_narrow, (w_query, w_key, w_value, w_gate_out)
     )
     half = width // 2
     out_half = lax.dynamic_slice_in_dim(after(w_out, narrow), core * half, half, 0)
     out_mine = lax.all_gather(out_half, "tensor", axis=0)
     forth = [(i, i + 1) for i in range(dp_parts - 1)]
-    rims = lax.ppermute(
-        jnp.stack([piece[group_rows - HALO :] for piece in pieces]), "dp", forth
-    )
+    rims = lax.ppermute(rims, "dp", forth)
     rims = [rims[i] for i in range(3)]
     x, p, kg, w, u, qt, ou, t, o, totals = intra(
         scalars, pieces, rims, narrow, taps, params, docs, heads
@@ -1532,17 +1535,19 @@
     state_in = exchange(dp_parts, totals, heads, False, 3)
     rows_out, v2, s, mixed = outward(state_in, w, u, qt, ou, t, o, gate_raw, gain_heads, heads)
 
-    mixed_own = lax.all_to_all(mixed, "tensor", split_axis=0, concat_axis=1, tiled=True)
+    mixed_all = lax.all_to_all(
+        mixed.reshape(tensor_parts, rows_own, width), "tensor", split_axis=0, concat_axis=0, tiled=True
+    )
     out_mine, _ = lax.optimization_barrier((out_mine, mixed))
     out_other = lax.ppermute(out_mine, "dp", [(i, i ^ 1) for i in range(dp_parts)])
-    out_mine = out_mine.reshape(tensor_parts * half, model)
-    out_other = out_other.reshape(tensor_parts * half, model)
-    split = mixed_own.reshape(rows_own, tensor_parts, 2, half)
-
-    def of_core(index):
-        return lax.dynamic_index_in_dim(split, index, 2, keepdims=False).reshape(rows_own, -1)
-
-    residual = own_rows + (dot(of_core(core), out_mine) + dot(of_core(1 - core), out_other))
+
+    def of_core(index, weight):
+        return lax.dot_general(
+            lax.dynamic_slice_in_dim(mixed_all, index * half, half, 2), weight,
+            (((0, 2), (0, 1)), ((), ())), preferred_element_type=F32,
+        )
+
+    residual = own_rows + (of_core(core, out_mine) + of_core(1 - core, out_other))
     mlp_part, grad_mid, units_grad = feed(
         tensor_parts, residual, gain_mid_rows, (w_gate, w_up, w_down), out_grad
     )
@@ -1562,7 +1567,7 @@
     grad_mixed = jnp.concatenate(
         [
             lax.dot_general(
-                grad_mixer, weight.reshape(tensor_parts, half, model), (((1,), (2,)), ((), ())),
+                grad_mixer, weight, (((1,), (2,)), ((), ())),
                 preferred_element_type=F32,
             ).astype(LOW).swapaxes(0, 1)
             for weight in (out_mine, out_other)
@@ -1579,6 +1584,7 @@
         if ahead > 2:
             mlp_run = (mlp_run.astype(F32) + part_for(mlp_part, ahead - 1).astype(F32)).astype(LOW)
     mlp_left = lax.ppermute(part_for(mlp_late, -1), "tensor", left)
+    mixed_own = mixed_all.swapaxes(0, 1).reshape(rows_own, -1)
     out_w = contract_rows(grad_mixer, mixed_own).astype(LOW)
     out_w_sum = lax.psum_scatter(out_w, "dp", scatter_dimension=0, tiled=True)
     do, gate_low, head_gain_part, ds_total = inward(
@@ -1651,7 +1657,6 @@
         units_grad_sum[:, units : 2 * units].astype(F32),
         units_grad_sum[:, 2 * units :].T.astype(F32),
     ]
-    ready, out_pieces = lax.optimization_barrier((ready, out_pieces))
     out_w_sum = sum(piece.astype(F32) for piece in out_pieces)
     by_head = wide[13:15].reshape(2, tensor_parts, width)[:, :, :heads].reshape(2, -1)
     return (

time: 668 us -> 670 us (level)
  transfers between devices with their start and end apart: 15 -> 15, of which waited for: 8 -> 7; matrix products, arithmetic and copies ran while one was open for 12% -> 12% of each run, Pallas kernels for 37% -> 37%
where the time goes in v7:
time: 670 us; the launch traced here: 660 us
  Pallas kernels  464 us (69%)
  waiting for transfers between devices  66.4 us (10%)
  matrix products  40.8 us (6%)
  local copies, waits for them, and re-layouts  26.8 us (4%)
  other arithmetic  25.7 us (4%)
  starting transfers between devices  22.3 us (3%)
  between operations  14.7 us (2%)
    pallas_call x1, Pallas kernels, feed(): pl.pallas_call(functools.partial(feed_kernel, parts), out_shape=(low, sds...  145 us
    pallas_call x1, Pallas kernels, scatter(): pl.pallas_call(functools.partial(scatter_kernel, parts, len(lefts), count...  94.1 us
    pallas_call x1, Pallas kernels, project(): pl.pallas_call(functools.partial(project_kernel, parts), out_shape=(sds(t...  75.1 us
    pallas_call x1, Pallas kernels, back(): pl.pallas_call(functools.partial(back_kernel, docs, heads, chunks // GROU...  45.9 us
    pallas_call x2, Pallas kernels, exchange(): pl.pallas_call(functools.partial(state_kernel, count, heads, backward), o...  45.5 us
    pallas_call x1, Pallas kernels, intra(): pl.pallas_call(functools.partial(intra_kernel, docs, heads), out_shape=(t...  35.3 us
    all_to_all x1, waiting for transfers between devices, local(): lax.all_to_all(mixed.reshape(tensor_parts, rows_own, width), 'tensor', sp...  23.4 us
    dot_general x2, matrix products, contract_rows(): return lax.dot_general(left, right, TN, preferred_element_type=F32)  22.4 us
  transfers between devices with their start and end apart: 15, of which 7 were waited for; matrix products, arithmetic and copies ran while one was open for 12% of the time, Pallas kernels for 37%

profile of v7, /device:TPU:12, one launch (start us, length us, event | category | flops | bytes accessed | tf_op | source)
XLA Modules:
  0.0 660.3 jit_solution(894551123184148923)
XLA Ops:
  9.3 75.1 %project.1 = (bf16[1024,2048]{1,0:T(8,128)(2,1)}, bf16[1024,512]{1,0:T(8,128)(2,1)}, bf16[1024,512]{1,0:T(8,128)(2,1)}, bf16[1024,512]{1,0:T(8,128)(2,1)}, f32[1...) custom-call(bf16[256,2048]{1,0:T(8,128)(2,1)} %refs_6_.1, f32[1,2048]{1,0:T(1,128)} %bitcast.71, ...), custom_call_target="tpu_custom_call" | custom-call | flops 9126805504 | bytes 62914560 | tf_op jit(solution)/shard_map/project/pallas_call | solution.py:764
  89.4 2.6 collective-permute-done
  92.6 35.3 %intra.1 = (f32[8,4,128,128]{3,2,1,0:T(8,128)}, f32[8,4,128,128]{3,2,1,0:T(8,128)}, f32[8,4,128,128]{3,2,1,0:T(8,128)}, f32[1024,512]{1,0:T(8,128)}, f32[1024,51...) custom-call(s32[6]{0:T(128)} %pad_add_fusion.scalars, ...), custom_call_target="tpu_custom_call" | custom-call | flops 24159191040 | bytes 62914560 | tf_op jit(solution)/shard_map/intra/pallas_call | solution.py:255
  128.0 16.0 %exchange3.1.s_in = f32[4,128,128]{2,1,0:T(8,128)} custom-call(f32[4,128,256]{2,1,0:T(8,128)} %get-tuple-element.124.own_ref.maps_ref), custom_call_target="tpu_custom_call" | custom-call | flops 402653184 | bytes 4194304 | tf_op jit(solution)/shard_map/exchange3/pallas_call | solution.py:1459
  144.6 11.5 %outward.1 = (f32[1024,512]{1,0:T(8,128)}, f32[1024,512]{1,0:T(8,128)}, f32[8,4,128,128]{3,2,1,0:T(8,128)}, bf16[1024,512]{1,0:T(8,128)(2,1)}) custom-call(f32[4,128,128]{2,1,0:T(8,128)} %exchange3.1.s_in, f32[1024,512]{1,0:T(8,128)} %get-tuple-element.125.w_ref.refs_19_, f32[1024,512]{1,0:T(8,128)} %get-tuple-element.126.u_ref.refs_20_, ...), custom_call_target="tpu_custom_call" | custom-call | flops 1207959552 | bytes 23068672 | tf_op jit(solution)/shard_map/outward/pallas_call | solution.py:311
  156.2 11.5 %all-gather.3.cloned.1.call-done = bf16[1024,2048]{1,0:T(8,128)(2,1)} async-done(((bf16[256,2048]{1,0:T(8,128)(2,1)}), bf16[1024,2048]{1,0:T(8,128)(2,1)}) %all-gather.3.cloned.1.call-update) | async-done | bytes 4194320 | tf_op jit(solution)/shard_map/all_gather | solution.py:1528
  167.7 7.0 %all-to-all-start = ((bf16[4,256,512]{2,1,0:T(8,128)(2,1)}), bf16[4,256,512]{2,1,0:T(8,128)(2,1)S(1)}, u32[]{:S(2)}, u32[]{:S(2)}) async-start(bf16[4,256,512]{2,1,0:T(8,128)(2,1)} %bitcast.62), calls=%async_computation | async-start | bytes 2097152 | tf_op jit(solution)/shard_map/all_to_all | solution.py:1538
  174.7 23.4 %all-to-all-done = bf16[4,256,512]{2,1,0:T(8,128)(2,1)S(1)} async-done(((bf16[4,256,512]{2,1,0:T(8,128)(2,1)}), bf16[4,256,512]{2,1,0:T(8,128)(2,1)S(1)}, u32[]{:S(2)}, u32[]{:S(2)}) %all-to-all-start) | async-done | bytes 1048608 | tf_op jit(solution)/shard_map/all_to_all | solution.py:1538
  198.1 3.5 convolution_bitcast_fusion.1
  201.6 5.1 multiply_reduce_fusion.2
  206.7 144.6 %feed.1 = (bf16[1024,2048]{1,0:T(8,128)(2,1)}, f32[256,2048]{1,0:T(8,128)}, bf16[2048,4224]{1,0:T(8,128)(2,1)}) custom-call(f32[256,2048]{1,0:T(8,128)} %get-tuple-element.268.res_ref, f32[1,2048]{1,0:T(1,128)} %bitcast.63, bf16[2048,1408]{1,0:T(8,128)(2,1)} %refs_0_.3, bf16[2048,1408]{1,0:T(8,128)(2,1)} %refs_1_.4, bf16[1408,2048]{1,0:T(8,128)(2,1)} %refs_2_.4, ...), custom_call_target="tpu_custom_call" | custom-call | flops 53150220288 | bytes 125829120 | tf_op jit(solution)/shard_map/feed/pallas_call | solution.py:1004
  353.1 2.3 multiply_reduce_fusion
  359.0 7.0 %convolution_convert_fusion.1 = bf16[2048,2048]{1,0:T(8,128)(2,1)} fusion(bf16[256,2048]{0,1:T(8,128)(2,1)S(1)} %bitcast.61, f32[256,2048]{1,0:T(8,128)S(1)} %subtract_add_fusion), kind=kOutput, calls=%fused_computation.1 | convolution fusion | flops 2152202240 | bytes 11534336 | tf_op jit(solution)/shard_map/dot_general | solution.py:565
  366.1 5.5 fusion.2
  371.6 4.3 fusion.3
  376.9 3.5 all-to-all-start.1
  380.5 20.2 %all-to-all-done.1 = bf16[4,256,512]{1,2,0:T(8,128)(2,1)S(1)} async-done(((bf16[4,256,512]{1,2,0:T(8,128)(2,1)}), bf16[4,256,512]{1,2,0:T(8,128)(2,1)S(1)}, u32[]{:S(2)}, u32[]{:S(2)}) %all-to-all-start.1) | async-done | bytes 1048608 | tf_op jit(solution)/shard_map/all_to_all | solution.py:1577
  402.0 2.9 constant_dynamic-slice_fusion.4
  407.2 11.4 %inward.1 = (f32[1024,512]{1,0:T(8,128)}, bf16[1024,512]{1,0:T(8,128)(2,1)}, f32[8,512]{1,0:T(8,128)}, f32[4,128,256]{2,1,0:T(8,128)}) custom-call(s32[6]{0:T(128)} %pad_add_fusion.scalars, bf16[1024,512]{1,0:T(8,128)(2,1)} %bitcast.57, f32[1024,512]{1,0:T(8,128)} %get-tuple-element.137.out_ref, f32[1024,512]{1,0:T(8,128)} %get-tuple-element.131.gate_ref, ...), custom_call_target="tpu_custom_call" | custom-call | flops 805306368 | bytes 14680064 | tf_op jit(solution)/shard_map/inward/pallas_call | solution.py:365
  418.6 29.5 %exchange5.1.refs_12_ = f32[4,128,128]{2,1,0:T(8,128)} custom-call(f32[4,128,256]{2,1,0:T(8,128)} %get-tuple-element.138.own_ref), custom_call_target="tpu_custom_call" | custom-call | flops 402653184 | bytes 4194304 | tf_op jit(solution)/shard_map/exchange5/pallas_call | solution.py:1459
  451.5 45.9 %back.1 = (bf16[1024,2176]{1,0:T(8,128)(2,1)}, f32[16,1536]{1,0:T(8,128)}, f32[8,1536]{1,0:T(8,128)}, f32[12,8,512]{2,1,0:T(8,128)}, f32[16,128]{1,0:T(8,128)}) custom-call(s32[6]{0:T(128)} %pad_add_fusion.scalars, bf16[1024,512]{1,0:T(8,128)(2,1)} %get-tuple-element.119.refs_0_.refs_3_, bf16[1024,512]{1,0:T(8,128)(2,1)} %get-tuple-element.120.refs_1_.refs_4_, ...), custom_call_target="tpu_custom_call" | custom-call | flops 8053063680 | bytes 33554432 | tf_op jit(solution)/shard_map/back/pallas_call | solution.py:539
  497.4 2.2 collective-permute-start.5
  504.4 15.3 %convolution_convert_fusion = bf16[2048,2176]{1,0:T(8,128)(2,1)} fusion(bf16[1024,2048]{1,0:T(8,128)(2,1)} %get-tuple-element.158.refs_9_, bf16[1024,2176]{1,0:T(8,128)(2,1)} %convert_dynamic-update-slice_fusion.refs_0_), kind=kOutput, calls=%fused_computation | convolution fusion | flops 9131261952 | bytes 17563648 | tf_op jit(solution)/shard_map/dot_general | solution.py:565
  521.4 94.1 %scatter6.1 = (f32[256,2048]{1,0:T(8,128)}, f32[16,2048]{1,0:T(8,128)}, f32[8,512]{1,0:T(8,128)}, f32[8,256]{1,0:T(8,128)}) custom-call(bf16[1024,2176]{1,0:T(8,128)(2,1)} %convert_dynamic-update-slice_fusion.refs_0_, bf16[2048,512]{1,0:T(8,128)(2,1)} %refs_1_.5, bf16[2048,512]{1,0:T(8,128)(2,1)} %refs_2_.5, bf16[2048,512]{1,0:T(8,128)(2,1)} %refs_3_.5, ...), custom_call_target="tpu_custom_call" | custom-call | flops 9126805504 | bytes 62914560 | tf_op jit(solution)/shard_map/scatter6/pallas_call | solution.py:1336
  615.5 2.2 constant_dynamic-slice_fusion
  620.0 3.7 collective-permute-start.7
  623.8 3.4 convert_bitcast_fusion
  628.7 4.0 add.161
  635.1 3.6 add_convert_fusion
  639.4 3.3 collective-permute-done.7
  642.7 3.4 collective-permute-done.8
  650.7 2.6 fusion.14
  (118 shorter events, 39.4 us)
Async XLA Ops:
  7.2 77.4 %copy-start = (bf16[512,2048]{1,0:T(8,128)(2,1)S(1)}, bf16[512,2048]{1,0:T(8,128)(2,1)}, u32[]{:S(2)}) copy-start(bf16[512,2048]{1,0:T(8,128)(2,1)} %param.41) | copy-start | bytes 6291460
  7.2 160.5 %all-gather.3.cloned.1.call-start = ((), (), s32[]{:S(2)}) async-start(), calls=%async_computation.8 | async-start | bytes 5242880 | tf_op jit(solution)/shard_map/all_gather | solution.py:1528
  84.5 3.1 copy-start.24
  84.5 3.4 copy-start.13
  84.5 3.4 copy-start.14
  84.5 3.4 copy-start.15
  84.5 4.7 copy-start.21
  84.6 4.6 copy-start.22
  85.7 6.3 collective-permute-start
  89.4 3.2 copy-start.18
  92.6 51.4 %copy-start.20 = (f32[512]{0:T(512)S(1)}, f32[512]{0:T(512)}, u32[]{:S(2)}) copy-start(f32[512]{0:T(512)} %param.40) | copy-start | bytes 6148
  167.7 33.9 %collective-permute-start.1 = (bf16[4,256,2048]{2,1,0:T(8,128)(2,1)}, bf16[4,256,2048]{2,1,0:T(8,128)(2,1)}, u32[]{:S(2)}, u32[]{:S(2)}) collective-permute-start(bf16[4,256,2048]{2,1,0:T(8,128)(2,1)} %bitcast.58), channel_id=1, source_target_pairs={{0,4},{4,0},{8,12},{12,8},{16,20},{20,16},{24,28},{28,24},{1,5},{5... | collective-permute-start | bytes 12582920 | tf_op jit(solution)/shard_map/ppermute | solution.py:1542
  167.7 30.4 %all-to-all-start = ((bf16[4,256,512]{2,1,0:T(8,128)(2,1)}), bf16[4,256,512]{2,1,0:T(8,128)(2,1)S(1)}, u32[]{:S(2)}, u32[]{:S(2)}) async-start(bf16[4,256,512]{2,1,0:T(8,128)(2,1)} %bitcast.62), calls=%async_computation | async-start | bytes 2097152 | tf_op jit(solution)/shard_map/all_to_all | solution.py:1538
  174.7 322.7 %reduce-scatter.4.cloned.1.call-start = ((), (), s32[]{:S(2)}) async-start(), calls=%async_computation.5 | async-start | bytes 19464192 | tf_op jit(solution)/shard_map/reduce_scatter | solution.py:1562
  198.1 3.5 copy-start.8
  351.4 264.1 %reduce-scatter.6.cloned.1.call-start = ((), (), s32[]{:S(2)}) async-start(), calls=%async_computation.6 | async-start | bytes 9437184 | tf_op jit(solution)/shard_map/reduce_scatter | solution.py:1589
  355.5 3.5 copy-start.6
  366.1 5.5 copy-start.4
  376.9 23.7 %all-to-all-start.1 = ((bf16[4,256,512]{1,2,0:T(8,128)(2,1)}), bf16[4,256,512]{1,2,0:T(8,128)(2,1)S(1)}, u32[]{:S(2)}, u32[]{:S(2)}) async-start(bf16[4,256,512]{1,2,0:T(8,128)(2,1)} %pad_maximum_fusion), calls=%async_computation.1 | async-start | bytes 2097152 | tf_op jit(solution)/shard_map/all_to_all | solution.py:1577
  380.5 267.9 %reduce-scatter.8.cloned.1.call-start = ((), (), s32[]{:S(2)}) async-start(), calls=%async_computation.7 | async-start | bytes 10027008 | tf_op jit(solution)/shard_map/reduce_scatter | solution.py:1611
  404.9 43.3 %collective-permute-start.2 = (bf16[256,2048]{1,0:T(8,128)(2,1)}, bf16[256,2048]{1,0:T(8,128)(2,1)}, u32[]{:S(2)}, u32[]{:S(2)}) collective-permute-start(bf16[256,2048]{1,0:T(8,128)(2,1)} %get-tuple-element.245), channel_id=1, source_target_pairs={{0,1},{1,2},{2,3},{3,0},{4,5},{5,6},{6,7},{7,4},{8,9},{9,10},{10,1... | collective-permute-start | bytes 3145736 | tf_op jit(solution)/shard_map/ppermute | solution.py:1583
  405.4 92.0 %collective-permute-start.4 = (bf16[256,2048]{1,0:T(8,128)(2,1)S(1)}, bf16[256,2048]{1,0:T(8,128)(2,1)}, u32[]{:S(2)}, u32[]{:S(2)}) collective-permute-start(bf16[256,2048]{1,0:T(8,128)(2,1)S(1)} %get-tuple-element.244), channel_id=1, source_target_pairs={{0,3},{1,0},{2,1},{3,2},{4,7},{5,4},{6,5},{7,6},{8,11},{9,8},{10,9... | collective-permute-start | bytes 3145736 | tf_op jit(solution)/shard_map/ppermute | solution.py:1586
  450.1 47.3 %collective-permute-start.3 = (bf16[256,2048]{1,0:T(8,128)(2,1)S(1)}, bf16[256,2048]{1,0:T(8,128)(2,1)}, u32[]{:S(2)}, u32[]{:S(2)}) collective-permute-start(bf16[256,2048]{1,0:T(8,128)(2,1)S(1)} %add_convert_fusion.1), channel_id=1, source_target_pairs={{0,1},{1,2},{2,3},{3,0},{4,5},{5,6},{6,7},{7,4},{8,9},{9,10},{10,1... | collective-permute-start | bytes 3145736 | tf_op jit(solution)/shard_map/ppermute | solution.py:1595
  497.4 4.0 collective-permute-start.5
  620.0 19.4 %collective-permute-start.6 = (bf16[256,512]{1,0:T(8,128)(2,1)}, bf16[256,512]{1,0:T(8,128)(2,1)}, u32[]{:S(2)}, u32[]{:S(2)}) collective-permute-start(bf16[256,512]{1,0:T(8,128)(2,1)} %get-tuple-element.177), channel_id=1, source_target_pairs={{0,1},{1,2},{2,3},{3,0},{4,5},{5,6},{6,7},{7,4},{8,9},{9,10},{10,1... | collective-permute-start | bytes 786440 | tf_op jit(solution)/shard_map/ppermute | solution.py:1643
  620.0 22.7 %collective-permute-start.7 = (bf16[256,512]{1,0:T(8,128)(2,1)}, bf16[256,512]{1,0:T(8,128)(2,1)}, u32[]{:S(2)}, u32[]{:S(2)}) collective-permute-start(bf16[256,512]{1,0:T(8,128)(2,1)} %get-tuple-element.178), channel_id=1, source_target_pairs={{0,2},{1,3},{2,0},{3,1},{4,6},{5,7},{6,4},{7,5},{8,10},{9,11},{10,... | collective-permute-start | bytes 786440 | tf_op jit(solution)/shard_map/ppermute | solution.py:1643
  623.8 22.4 %collective-permute-start.8 = (bf16[256,512]{1,0:T(8,128)(2,1)}, bf16[256,512]{1,0:T(8,128)(2,1)}, u32[]{:S(2)}, u32[]{:S(2)}) collective-permute-start(bf16[256,512]{1,0:T(8,128)(2,1)} %get-tuple-element.179), channel_id=1, source_target_pairs={{0,3},{1,0},{2,1},{3,2},{4,7},{5,4},{6,5},{7,6},{8,11},{9,8},{10,9... | collective-permute-start | bytes 786440 | tf_op jit(solution)/shard_map/ppermute | solution.py:1643
  628.7 5.2 copy-start.19
  628.7 5.8 copy-start.17
  635.1 3.6 copy-start.10
  635.1 11.0 %copy-start.7 = (bf16[256,512]{1,0:T(8,128)(2,1)S(1)}, bf16[256,512]{1,0:T(8,128)(2,1)}, u32[]{:S(2)}) copy-start(bf16[256,512]{1,0:T(8,128)(2,1)} %get-tuple-element.176) | copy-start | bytes 786436
  650.1 3.3 copy-start.1
  (8 other events, 11.1 us)
Sparse Core Ops, SparseCore 0:
  85.8 81.8 all-gather.2
  351.5 128.8 reduce-scatter.3
  484.2 74.6 reduce-scatter.5
  562.4 73.7 reduce-scatter.7
